TPU v7x, 32 devices: a whole 2x2x4 slice. The times are simulated.
32 devices in a mesh: wave: 8 (over z, x), lev: 4 (over y, core).
Axes of the slice: x: 2, y: 2, z: 4, core: 2. Of those that a mesh axis runs over, the one named last changes fastest.
Arguments:
- spectrum: bfloat16 [1024, 1024, 96, 6], P('wave', None, 'lev'), may hold values from -0.3125 to 0.3125
- legendre: bfloat16 [1024, 1024, 16], P('wave'), may hold values from -0.1875 to 0.1875
- wave_numbers: int32 [1024], replicated, may hold values from 0 to 1023, as said below
- vertical: float32 [96, 96], replicated, may hold values from -0.625 to 0.625
Outputs:
- tracer: float32 [96, 32, 2048], P(None, 'wave', 'lev')
Inputs may be any that keep to these rules, and one draw needn't show every extreme that they name: wave_numbers is a permutation of 0 to 1023 in which slots 2 i and 2 i + 1 hold m and 1023 - m for some m, in either order.
All inputs are finite; a program needn't handle non-finite values.
Results may differ from a plain program's by a relative error of at most 0.0066.
Values may be sent and summed in bfloat16 or wider, within the bound.
No kernel may reach another device: no remote copies, remote signals or barrier semaphores. Data moves between devices by JAX's collectives and lax.ppermute only.
A program may use at most 256 MiB of HBM per device.

v0:
```python
import math

import jax
import jax.numpy as jnp
from jax import lax
from jax.sharding import PartitionSpec as P

NLON = 2048


courant_max = 0.45


def padded(block, sides, width, periodic):
    for axis, dim in sides:
        count = lax.axis_size(axis)
        forward = [(i, i + 1) for i in range(count - 1)]
        if periodic:
            forward.append((count - 1, 0))
        backward = [(target, source) for source, target in forward]
        low = lax.ppermute(
            lax.slice_in_dim(block, block.shape[dim] - width, None, axis=dim), axis, forward
        )
        high = lax.ppermute(lax.slice_in_dim(block, 0, width, axis=dim), axis, backward)
        block = jnp.concatenate([low, block, high], axis=dim)
    return block


def twiddles(numbers):
    longitude = jnp.arange(NLON, dtype=jnp.int32)
    residue = numbers[:, None] * longitude[None, :] % NLON
    angles = residue.astype(jnp.float32) * (2.0 * math.pi / NLON)
    weight = jnp.where(numbers == 0, 1.0, 2.0).astype(jnp.float32)[:, None]
    return jnp.stack([weight * jnp.cos(angles), -weight * jnp.sin(angles)]).astype(jnp.bfloat16)


def parity_columns(coefficient, degree, lengths):
    counted = degree < lengths[:, None]
    even_mask = counted & (degree % 2 == 0)
    odd_mask = counted & (degree % 2 == 1)
    return jnp.concatenate(
        [
            jnp.where(even_mask[:, :, None], coefficient, 0),
            jnp.where(odd_mask[:, :, None], coefficient, 0),
        ],
        axis=2,
    )


def padded_sums(coefficient, basis, own_numbers):
    degree_count = coefficient.shape[1]
    degree = jnp.arange(degree_count, dtype=jnp.int32)[None, :]
    masked = parity_columns(coefficient, degree, degree_count - own_numbers)
    return jnp.einsum("skc,ski->sci", masked, basis, preferred_element_type=jnp.float32)


def upwind_core(extended, courant_x, courant_y):
    center = extended[:, 1:-1, 1:-1]
    western = extended[:, 1:-1, :-2]
    eastern = extended[:, 1:-1, 2:]
    northern = extended[:, :-2, 1:-1]
    southern = extended[:, 2:, 1:-1]
    return (
        center
        - jnp.maximum(courant_x, 0.0) * (center - western)
        - jnp.minimum(courant_x, 0.0) * (eastern - center)
        - jnp.maximum(courant_y, 0.0) * (center - northern)
        - jnp.minimum(courant_y, 0.0) * (southern - center)
    )


def body(spectrum, legendre, wave_numbers, vertical):
    slot_count, degree_count, level_count, part_count = spectrum.shape
    columns = level_count * part_count
    coefficient = spectrum.reshape(slot_count, degree_count, columns)
    first_slot = lax.axis_index("wave") * slot_count
    own_numbers = lax.dynamic_slice_in_dim(wave_numbers, first_slot, slot_count)
    partial_sums = padded_sums(coefficient, legendre, own_numbers)
    even_sums = partial_sums[:, :columns]
    odd_sums = partial_sums[:, columns:]
    northern = even_sums + odd_sums
    southern = jnp.flip(even_sums - odd_sums, axis=2)
    fourier = jnp.concatenate([northern, southern], axis=2).astype(jnp.bfloat16)
    received = lax.all_to_all(fourier, "wave", split_axis=2, concat_axis=0, tiled=True)
    lat_count = received.shape[2]
    received = received.reshape(received.shape[0], level_count, 3, 2, lat_count)
    twiddle = twiddles(wave_numbers)
    grid_values = jnp.einsum(
        "smfrl,rsj->lmfj", received, twiddle, preferred_element_type=jnp.float32
    ).astype(jnp.bfloat16)
    column_values = lax.all_to_all(grid_values, "lev", split_axis=3, concat_axis=1, tiled=True)
    fields = jnp.einsum(
        "vm,lmfj->fvlj",
        vertical,
        column_values.astype(jnp.float32),
        precision=lax.Precision.HIGHEST,
    )
    courant_x = courant_max * jnp.tanh(fields[0])
    courant_y = courant_max * jnp.tanh(fields[1])
    tracer = fields[2]
    for sweep in range(2):
        extended = padded(tracer, (("wave", 1),), 1, False)
        extended = padded(extended, (("lev", 2),), 1, True)
        tracer = upwind_core(extended, courant_x, courant_y)
    return tracer


def solution(mesh):
    in_specs = (P("wave", None, "lev", None), P("wave", None, None), P(), P())
    out_specs = P(None, "wave", "lev")
    return jax.shard_map(body, mesh=mesh, in_specs=in_specs, out_specs=out_specs, check_vma=False)
```

profile of v0, /device:TPU:16, one launch (start us, length us, event | category | flops | bytes accessed | tf_op | source)
XLA Modules:
  0.0 266.5 jit_solution(447221664116549189)
XLA Ops:
  0.0 0.0 copy-start
  0.0 0.0 copy-start.1
  0.0 34.3 %copy.26 = bf16[128,1024,24,6]{1,0,3,2:T(8,128)(2,1)} copy(bf16[128,1024,24,6]{1,2,3,0:T(8,128)(2,1)} %param.4) | data formatting | bytes 75497472 | tf_op args[0]
  34.3 0.0 copy-done.1
  34.3 0.1 dynamic-slice_subtract_fusion
  34.4 0.2 fusion.45
  34.6 39.0 %broadcast_select_fusion.1 = (bf16[128,1024,144]{1,2,0:T(8,128)(2,1)}, bf16[128,1024,144]{1,2,0:T(8,128)(2,1)}) fusion(pred[128,1024]{1,0:T(8,128)(4,1)S(1)} %get-tuple-element.19, bf16[128,1024,144]{1,0,2:T(8,128)(2,1)} %bitcast.87, pred[128,1024]{1,0:T(8,128)(4,1)S(1)} %get-tuple-element.20), kind=kLoop, calls=%fused_computation.5 | loop fusion | flops 37748736 | bytes 113508352 | tf_op jit(solution)/shard_map/jit(_where)/select_n | solution.py:43
  73.6 29.2 %fusion = f32[128,288,16]{1,2,0:T(8,128)S(1)} fusion(bf16[128,1024,16]{1,2,0:T(8,128)(2,1)} %param.5, bf16[128,1024,144]{1,2,0:T(8,128)(2,1)} %get-tuple-element.6, bf16[128,1024,144]{1,2,0:T(8,128)(2,1)} %get-tuple-element.5), kind=kOutput, calls=%fused_computation | convolution fusion | flops 1358954496 | bytes 82051072 | tf_op jit(solution)/shard_map/skc,ski->sci/dot_general | solution.py:54
  102.8 0.6 slice_subtract_fusion
  103.5 1.6 add_convert_fusion
  105.1 1.8 rev.4
  106.9 2.1 pad_maximum_fusion
  109.0 2.9 %copy.29 = bf16[128,144,32]{0,1,2:T(8,128)(2,1)} copy(bf16[128,144,32]{1,2,0:T(8,128)(2,1)S(1)} %pad_maximum_fusion) | data formatting | bytes 2359296 | tf_op jit(solution)/shard_map/concatenate | solution.py:83
  111.9 6.1 %all-to-all-start = ((bf16[128,144,32]{0,1,2:T(8,128)(2,1)}), bf16[128,144,32]{0,1,2:T(8,128)(2,1)S(1)}, u32[]{:S(2)}, u32[]{:S(2)}) async-start(bf16[128,144,32]{0,1,2:T(8,128)(2,1)} %copy.29), calls=%async_computation | async-start | bytes 2359296 | tf_op jit(solution)/shard_map/all_to_all | solution.py:84
  118.0 37.3 %multiply_convert_fusion.1 = (bf16[1,1024,2048]{2,1,0:T(8,128)(2,1)}, bf16[1,1024,2048]{2,1,0:T(8,128)(2,1)}) fusion(s32[1024]{0:T(1024)S(1)} %copy-done.1, f32[1024]{0:T(1024)S(1)} %get-tuple-element.17, f32[1024]{0:T(1024)S(1)} %get-tuple-element.18), kind=kLoop, calls=%fused_computation.17 | loop fusion | flops 37748736 | bytes 8400896 | tf_op jit(solution)/shard_map/convert.2
  155.3 0.0 all-to-all-done
  155.3 0.8 copy.30
  156.1 1.3 reshape.242
  157.3 6.5 %fusion.15 = bf16[4,24,3,2048]{3,1,0,2:T(8,128)(2,1)S(1)} fusion(bf16[1,1024,2048]{2,1,0:T(8,128)(2,1)} %get-tuple-element.16, bf16[1,1024,2048]{2,1,0:T(8,128)(2,1)} %get-tuple-element.15, bf16[1024,24,3,2,4]{0,4,3,2,1:T(4,128)(2,1)} %reshape.242), kind=kOutput, calls=%fused_computation.23 | convolution fusion | flops 2433286144 | bytes 10747904 | tf_op jit(solution)/shard_map/smfrl,rsj->lmfj/dot_general | solution.py:88
  163.8 7.1 %copy.32 = bf16[4,24,3,2048]{1,0,2,3:T(4,128)(2,1)} copy(bf16[4,24,3,2048]{3,1,0,2:T(8,128)(2,1)S(1)} %fusion.15) | data formatting | bytes 2359296 | tf_op jit(solution)/shard_map/convert_element_type | solution.py:90
  170.9 9.5 %reshape.246 = bf16[4,2,73728]{2,1,0:T(2,128)(2,1)S(1)} reshape(bf16[2048,3,4,24]{3,2,1,0:T(4,128)(2,1)} %bitcast.88) | data formatting | bytes 2359296
  180.5 18.4 %all_to_all.33 = bf16[4,2,73728]{2,1,0:T(2,128)(2,1)S(1)} all-to-all(bf16[4,2,73728]{2,1,0:T(2,128)(2,1)S(1)} %reshape.246), channel_id=1, replica_groups=mesh['wave'=8,'lev'=4] {'lev'}, dimensions={0} | all-to-all | bytes 2359296 | tf_op jit(solution)/shard_map/all_to_all | solution.py:91
  198.9 10.2 %reshape.247 = bf16[2048,3,4,24]{3,2,1,0:T(4,128)(2,1)} reshape(bf16[4,2,73728]{2,1,0:T(2,128)(2,1)S(1)} %all_to_all.33) | data formatting | bytes 2359296
  209.1 8.1 %copy.33 = bf16[4,24,3,4,512]{4,1,3,2,0:T(8,128)(2,1)S(1)} copy(bf16[4,24,3,4,512]{1,0,2,4,3:T(4,128)(2,1)} %bitcast.89) | data formatting | bytes 2359296 | tf_op jit(solution)/shard_map/all_to_all | solution.py:91
  217.3 0.0 copy-done
  217.3 1.3 convolution_bitcast_fusion
  218.6 0.1 slice_bitcast_fusion.1
  218.7 3.4 %collective-permute-start = (f32[96,1,512]{2,0,1:T(8,128)S(1)}, f32[96,1,512]{2,0,1:T(8,128)S(1)}, u32[]{:S(2)}, u32[]{:S(2)}) collective-permute-start(f32[96,1,512]{2,0,1:T(8,128)S(1)} %get-tuple-element.13), channel_id=1, source_target_pairs={{0,4},{4,8},{8,12},{12,16},{16,20},{20,24},{24,28},{1,5},{5,9},{9,... | collective-permute-start | bytes 589832 | tf_op jit(solution)/shard_map/ppermute | solution.py:21
  222.0 3.4 %collective-permute-start.1 = (f32[96,1,512]{2,0,1:T(8,128)S(1)}, f32[96,1,512]{2,0,1:T(8,128)S(1)}, u32[]{:S(2)}, u32[]{:S(2)}) collective-permute-start(f32[96,1,512]{2,0,1:T(8,128)S(1)} %get-tuple-element.14), channel_id=1, source_target_pairs={{4,0},{8,4},{12,8},{16,12},{20,16},{24,20},{28,24},{5,1},{9,5},{13... | collective-permute-start | bytes 589832 | tf_op jit(solution)/shard_map/ppermute | solution.py:24
  225.4 2.4 collective-permute-done
  227.8 4.1 %collective-permute-done.1 = f32[96,1,512]{2,0,1:T(8,128)S(1)} collective-permute-done((f32[96,1,512]{2,0,1:T(8,128)S(1)}, f32[96,1,512]{2,0,1:T(8,128)S(1)}, u32[]{:S(2)}, u32[]{:S(2)}) %collective-permute-start.1) | collective-permute-done | bytes 196640 | tf_op jit(solution)/shard_map/ppermute | solution.py:24
  232.0 0.2 pad_maximum_fusion.22
  232.1 0.1 collective-permute-start.2
  232.2 1.7 collective-permute-start.3
  233.9 6.4 %collective-permute-done.2 = f32[96,6,1]{2,0,1:T(8,128)S(1)} collective-permute-done((f32[96,6,1]{2,0,1:T(8,128)S(1)}, f32[96,6,1]{2,0,1:T(8,128)S(1)}, u32[]{:S(2)}, u32[]{:S(2)}) %collective-permute-start.2) | collective-permute-done | bytes 2336 | tf_op jit(solution)/shard_map/ppermute | solution.py:21
  240.3 0.0 collective-permute-done.3
  240.3 0.7 fusion.31
  241.1 2.5 collective-permute-start.4
  243.5 4.3 %collective-permute-start.5 = (f32[96,1,512]{2,0,1:T(8,128)S(1)}, f32[96,1,512]{2,0,1:T(8,128)S(1)}, u32[]{:S(2)}, u32[]{:S(2)}) collective-permute-start(f32[96,1,512]{2,0,1:T(8,128)S(1)} %get-tuple-element.12), channel_id=1, source_target_pairs={{4,0},{8,4},{12,8},{16,12},{20,16},{24,20},{28,24},{5,1},{9,5},{13... | collective-permute-start | bytes 589832 | tf_op jit(solution)/shard_map/ppermute | solution.py:24
  247.8 3.9 %collective-permute-done.4 = f32[96,1,512]{2,0,1:T(8,128)S(1)} collective-permute-done((f32[96,1,512]{2,0,1:T(8,128)S(1)}, f32[96,1,512]{2,0,1:T(8,128)S(1)}, u32[]{:S(2)}, u32[]{:S(2)}) %collective-permute-start.4) | collective-permute-done | bytes 196640 | tf_op jit(solution)/shard_map/ppermute | solution.py:21
  251.7 4.1 %collective-permute-done.5 = f32[96,1,512]{2,0,1:T(8,128)S(1)} collective-permute-done((f32[96,1,512]{2,0,1:T(8,128)S(1)}, f32[96,1,512]{2,0,1:T(8,128)S(1)}, u32[]{:S(2)}, u32[]{:S(2)}) %collective-permute-start.5) | collective-permute-done | bytes 196640 | tf_op jit(solution)/shard_map/ppermute | solution.py:24
  255.8 0.2 pad_maximum_fusion.19
  256.0 0.2 collective-permute-start.6
  256.2 1.6 collective-permute-start.7
  257.8 6.6 %collective-permute-done.6 = f32[96,6,1]{2,0,1:T(8,128)S(1)} collective-permute-done((f32[96,6,1]{2,0,1:T(8,128)S(1)}, f32[96,6,1]{2,0,1:T(8,128)S(1)}, u32[]{:S(2)}, u32[]{:S(2)}) %collective-permute-start.6) | collective-permute-done | bytes 2336 | tf_op jit(solution)/shard_map/ppermute | solution.py:21
  264.4 0.0 collective-permute-done.7
  264.4 0.7 fusion.19
  265.1 1.4 copy.39
  (4 shorter events, 0.1 us)
Async XLA Ops:
  0.0 217.3 %copy-start = (f32[96,96]{1,0:T(8,128)S(1)}, f32[96,96]{1,0:T(8,128)}, u32[]{:S(2)}) copy-start(f32[96,96]{1,0:T(8,128)} %param.7) | copy-start | bytes 110596
  0.0 34.3 %copy-start.1 = (s32[1024]{0:T(1024)S(1)}, s32[1024]{0:T(1024)}, u32[]{:S(2)}) copy-start(s32[1024]{0:T(1024)} %param.6) | copy-start | bytes 12292
  111.9 43.4 %all-to-all-start = ((bf16[128,144,32]{0,1,2:T(8,128)(2,1)}), bf16[128,144,32]{0,1,2:T(8,128)(2,1)S(1)}, u32[]{:S(2)}, u32[]{:S(2)}) async-start(bf16[128,144,32]{0,1,2:T(8,128)(2,1)} %copy.29), calls=%async_computation | async-start | bytes 2359296 | tf_op jit(solution)/shard_map/all_to_all | solution.py:84
  218.7 9.2 %collective-permute-start = (f32[96,1,512]{2,0,1:T(8,128)S(1)}, f32[96,1,512]{2,0,1:T(8,128)S(1)}, u32[]{:S(2)}, u32[]{:S(2)}) collective-permute-start(f32[96,1,512]{2,0,1:T(8,128)S(1)} %get-tuple-element.13), channel_id=1, source_target_pairs={{0,4},{4,8},{8,12},{12,16},{16,20},{20,24},{24,28},{1,5},{5,9},{9,... | collective-permute-start | bytes 589832 | tf_op jit(solution)/shard_map/ppermute | solution.py:21
  222.0 9.9 %collective-permute-start.1 = (f32[96,1,512]{2,0,1:T(8,128)S(1)}, f32[96,1,512]{2,0,1:T(8,128)S(1)}, u32[]{:S(2)}, u32[]{:S(2)}) collective-permute-start(f32[96,1,512]{2,0,1:T(8,128)S(1)} %get-tuple-element.14), channel_id=1, source_target_pairs={{4,0},{8,4},{12,8},{16,12},{20,16},{24,20},{28,24},{5,1},{9,5},{13... | collective-permute-start | bytes 589832 | tf_op jit(solution)/shard_map/ppermute | solution.py:24
  232.1 8.2 %collective-permute-start.2 = (f32[96,6,1]{2,0,1:T(8,128)S(1)}, f32[96,6,1]{2,0,1:T(8,128)S(1)}, u32[]{:S(2)}, u32[]{:S(2)}) collective-permute-start(f32[96,6,1]{2,0,1:T(8,128)S(1)} %get-tuple-element.9), channel_id=1, source_target_pairs={{0,1},{1,2},{2,3},{3,0},{4,5},{5,6},{6,7},{7,4},{8,9},{9,10},{10,1... | collective-permute-start | bytes 6920 | tf_op jit(solution)/shard_map/ppermute | solution.py:21
  232.2 8.1 %collective-permute-start.3 = (f32[96,6,1]{2,0,1:T(8,128)S(1)}, f32[96,6,1]{2,0,1:T(8,128)S(1)}, u32[]{:S(2)}, u32[]{:S(2)}) collective-permute-start(f32[96,6,1]{2,0,1:T(8,128)S(1)} %get-tuple-element.10), channel_id=1, source_target_pairs={{1,0},{2,1},{3,2},{0,3},{5,4},{6,5},{7,6},{4,7},{9,8},{10,9},{11,1... | collective-permute-start | bytes 6920 | tf_op jit(solution)/shard_map/ppermute | solution.py:24
  241.1 10.7 %collective-permute-start.4 = (f32[96,1,512]{2,0,1:T(8,128)S(1)}, f32[96,1,512]{2,0,1:T(8,128)S(1)}, u32[]{:S(2)}, u32[]{:S(2)}) collective-permute-start(f32[96,1,512]{2,0,1:T(8,128)S(1)} %get-tuple-element.11), channel_id=1, source_target_pairs={{0,4},{4,8},{8,12},{12,16},{16,20},{20,24},{24,28},{1,5},{5,9},{9,... | collective-permute-start | bytes 589832 | tf_op jit(solution)/shard_map/ppermute | solution.py:21
  243.5 12.3 %collective-permute-start.5 = (f32[96,1,512]{2,0,1:T(8,128)S(1)}, f32[96,1,512]{2,0,1:T(8,128)S(1)}, u32[]{:S(2)}, u32[]{:S(2)}) collective-permute-start(f32[96,1,512]{2,0,1:T(8,128)S(1)} %get-tuple-element.12), channel_id=1, source_target_pairs={{4,0},{8,4},{12,8},{16,12},{20,16},{24,20},{28,24},{5,1},{9,5},{13... | collective-permute-start | bytes 589832 | tf_op jit(solution)/shard_map/ppermute | solution.py:24
  256.0 8.4 %collective-permute-start.6 = (f32[96,6,1]{2,0,1:T(8,128)S(1)}, f32[96,6,1]{2,0,1:T(8,128)S(1)}, u32[]{:S(2)}, u32[]{:S(2)}) collective-permute-start(f32[96,6,1]{2,0,1:T(8,128)S(1)} %get-tuple-element.7), channel_id=1, source_target_pairs={{0,1},{1,2},{2,3},{3,0},{4,5},{5,6},{6,7},{7,4},{8,9},{9,10},{10,1... | collective-permute-start | bytes 6920 | tf_op jit(solution)/shard_map/ppermute | solution.py:21
  256.2 8.2 %collective-permute-start.7 = (f32[96,6,1]{2,0,1:T(8,128)S(1)}, f32[96,6,1]{2,0,1:T(8,128)S(1)}, u32[]{:S(2)}, u32[]{:S(2)}) collective-permute-start(f32[96,6,1]{2,0,1:T(8,128)S(1)} %get-tuple-element.8), channel_id=1, source_target_pairs={{1,0},{2,1},{3,2},{0,3},{5,4},{6,5},{7,6},{4,7},{9,8},{10,9},{11,1... | collective-permute-start | bytes 6920 | tf_op jit(solution)/shard_map/ppermute | solution.py:24
where the time goes:
time: 268 us; the launch traced here: 266 us
  other arithmetic  82.6 us (31%)
  local copies, waits for them, and re-layouts  77.5 us (29%)
  matrix products  37 us (14%)
  waiting for transfers between devices  27.5 us (10%)
  starting transfers between devices  23.2 us (9%)
  blocking collectives  18.4 us (7%)
    unnamed x7, local copies, waits for them, and re-layouts  54.1 us
    select_n x1, other arithmetic, parity_columns(): jnp.where(even_mask[:, :, None], coefficient, 0)  39 us
    another operation x2, other arithmetic  38.9 us
    dot_general x1, matrix products, padded_sums(): jnp.einsum('skc,ski->sci', masked, basis, preferred_element_type=jnp.floa...  29.2 us
    ppermute x4, waiting for transfers between devices, padded(): lax.ppermute(lax.slice_in_dim(block, block.shape[dim] - width, None, axis...  19.3 us
    all_to_all x1, blocking collectives, body(): lax.all_to_all(grid_values, 'lev', split_axis=3, concat_axis=1, tiled=True)  18.4 us
    ppermute x4, starting transfers between devices, padded(): lax.ppermute(lax.slice_in_dim(block, 0, width, axis=dim), axis, backward)  11 us
    ppermute x4, waiting for transfers between devices, padded(): lax.ppermute(lax.slice_in_dim(block, 0, width, axis=dim), axis, backward)  8.23 us
  transfers between devices with their start and end apart: 9, of which 6 were waited for; matrix products, arithmetic and copies ran while one was open for 14% of the time, Pallas kernels for 0%

commit v1 on v0

--- a/solution.py
+++ b/solution.py
@@ -1,12 +1,19 @@
+import functools
 import math
 
 import jax
 import jax.numpy as jnp
 from jax import lax
+from jax.experimental import pallas as pl
+from jax.experimental.pallas import tpu as pltpu
 from jax.sharding import PartitionSpec as P
 
 NLON = 2048
-
+FIELDS = 3
+PARTS = 2
+LANES = 128
+CHUNK = 256
+TILE = 256
 
 courant_max = 0.45
 
@@ -69,7 +76,7 @@
     )
 
 
-def body(spectrum, legendre, wave_numbers, vertical):
+def plain_body(spectrum, legendre, wave_numbers, vertical):
     slot_count, degree_count, level_count, part_count = spectrum.shape
     columns = level_count * part_count
     coefficient = spectrum.reshape(slot_count, degree_count, columns)
@@ -83,7 +90,7 @@
     fourier = jnp.concatenate([northern, southern], axis=2).astype(jnp.bfloat16)
     received = lax.all_to_all(fourier, "wave", split_axis=2, concat_axis=0, tiled=True)
     lat_count = received.shape[2]
-    received = received.reshape(received.shape[0], level_count, 3, 2, lat_count)
+    received = received.reshape(received.shape[0], level_count, FIELDS, PARTS, lat_count)
     twiddle = twiddles(wave_numbers)
     grid_values = jnp.einsum(
         "smfrl,rsj->lmfj", received, twiddle, preferred_element_type=jnp.float32
@@ -105,6 +112,460 @@
     return tracer
 
 
+def vmem():
+    return pl.BlockSpec(memory_space=pltpu.VMEM)
+
+
+def cost(flops, count_bytes):
+    return pl.CostEstimate(flops=flops, bytes_accessed=count_bytes, transcendentals=0)
+
+
+def legendre_kernel(
+    waves, lats, modes, pairs, numbers_ref, place_ref, spectrum_ref, legendre_ref, *refs
+):
+    outs, (held, sums, arrived) = refs[:-3], refs[-3:]
+    half = legendre_ref.shape[1]
+    degrees = legendre_ref.shape[2]
+    rows = spectrum_ref.shape[1]
+    slots = spectrum_ref.shape[0]
+    chunks = degrees // CHUNK + 1
+    step, steps = pl.program_id(0), pl.num_programs(0)
+
+    def plan(pair):
+        first = degrees - numbers_ref[2 * pair]
+        second = degrees - numbers_ref[2 * pair + 1]
+        return first, second, (first + CHUNK - 1) // CHUNK
+
+    def copy(group, slot, pair, t):
+        index = group * pairs + pair
+        _, _, edge = plan(index)
+        inside = t < edge
+        source = 2 * index + jnp.where(inside, 0, 1)
+        block = jnp.where(inside, t, t - edge)
+        start = pl.multiple_of(block * CHUNK, CHUNK)
+        return pltpu.make_async_copy(
+            spectrum_ref.at[source, :, pl.ds(start, CHUNK)],
+            held.at[slot, pair, :, pl.ds(t * CHUNK, CHUNK)],
+            arrived.at[slot],
+        )
+
+    def fetch(group, slot):
+        for pair in range(pairs):
+            for t in range(chunks):
+                copy(group, slot, pair, t).start()
+
+    @pl.when(step == 0)
+    def _():
+        fetch(0, 0)
+
+    now = lax.rem(step, 2)
+
+    @pl.when(step + 1 < steps)
+    def _():
+        fetch(step + 1, 1 - now)
+
+    for pair in range(pairs):
+        for t in range(chunks):
+            copy(step, now, pair, t).wait()
+
+    lane = lax.broadcasted_iota(jnp.int32, (half, CHUNK), 1)
+    sign = jnp.where(lane % 2 == 0, 1.0, -1.0)
+    for pair in range(pairs):
+        index = step * pairs + pair
+        first, second, edge = plan(index)
+        columns = []
+        for t in range(chunks):
+            inside = t < edge
+            local = 2 * pair + jnp.where(inside, 0, 1)
+            block = jnp.where(inside, t, t - edge)
+            start = pl.multiple_of(block * CHUNK, CHUNK)
+            length = jnp.where(inside, first, second) - start
+            values = legendre_ref[local, :, pl.ds(start, CHUNK)].astype(jnp.float32)
+            values = jnp.where(lane < length, values, 0.0)
+            own = jnp.where(inside, 1.0, 0.0)
+            north_first = values * own
+            north_second = values - north_first
+            columns.append(
+                jnp.concatenate(
+                    [
+                        north_first,
+                        north_first * sign,
+                        north_second,
+                        north_second * sign,
+                    ],
+                    axis=0,
+                ).astype(jnp.bfloat16)
+            )
+        basis = jnp.concatenate(columns, axis=1)
+        result = lax.dot_general(
+            basis,
+            held[now, pair],
+            (((1,), (1,)), ((), ())),
+            preferred_element_type=jnp.float32,
+        )
+        for which in range(2):
+            part = result[which * 2 * half : (which + 1) * 2 * half]
+            for low in range(0, rows, LANES):
+                width = min(LANES, rows - low)
+                sums[low // LANES, pl.ds(2 * index + which, 2 * half, stride=slots), :width] = part[
+                    :, low : low + width
+                ]
+
+    @pl.when(step == steps - 1)
+    def _():
+        place = place_ref[0]
+        for d in range(waves):
+            for l in range(lats):
+                lat = (place ^ d) * lats + l
+                row = jnp.where(lat < half, lat, 3 * half - 1 - lat)
+                start = pl.multiple_of(row * slots, slots)
+                turned = [
+                    sums[low // LANES, pl.ds(start, slots), :].T.astype(jnp.bfloat16)
+                    for low in range(0, rows, LANES)
+                ]
+                whole = jnp.concatenate(turned, axis=0)
+                for f in range(FIELDS):
+                    for p in range(PARTS):
+                        base = (f * PARTS + p) * modes
+                        outs[f * waves + d][p, l] = whole[base : base + modes]
+
+
+def legendre_stage(spectrum, legendre, own_numbers, place, waves):
+    slots, degrees, modes, _ = spectrum.shape
+    half = legendre.shape[2]
+    lats = 2 * half // waves
+    rows = modes * FIELDS * PARTS
+    turned = jnp.transpose(spectrum, (0, 3, 2, 1)).reshape(slots, rows, degrees)
+    basis = jnp.transpose(legendre, (0, 2, 1))
+    pairs = 4
+    chunks = degrees // CHUNK + 1
+    outs = [jax.ShapeDtypeStruct((PARTS, lats, modes, slots), jnp.bfloat16)] * (FIELDS * waves)
+    tiles = -(-rows // LANES)
+    return pl.pallas_call(
+        functools.partial(legendre_kernel, waves, lats, modes, pairs),
+        out_shape=outs,
+        grid_spec=pltpu.PrefetchScalarGridSpec(
+            num_scalar_prefetch=2,
+            grid=(slots // (2 * pairs),),
+            in_specs=[
+                pl.BlockSpec(memory_space=pl.ANY),
+                pl.BlockSpec((2 * pairs, half, degrees), lambda i, *_: (i, 0, 0)),
+            ],
+            out_specs=[
+                pl.BlockSpec((PARTS, lats, modes, slots), lambda i, *_: (0, 0, 0, 0))
+                for _ in outs
+            ],
+            scratch_shapes=[
+                pltpu.VMEM((2, pairs, rows, chunks * CHUNK), jnp.bfloat16),
+                pltpu.VMEM((tiles, 2 * half * slots, LANES), jnp.float32),
+                pltpu.SemaphoreType.DMA((2,)),
+            ],
+        ),
+        compiler_params=pltpu.CompilerParams(dimension_semantics=("arbitrary",)),
+        cost_estimate=cost(slots * rows * degrees * 2 * half, slots * rows * degrees),
+        name="legendre_sums",
+    )(own_numbers, place, turned, basis)
+
+
+def twiddle_kernel(low_cos_ref, low_sin_ref, high_cos_ref, high_sin_ref, out_ref):
+    low_cos, low_sin = low_cos_ref[0], low_sin_ref[0]
+    for block in range(out_ref.shape[3] // LANES):
+        high_cos = high_cos_ref[0, :, block : block + 1]
+        high_sin = high_sin_ref[0, :, block : block + 1]
+        lanes = pl.ds(block * LANES, LANES)
+        out_ref[0, 0, :, lanes] = (high_cos * low_cos - high_sin * low_sin).astype(jnp.bfloat16)
+        out_ref[0, 1, :, lanes] = -(high_sin * low_cos + high_cos * low_sin).astype(jnp.bfloat16)
+
+
+def twiddle_stage(numbers):
+    waves, slots = numbers.shape
+    count = NLON // 2
+    blocks = count // LANES
+
+    def angles(steps):
+        residue = numbers[:, :, None] * steps[None, None, :] % NLON
+        return residue.astype(jnp.float32) * (2.0 * math.pi / NLON)
+
+    low = angles(jnp.arange(LANES, dtype=jnp.int32))
+    high = angles(jnp.arange(blocks, dtype=jnp.int32) * LANES)
+    weight = jnp.where(numbers == 0, 1.0, 2.0).astype(jnp.float32)[:, :, None]
+
+    def spec(last):
+        return pl.BlockSpec((1, slots, last), lambda i: (i, 0, 0))
+
+    return pl.pallas_call(
+        twiddle_kernel,
+        out_shape=jax.ShapeDtypeStruct((waves, PARTS, slots, count), jnp.bfloat16),
+        grid=(waves,),
+        in_specs=[spec(LANES), spec(LANES), spec(blocks), spec(blocks)],
+        out_specs=pl.BlockSpec((1, PARTS, slots, count), lambda i: (i, 0, 0, 0)),
+        cost_estimate=cost(8 * waves * slots * count, 4 * waves * slots * count),
+        name="twiddles",
+    )(jnp.cos(low), jnp.sin(low), weight * jnp.cos(high), weight * jnp.sin(high))
+
+
+def synthesis_kernel(waves, levs, place_ref, *refs):
+    blocks, (sign_ref, twiddle_ref) = refs[:waves], refs[waves : waves + 2]
+    outs, (left, grid) = refs[waves + 2 : -2], refs[-2:]
+    _, lats, modes, slots = blocks[0].shape
+    rows = lats * modes
+    step, steps = pl.program_id(0), pl.num_programs(0)
+
+    @pl.when(step == 0)
+    def _():
+        for d in range(waves):
+            sign = sign_ref[d]
+            for p in range(PARTS):
+                values = blocks[d][p].reshape(rows, slots)
+                lanes = pl.ds((d * PARTS + p) * slots, slots)
+                left[:rows, lanes] = values
+                left[rows:, lanes] = values * sign
+
+    right = twiddle_ref[...].reshape(waves * PARTS * slots, TILE)
+    result = jnp.dot(left[...], right, preferred_element_type=jnp.float32).astype(jnp.bfloat16)
+    width = NLON // levs
+    ratio = width // TILE
+    lane = lax.broadcasted_iota(jnp.int32, (rows, LANES), 1)
+    for which in range(2):
+        values = result[which * rows : (which + 1) * rows]
+        block = step + which * steps
+        owner = block // ratio
+        inner = lax.rem(block, ratio)
+        start = pl.multiple_of(inner * TILE, TILE)
+        grid[owner, :, pl.ds(start, TILE)] = values
+
+        @pl.when(inner == 0)
+        def _():
+            west = lax.rem(owner + levs - 1, levs)
+            grid[west, :, pl.ds(width, LANES)] = jnp.where(
+                lane < LANES // 2, values[:, :LANES], grid[west, :, pl.ds(width, LANES)]
+            )
+
+        @pl.when(inner == ratio - 1)
+        def _():
+            east = lax.rem(owner + 1, levs)
+            grid[east, :, pl.ds(width, LANES)] = jnp.where(
+                lane < LANES // 2, grid[east, :, pl.ds(width, LANES)], values[:, -LANES:]
+            )
+
+    @pl.when(step == steps - 1)
+    def _():
+        place = place_ref[0]
+        for e in range(levs):
+            outs[e][...] = grid[place ^ e]
+
+
+def synthesis_stage(blocks, sign, twiddle, place, levs):
+    waves, _, slots, count = twiddle.shape
+    _, lats, modes, _ = blocks[0].shape
+    rows = lats * modes
+    width = NLON // levs + LANES
+    depth = waves * PARTS * slots
+    return pl.pallas_call(
+        functools.partial(synthesis_kernel, waves, levs),
+        out_shape=[jax.ShapeDtypeStruct((rows, width), jnp.bfloat16)] * levs,
+        grid_spec=pltpu.PrefetchScalarGridSpec(
+            num_scalar_prefetch=1,
+            grid=(count // TILE,),
+            in_specs=[
+                pl.BlockSpec((PARTS, lats, modes, slots), lambda i, *_: (0, 0, 0, 0))
+                for _ in blocks
+            ]
+            + [
+                pl.BlockSpec((waves, 1, slots), lambda i, *_: (0, 0, 0)),
+                pl.BlockSpec((waves, PARTS, slots, TILE), lambda i, *_: (0, 0, 0, i)),
+            ],
+            out_specs=[pl.BlockSpec((rows, width), lambda i, *_: (0, 0))] * levs,
+            scratch_shapes=[
+                pltpu.VMEM((2 * rows, depth), jnp.bfloat16),
+                pltpu.VMEM((levs, rows, width), jnp.bfloat16),
+            ],
+        ),
+        compiler_params=pltpu.CompilerParams(dimension_semantics=("arbitrary",)),
+        cost_estimate=cost(4 * rows * depth * count, 2 * depth * count),
+        name="synthesis",
+    )(place, *blocks, sign, twiddle)
+
+
+def three_terms(matrix):
+    high = matrix.astype(jnp.bfloat16)
+    rest = matrix - high.astype(jnp.float32)
+    middle = rest.astype(jnp.bfloat16)
+    low = (rest - middle.astype(jnp.float32)).astype(jnp.bfloat16)
+    return jnp.concatenate([high, middle, low], axis=0)
+
+
+def levels_of(terms, blocks, lat, modes):
+    count = terms.shape[0] // 3
+    rows = jnp.concatenate(
+        [block[lat * modes : (lat + 1) * modes].astype(jnp.float32) for block in blocks], axis=0
+    ).astype(jnp.bfloat16)
+    result = jnp.dot(terms, rows, preferred_element_type=jnp.float32)
+    return result[:count] + (result[count : 2 * count] + result[2 * count :])
+
+
+def tracer_kernel(modes, vertical_ref, *refs):
+    blocks, (field_ref, north_ref, south_ref) = refs[:-3], refs[-3:]
+    terms = three_terms(vertical_ref[...])
+    lats = field_ref.shape[0]
+    for lat in range(lats):
+        values = levels_of(terms, blocks, lat, modes)
+        field_ref[lat] = values
+        if lat == 0:
+            north_ref[...] = values.astype(jnp.bfloat16)
+        if lat == lats - 1:
+            south_ref[...] = values.astype(jnp.bfloat16)
+
+
+def courant_kernel(modes, vertical_ref, *refs):
+    blocks, field_ref = refs[:-1], refs[-1]
+    terms = three_terms(vertical_ref[...])
+    for lat in range(field_ref.shape[0]):
+        field_ref[lat] = courant_max * jnp.tanh(levels_of(terms, blocks, lat, modes))
+
+
+def upwind(center, western, eastern, northern, southern, courant_x, courant_y):
+    return (
+        center
+        - jnp.maximum(courant_x, 0.0) * (center - western)
+        - jnp.minimum(courant_x, 0.0) * (eastern - center)
+        - jnp.maximum(courant_y, 0.0) * (center - northern)
+        - jnp.minimum(courant_y, 0.0) * (southern - center)
+    )
+
+
+def stepped(lat, tracer_ref, above_ref, below_ref, courant_x, courant_y):
+    lats, _, width = tracer_ref.shape
+    center = tracer_ref[lat]
+    northern = tracer_ref[lat - 1] if lat > 0 else above_ref[...].astype(jnp.float32)
+    southern = tracer_ref[lat + 1] if lat < lats - 1 else below_ref[...].astype(jnp.float32)
+    return upwind(
+        center,
+        pltpu.roll(center, 1, 1),
+        pltpu.roll(center, width - 1, 1),
+        northern,
+        southern,
+        courant_x,
+        courant_y,
+    )
+
+
+def first_step_kernel(modes, vertical_ref, tracer_ref, above_ref, below_ref, x_ref, *refs):
+    blocks, (y_ref, out_ref, north_ref, south_ref) = refs[:-4], refs[-4:]
+    terms = three_terms(vertical_ref[...])
+    lats = tracer_ref.shape[0]
+    for lat in range(lats):
+        courant_y = courant_max * jnp.tanh(levels_of(terms, blocks, lat, modes))
+        y_ref[lat] = courant_y
+        values = stepped(lat, tracer_ref, above_ref, below_ref, x_ref[lat], courant_y)
+        out_ref[lat] = values
+        if lat == 0:
+            north_ref[...] = values.astype(jnp.bfloat16)
+        if lat == lats - 1:
+            south_ref[...] = values.astype(jnp.bfloat16)
+
+
+def second_step_kernel(tracer_ref, above_ref, below_ref, x_ref, y_ref, out_ref):
+    width = out_ref.shape[2]
+    for lat in range(tracer_ref.shape[0]):
+        values = stepped(lat, tracer_ref, above_ref, below_ref, x_ref[lat], y_ref[lat])
+        out_ref[:, lat, :] = values[:, :width]
+
+
+def local_call(kernel, outs, name, *operands):
+    return pl.pallas_call(
+        kernel,
+        out_shape=outs,
+        in_specs=[vmem() for _ in operands],
+        out_specs=jax.tree.map(lambda _: vmem(), outs),
+        cost_estimate=cost(4_000_000, 4_000_000),
+        name=name,
+    )(*operands)
+
+
+def exchange(blocks, axis):
+    count = lax.axis_size(axis)
+    return [blocks[0]] + [
+        lax.ppermute(blocks[d], axis, [(i, i ^ d) for i in range(count)]) for d in range(1, count)
+    ]
+
+
+def edges(north, south):
+    count = lax.axis_size("wave")
+    above = lax.ppermute(south, "wave", [(i, i + 1) for i in range(count - 1)])
+    below = lax.ppermute(north, "wave", [(i + 1, i) for i in range(count - 1)])
+    return above, below
+
+
+def tiled_body(spectrum, legendre, wave_numbers, vertical):
+    waves, levs = lax.axis_size("wave"), lax.axis_size("lev")
+    slots, degrees, modes, _ = spectrum.shape
+    levels = vertical.shape[0]
+    lats = 2 * legendre.shape[2] // waves
+    width = NLON // levs
+    wave_place, lev_place = lax.axis_index("wave"), lax.axis_index("lev")
+    by_wave = wave_numbers.reshape(waves, slots)[wave_place ^ jnp.arange(waves)]
+    by_lev = vertical.reshape(levels, levs, modes)[:, lev_place ^ jnp.arange(levs)]
+    by_lev = by_lev.reshape(levels, levs * modes)
+    sign = jnp.where(by_wave % 2 == 0, 1.0, -1.0).astype(jnp.bfloat16)[:, None, :]
+
+    fourier = legendre_stage(spectrum, legendre, by_wave[0], wave_place[None], waves)
+    twiddle = twiddle_stage(by_wave)
+    columns = {}
+    for field in (2, 0, 1):
+        received = exchange(fourier[field * waves : (field + 1) * waves], "wave")
+        grid = synthesis_stage(received, sign, twiddle, lev_place[None], levs)
+        columns[field] = exchange(grid, "lev")
+
+    whole = jax.ShapeDtypeStruct((lats, levels, width + LANES), jnp.float32)
+    row = jax.ShapeDtypeStruct((levels, width + LANES), jnp.bfloat16)
+    tracer, north, south = local_call(
+        functools.partial(tracer_kernel, modes), (whole, row, row), "tracer", by_lev, *columns[2]
+    )
+    above, below = edges(north, south)
+    courant_x = local_call(
+        functools.partial(courant_kernel, modes), whole, "courant_x", by_lev, *columns[0]
+    )
+    courant_y, tracer, north, south = local_call(
+        functools.partial(first_step_kernel, modes),
+        (whole, whole, row, row),
+        "first_step",
+        by_lev,
+        tracer,
+        above,
+        below,
+        courant_x,
+        *columns[1],
+    )
+    above, below = edges(north, south)
+    return local_call(
+        second_step_kernel,
+        jax.ShapeDtypeStruct((levels, lats, width), jnp.float32),
+        "second_step",
+        tracer,
+        above,
+        below,
+        courant_x,
+        courant_y,
+    )
+
+
+def body(spectrum, legendre, wave_numbers, vertical):
+    waves, levs = lax.axis_size("wave"), lax.axis_size("lev")
+    slots, degrees, modes, _ = spectrum.shape
+    tiled = (
+        slots % LANES == 0
+        and modes % 8 == 0
+        and degrees % CHUNK == 0
+        and waves & (waves - 1) == 0
+        and levs & (levs - 1) == 0
+        and NLON // levs % TILE == 0
+        and levs % 2 == 0
+    )
+    form = tiled_body if tiled else plain_body
+    return form(spectrum, legendre, wave_numbers, vertical)
+
+
 def solution(mesh):
     in_specs = (P("wave", None, "lev", None), P("wave", None, None), P(), P())
     out_specs = P(None, "wave", "lev")

time: 268 us -> 134 us (0.50)
  other arithmetic: 82.6 us -> 6.86 us
  local copies, waits for them, and re-layouts: 77.5 us -> 5.29 us
  Pallas kernels: 0 us -> 57.4 us
  matrix products: 37 us -> 0 us
  starting transfers between devices: 23.2 us -> 51 us
  blocking collectives: 18.4 us -> 0 us
  waiting for transfers between devices: 27.5 us -> 11.3 us
    pallas_call x0 -> x9, Pallas kernels: none -> 57.4 us  [the longest x1 22.5 us: legendre_stage(): pl.pallas_call(functools.partial(legendre_kernel, waves, lats, modes, pai...]
    unnamed x7 -> x103, local copies, waits for them, and re-layouts: 54.1 us -> 2.7 us
    select_n x2 -> x3, other arithmetic: 39 us -> 0.02 us  [the longest x1 0.01 us: tiled_body(): vertical.reshape(levels, levs, modes)[:, lev_place ^ jnp.arange(levs)]]
    another operation x2 -> x0, other arithmetic: 38.9 us -> none
    dot_general x3 -> x0, matrix products: 37 us -> none  [the longest x1 29.2 us: padded_sums(): jnp.einsum('skc,ski->sci', masked, basis, preferred_element_type=jnp.floa...]
    ppermute x8 -> x34, starting transfers between devices: 17.1 us -> 51 us  [the longest x30 37.5 us: exchange(): lax.ppermute(blocks[d], axis, [(i, i ^ d) for i in range(count)])]
    all_to_all x1 -> x0, blocking collectives: 18.4 us -> none  [body(): lax.all_to_all(grid_values, 'lev', split_axis=3, concat_axis=1, tiled=True)]
    ppermute x8 -> x34, waiting for transfers between devices: 27.5 us -> 11.3 us  [the longest x2 6.83 us: edges(): below = lax.ppermute(north, 'wave', [(i + 1, i) for i in range(count - 1)])]
  transfers between devices with their start and end apart: 9 -> 34, of which waited for: 6 -> 5; matrix products, arithmetic and copies ran while one was open for 14% -> 6% of each run, Pallas kernels for 0% -> 21%
where the time goes in v1:
time: 134 us; the launch traced here: 132 us
  Pallas kernels  57.4 us (43%)
  starting transfers between devices  51 us (38%)
  waiting for transfers between devices  11.3 us (8%)
  other arithmetic  6.86 us (5%)
  local copies, waits for them, and re-layouts  5.29 us (4%)
    ppermute x30, starting transfers between devices, exchange(): lax.ppermute(blocks[d], axis, [(i, i ^ d) for i in range(count)])  37.5 us
    pallas_call x1, Pallas kernels, legendre_stage(): pl.pallas_call(functools.partial(legendre_kernel, waves, lats, modes, pai...  22.5 us
    pallas_call x3, Pallas kernels, synthesis_stage(): pl.pallas_call(functools.partial(synthesis_kernel, waves, levs), out_shap...  14.7 us
    pallas_call x4, Pallas kernels, local_call(): pl.pallas_call(kernel, out_shape=outs, in_specs=[vmem() for _ in operands...  12.8 us
    pallas_call x1, Pallas kernels, twiddle_stage(): pl.pallas_call(twiddle_kernel, out_shape=jax.ShapeDtypeStruct((waves, PAR...  7.38 us
    ppermute x2, starting transfers between devices, edges(): below = lax.ppermute(north, 'wave', [(i + 1, i) for i in range(count - 1)])  6.93 us
    ppermute x2, waiting for transfers between devices, edges(): below = lax.ppermute(north, 'wave', [(i + 1, i) for i in range(count - 1)])  6.83 us
    ppermute x2, starting transfers between devices, edges(): above = lax.ppermute(south, 'wave', [(i, i + 1) for i in range(count - 1)])  6.53 us
  transfers between devices with their start and end apart: 34, of which 5 were waited for; matrix products, arithmetic and copies ran while one was open for 6% of the time, Pallas kernels for 21%

profile of v1, /device:TPU:16, one launch (start us, length us, event | category | flops | bytes accessed | tf_op | source)
XLA Modules:
  0.0 132.3 jit_solution(4610633175324210853)
XLA Ops:
  0.0 0.7 copy-done
  0.7 0.6 gather_fusion.1
  1.2 0.6 slice_bitcast_fusion.numbers_ref
  1.8 22.5 %legendre_sums.1 = (bf16[2,4,24,128]{3,2,1,0:T(8,128)(2,1)}, bf16[2,4,24,128]{3,2,1,0:T(8,128)(2,1)}, bf16[2,4,24,128]{3,2,1,0:T(8,128)(2,1)}, bf16[2,4,24,128]{...) custom-call(s32[128]{0:T(128)} %slice_bitcast_fusion.numbers_ref, ...), custom_call_target="tpu_custom_call" | custom-call | flops 603979776 | bytes 18874368 | tf_op jit(solution)/shard_map/legendre_sums/pallas_call | solution.py:244
  24.3 1.6 %collective-permute-start.22 = (bf16[2,4,24,128]{3,2,1,0:T(8,128)(2,1)}, bf16[2,4,24,128]{3,2,1,0:T(8,128)(2,1)S(1)}, u32[]{:S(2)}, u32[]{:S(2)}) collective-permute-start(bf16[2,4,24,128]{3,2,1,0:T(8,128)(2,1)} %get-tuple-element.76), channel_id=1, source_target_pairs={{0,4},{4,0},{8,12},{12,8},{16,20},{20,16},{24,28},{28,24},{1,5},{5... | collective-permute-start | bytes 147464 | tf_op jit(solution)/shard_map/ppermute | solution.py:489
  25.9 0.5 collective-permute-start
  26.4 1.6 %collective-permute-start.1 = (bf16[2,4,24,128]{3,2,1,0:T(8,128)(2,1)}, bf16[2,4,24,128]{3,2,1,0:T(8,128)(2,1)S(1)}, u32[]{:S(2)}, u32[]{:S(2)}) collective-permute-start(bf16[2,4,24,128]{3,2,1,0:T(8,128)(2,1)} %get-tuple-element.50), channel_id=1, source_target_pairs={{0,8},{4,12},{8,0},{12,4},{16,24},{20,28},{24,16},{28,20},{1,9},{5... | collective-permute-start | bytes 147464 | tf_op jit(solution)/shard_map/ppermute | solution.py:489
  28.0 1.4 %collective-permute-start.2 = (bf16[2,4,24,128]{3,2,1,0:T(8,128)(2,1)}, bf16[2,4,24,128]{3,2,1,0:T(8,128)(2,1)S(1)}, u32[]{:S(2)}, u32[]{:S(2)}) collective-permute-start(bf16[2,4,24,128]{3,2,1,0:T(8,128)(2,1)} %get-tuple-element.51), channel_id=1, source_target_pairs={{0,12},{4,8},{8,4},{12,0},{16,28},{20,24},{24,20},{28,16},{1,13},{... | collective-permute-start | bytes 147464 | tf_op jit(solution)/shard_map/ppermute | solution.py:489
  29.4 0.3 collective-permute-start.3
  29.7 0.1 fusion.8
  29.8 0.2 copy.10
  30.0 2.9 %sine_multiply_fusion = (f32[8,128,8]{2,1,0:T(8,128)}, f32[8,128,8]{2,1,0:T(8,128)}) fusion(f32[8,128,8]{2,1,0:T(8,128)S(1)} %copy.10, f32[8,128]{1,0:T(8,128)S(1)} %compare_select_fusion.3), kind=kLoop, calls=%fused_computation.8 | loop fusion | flops 24576 | bytes 102400 | tf_op jit(solution)/shard_map/mul | solution.py:304
  32.9 3.2 %fusion.6 = (f32[8,128,128]{2,1,0:T(8,128)}, f32[8,128,128]{2,1,0:T(8,128)}) fusion(s32[8,128]{1,0:T(8,128)S(1)} %gather_fusion.1), kind=kLoop, calls=%fused_computation.13 | loop fusion | flops 1835008 | bytes 1052672 | tf_op jit(solution)/shard_map/sin | solution.py:304
  36.2 0.0 collective-permute-done.22.refs_1_
  36.2 2.6 %collective-permute-start.4 = (bf16[2,4,24,128]{3,2,1,0:T(8,128)(2,1)}, bf16[2,4,24,128]{3,2,1,0:T(8,128)(2,1)S(1)}, u32[]{:S(2)}, u32[]{:S(2)}) collective-permute-start(bf16[2,4,24,128]{3,2,1,0:T(8,128)(2,1)} %get-tuple-element.53), channel_id=1, source_target_pairs={{0,20},{4,16},{8,28},{12,24},{16,4},{20,0},{24,12},{28,8},{1,21},{... | collective-permute-start | bytes 147464 | tf_op jit(solution)/shard_map/ppermute | solution.py:489
  38.8 0.0 collective-permute-done.refs_1_
  38.8 0.4 collective-permute-start.5
  39.2 0.0 collective-permute-done.1.refs_2_
  39.2 2.5 %collective-permute-start.6 = (bf16[2,4,24,128]{3,2,1,0:T(8,128)(2,1)}, bf16[2,4,24,128]{3,2,1,0:T(8,128)(2,1)S(1)}, u32[]{:S(2)}, u32[]{:S(2)}) collective-permute-start(bf16[2,4,24,128]{3,2,1,0:T(8,128)(2,1)} %get-tuple-element.55), channel_id=1, source_target_pairs={{0,28},{4,24},{8,20},{12,16},{16,12},{20,8},{24,4},{28,0},{1,29},{... | collective-permute-start | bytes 147464 | tf_op jit(solution)/shard_map/ppermute | solution.py:489
  41.7 0.6 fusion.10.refs_8_
  42.4 7.4 %twiddles.1.refs_9_ = bf16[8,2,128,1024]{3,2,1,0:T(8,128)(2,1)} custom-call(f32[8,128,128]{2,1,0:T(8,128)} %get-tuple-element.94.low_cos_ref, f32[8,128,128]{2,1,0:T(8,128)} %get-tuple-element.93.low_sin_ref, f32[8,128,8]{2,1,0:T(8,128)} %get-tuple-element.92.high_cos_ref, f32[8,128,8]{2,1,0:T(8,128)} %get-tuple-element.91.high_sin_ref), custom_call_target="tpu_custom_call" | custom-call | flops 8388608 | bytes 4194304 | tf_op jit(solution)/shard_map/twiddles/pallas_call | solution.py:296
  49.8 3.4 %collective-permute-start.23 = (bf16[2,4,24,128]{3,2,1,0:T(8,128)(2,1)S(1)}, bf16[2,4,24,128]{3,2,1,0:T(8,128)(2,1)S(1)}, u32[]{:S(2)}, u32[]{:S(2)}) collective-permute-start(bf16[2,4,24,128]{3,2,1,0:T(8,128)(2,1)S(1)} %copy-done.50), channel_id=1, source_target_pairs={{0,8},{4,12},{8,0},{12,4},{16,24},{20,28},{24,16},{28,20},{1,9},{5... | collective-permute-start | bytes 147464 | tf_op jit(solution)/shard_map/ppermute | solution.py:489
  53.2 0.1 collective-permute-start.24
  53.3 1.5 %collective-permute-start.12 = (bf16[2,4,24,128]{3,2,1,0:T(8,128)(2,1)S(1)}, bf16[2,4,24,128]{3,2,1,0:T(8,128)(2,1)S(1)}, u32[]{:S(2)}, u32[]{:S(2)}) collective-permute-start(bf16[2,4,24,128]{3,2,1,0:T(8,128)(2,1)S(1)} %copy-done.48), channel_id=1, source_target_pairs={{0,4},{4,0},{8,12},{12,8},{16,20},{20,16},{24,28},{28,24},{1,5},{5... | collective-permute-start | bytes 147464 | tf_op jit(solution)/shard_map/ppermute | solution.py:489
  54.9 2.0 %collective-permute-start.13 = (bf16[2,4,24,128]{3,2,1,0:T(8,128)(2,1)S(1)}, bf16[2,4,24,128]{3,2,1,0:T(8,128)(2,1)S(1)}, u32[]{:S(2)}, u32[]{:S(2)}) collective-permute-start(bf16[2,4,24,128]{3,2,1,0:T(8,128)(2,1)S(1)} %copy-done.47), channel_id=1, source_target_pairs={{0,8},{4,12},{8,0},{12,4},{16,24},{20,28},{24,16},{28,20},{1,9},{5... | collective-permute-start | bytes 147464 | tf_op jit(solution)/shard_map/ppermute | solution.py:489
  56.9 0.1 collective-permute-start.14
  57.1 0.5 copy-done.32
  57.6 4.9 %synthesis.3 = (bf16[96,640]{1,0:T(8,128)(2,1)}, bf16[96,640]{1,0:T(8,128)(2,1)}, bf16[96,640]{1,0:T(8,128)(2,1)}, bf16[96,640]{1,0:T(8,128)(2,1)}) custom-call(s32[1]{0:T(128)} %bitcast.4.place_ref, bf16[2,4,24,128]{3,2,1,0:T(8,128)(2,1)} %get-tuple-element.48.refs_0_, bf16[2,4,24,128]{3,2,1,0:T(8,128)(2,1)} %copy-done.17, ...), custom_call_target="tpu_custom_call" | custom-call | flops 805306368 | bytes 4194304 | tf_op jit(solution)/shard_map/synthesis/pallas_call | solution.py:364
  62.5 0.2 collective-permute-start.15
  62.7 3.3 %collective-permute-start.16 = (bf16[2,4,24,128]{3,2,1,0:T(8,128)(2,1)S(1)}, bf16[2,4,24,128]{3,2,1,0:T(8,128)(2,1)S(1)}, u32[]{:S(2)}, u32[]{:S(2)}) collective-permute-start(bf16[2,4,24,128]{3,2,1,0:T(8,128)(2,1)S(1)} %copy-done.44), channel_id=1, source_target_pairs={{0,20},{4,16},{8,28},{12,24},{16,4},{20,0},{24,12},{28,8},{1,21},{... | collective-permute-start | bytes 147464 | tf_op jit(solution)/shard_map/ppermute | solution.py:489
  66.0 0.6 collective-permute-start.17
  66.6 2.0 %collective-permute-start.18 = (bf16[2,4,24,128]{3,2,1,0:T(8,128)(2,1)S(1)}, bf16[2,4,24,128]{3,2,1,0:T(8,128)(2,1)S(1)}, u32[]{:S(2)}, u32[]{:S(2)}) collective-permute-start(bf16[2,4,24,128]{3,2,1,0:T(8,128)(2,1)S(1)} %copy-done.42), channel_id=1, source_target_pairs={{0,28},{4,24},{8,20},{12,16},{16,12},{20,8},{24,4},{28,0},{1,29},{... | collective-permute-start | bytes 147464 | tf_op jit(solution)/shard_map/ppermute | solution.py:489
  68.6 2.1 %collective-permute-start.25 = (bf16[2,4,24,128]{3,2,1,0:T(8,128)(2,1)S(1)}, bf16[2,4,24,128]{3,2,1,0:T(8,128)(2,1)S(1)}, u32[]{:S(2)}, u32[]{:S(2)}) collective-permute-start(bf16[2,4,24,128]{3,2,1,0:T(8,128)(2,1)S(1)} %copy-done.41), channel_id=1, source_target_pairs={{0,16},{4,20},{8,24},{12,28},{16,0},{20,4},{24,8},{28,12},{1,17},{... | collective-permute-start | bytes 147464 | tf_op jit(solution)/shard_map/ppermute | solution.py:489
  70.7 1.5 %collective-permute-start.26 = (bf16[2,4,24,128]{3,2,1,0:T(8,128)(2,1)S(1)}, bf16[2,4,24,128]{3,2,1,0:T(8,128)(2,1)S(1)}, u32[]{:S(2)}, u32[]{:S(2)}) collective-permute-start(bf16[2,4,24,128]{3,2,1,0:T(8,128)(2,1)S(1)} %copy-done.40), channel_id=1, source_target_pairs={{0,20},{4,16},{8,28},{12,24},{16,4},{20,0},{24,12},{28,8},{1,21},{... | collective-permute-start | bytes 147464 | tf_op jit(solution)/shard_map/ppermute | solution.py:489
  72.2 2.4 %collective-permute-start.27 = (bf16[2,4,24,128]{3,2,1,0:T(8,128)(2,1)S(1)}, bf16[2,4,24,128]{3,2,1,0:T(8,128)(2,1)S(1)}, u32[]{:S(2)}, u32[]{:S(2)}) collective-permute-start(bf16[2,4,24,128]{3,2,1,0:T(8,128)(2,1)S(1)} %copy-done.39), channel_id=1, source_target_pairs={{0,24},{4,28},{8,16},{12,20},{16,8},{20,12},{24,0},{28,4},{1,25},{... | collective-permute-start | bytes 147464 | tf_op jit(solution)/shard_map/ppermute | solution.py:489
  74.6 1.5 %collective-permute-start.28 = (bf16[2,4,24,128]{3,2,1,0:T(8,128)(2,1)S(1)}, bf16[2,4,24,128]{3,2,1,0:T(8,128)(2,1)S(1)}, u32[]{:S(2)}, u32[]{:S(2)}) collective-permute-start(bf16[2,4,24,128]{3,2,1,0:T(8,128)(2,1)S(1)} %copy-done.38), channel_id=1, source_target_pairs={{0,28},{4,24},{8,20},{12,16},{16,12},{20,8},{24,4},{28,0},{1,29},{... | collective-permute-start | bytes 147464 | tf_op jit(solution)/shard_map/ppermute | solution.py:489
  76.1 4.9 %synthesis.4 = (bf16[96,640]{1,0:T(8,128)(2,1)}, bf16[96,640]{1,0:T(8,128)(2,1)}, bf16[96,640]{1,0:T(8,128)(2,1)}, bf16[96,640]{1,0:T(8,128)(2,1)}) custom-call(s32[1]{0:T(128)} %bitcast.4.place_ref, bf16[2,4,24,128]{3,2,1,0:T(8,128)(2,1)} %get-tuple-element.63.refs_0_, bf16[2,4,24,128]{3,2,1,0:T(8,128)(2,1)} %copy-done.18, ...), custom_call_target="tpu_custom_call" | custom-call | flops 805306368 | bytes 4194304 | tf_op jit(solution)/shard_map/synthesis/pallas_call | solution.py:364
  81.0 0.1 collective-permute-start.19
  81.1 1.6 %collective-permute-start.20 = (bf16[96,640]{1,0:T(8,128)(2,1)}, bf16[96,640]{1,0:T(8,128)(2,1)S(1)}, u32[]{:S(2)}, u32[]{:S(2)}) collective-permute-start(bf16[96,640]{1,0:T(8,128)(2,1)} %get-tuple-element.73), channel_id=1, source_target_pairs={{0,2},{1,3},{2,0},{3,1},{4,6},{5,7},{6,4},{7,5},{8,10},{9,11},{10,... | collective-permute-start | bytes 368648 | tf_op jit(solution)/shard_map/ppermute | solution.py:489
  82.7 0.2 collective-permute-start.21
  83.0 1.6 %collective-permute-start.8 = (bf16[96,640]{1,0:T(8,128)(2,1)S(1)}, bf16[96,640]{1,0:T(8,128)(2,1)S(1)}, u32[]{:S(2)}, u32[]{:S(2)}) collective-permute-start(bf16[96,640]{1,0:T(8,128)(2,1)S(1)} %copy-done.37), channel_id=1, source_target_pairs={{0,2},{1,3},{2,0},{3,1},{4,6},{5,7},{6,4},{7,5},{8,10},{9,11},{10,... | collective-permute-start | bytes 368648 | tf_op jit(solution)/shard_map/ppermute | solution.py:489
  84.6 0.3 collective-permute-start.9
  84.8 0.1 copy.9
  84.9 0.6 gather_fusion
  85.5 0.7 copy.13.vertical_ref
  86.2 4.9 %synthesis.5 = (bf16[96,640]{1,0:T(8,128)(2,1)}, bf16[96,640]{1,0:T(8,128)(2,1)}, bf16[96,640]{1,0:T(8,128)(2,1)}, bf16[96,640]{1,0:T(8,128)(2,1)}) custom-call(s32[1]{0:T(128)} %bitcast.4.place_ref, bf16[2,4,24,128]{3,2,1,0:T(8,128)(2,1)} %get-tuple-element.75.refs_0_, bf16[2,4,24,128]{3,2,1,0:T(8,128)(2,1)} %copy-done.14, ...), custom_call_target="tpu_custom_call" | custom-call | flops 805306368 | bytes 4194304 | tf_op jit(solution)/shard_map/synthesis/pallas_call | solution.py:364
  91.2 1.7 %collective-permute-done.8.refs_2_ = bf16[96,640]{1,0:T(8,128)(2,1)S(1)} collective-permute-done((bf16[96,640]{1,0:T(8,128)(2,1)S(1)}, bf16[96,640]{1,0:T(8,128)(2,1)S(1)}, u32[]{:S(2)}, u32[]{:S(2)}) %collective-permute-start.8) | collective-permute-done | bytes 122912 | tf_op jit(solution)/shard_map/ppermute | solution.py:489
  92.9 1.5 %collective-permute-done.9.refs_3_ = bf16[96,640]{1,0:T(8,128)(2,1)S(1)} collective-permute-done((bf16[96,640]{1,0:T(8,128)(2,1)S(1)}, bf16[96,640]{1,0:T(8,128)(2,1)S(1)}, u32[]{:S(2)}, u32[]{:S(2)}) %collective-permute-start.9) | collective-permute-done | bytes 122912 | tf_op jit(solution)/shard_map/ppermute | solution.py:489
  94.4 1.5 %collective-permute-start.30 = (bf16[96,640]{1,0:T(8,128)(2,1)}, bf16[96,640]{1,0:T(8,128)(2,1)S(1)}, u32[]{:S(2)}, u32[]{:S(2)}) collective-permute-start(bf16[96,640]{1,0:T(8,128)(2,1)} %get-tuple-element.85), channel_id=1, source_target_pairs={{0,2},{1,3},{2,0},{3,1},{4,6},{5,7},{6,4},{7,5},{8,10},{9,11},{10,... | collective-permute-start | bytes 368648 | tf_op jit(solution)/shard_map/ppermute | solution.py:489
  95.9 2.6 %tracer.1 = (f32[4,96,640]{2,1,0:T(8,128)}, bf16[96,640]{1,0:T(8,128)(2,1)}, bf16[96,640]{1,0:T(8,128)(2,1)}) custom-call(f32[96,96]{1,0:T(8,128)} %copy.13.vertical_ref, bf16[96,640]{1,0:T(8,128)(2,1)} %get-tuple-element.56.refs_0_, bf16[96,640]{1,0:T(8,128)(2,1)} %copy-done.1, bf16[96,640]{1,0:T(8,128)(2,1)} %copy-done.5, bf16[96,640]{1,0:T(8,128)(2,1)} %copy-done.6), custom_call_target="tpu_custom_call" | custom-call | flops 4000000 | bytes 4000000 | tf_op jit(solution)/shard_map/tracer/pallas_call | solution.py:476
  98.5 0.7 collective-permute-start.31
  99.2 2.0 %collective-permute-start.10 = (bf16[96,640]{1,0:T(8,128)(2,1)}, bf16[96,640]{1,0:T(8,128)(2,1)S(1)}, u32[]{:S(2)}, u32[]{:S(2)}) collective-permute-start(bf16[96,640]{1,0:T(8,128)(2,1)} %get-tuple-element.61), channel_id=1, source_target_pairs={{0,4},{4,8},{8,12},{12,16},{16,20},{20,24},{24,28},{1,5},{5,9},{9,... | collective-permute-start | bytes 368648 | tf_op jit(solution)/shard_map/ppermute | solution.py:495
  101.2 4.7 %collective-permute-start.11 = (bf16[96,640]{1,0:T(8,128)(2,1)}, bf16[96,640]{1,0:T(8,128)(2,1)S(1)}, u32[]{:S(2)}, u32[]{:S(2)}) collective-permute-start(bf16[96,640]{1,0:T(8,128)(2,1)} %get-tuple-element.62), channel_id=1, source_target_pairs={{4,0},{8,4},{12,8},{16,12},{20,16},{24,20},{28,24},{5,1},{9,5},{13... | collective-permute-start | bytes 368648 | tf_op jit(solution)/shard_map/ppermute | solution.py:496
  106.0 2.6 %courant_x.1.x_ref = f32[4,96,640]{2,1,0:T(8,128)} custom-call(f32[96,96]{1,0:T(8,128)} %copy.13.vertical_ref, bf16[96,640]{1,0:T(8,128)(2,1)} %get-tuple-element.71.refs_0_, bf16[96,640]{1,0:T(8,128)(2,1)} %copy-done.2, bf16[96,640]{1,0:T(8,128)(2,1)} %copy-done.3, bf16[96,640]{1,0:T(8,128)(2,1)} %copy-done.4), custom_call_target="tpu_custom_call" | custom-call | flops 4000000 | bytes 4000000 | tf_op jit(solution)/shard_map/courant_x/pallas_call | solution.py:476
  108.7 0.0 copy-start.12
  108.7 3.2 %collective-permute-done.11.below_ref = bf16[96,640]{1,0:T(8,128)(2,1)S(1)} collective-permute-done((bf16[96,640]{1,0:T(8,128)(2,1)}, bf16[96,640]{1,0:T(8,128)(2,1)S(1)}, u32[]{:S(2)}, u32[]{:S(2)}) %collective-permute-start.11) | collective-permute-done | bytes 122912 | tf_op jit(solution)/shard_map/ppermute | solution.py:496
  111.9 0.6 copy-done.13
  112.5 4.1 %first_step.1 = (f32[4,96,640]{2,1,0:T(8,128)}, f32[4,96,640]{2,1,0:T(8,128)}, bf16[96,640]{1,0:T(8,128)(2,1)}, bf16[96,640]{1,0:T(8,128)(2,1)}) custom-call(f32[96,96]{1,0:T(8,128)} %copy.13.vertical_ref, f32[4,96,640]{2,1,0:T(8,128)} %get-tuple-element.60.tracer_ref, bf16[96,640]{1,0:T(8,128)(2,1)} %copy-done.12, bf16[96,640]{1,0:T(8,128)(2,1)} %copy-done.13, ...), custom_call_target="tpu_custom_call" | custom-call | flops 4000000 | bytes 4000000 | tf_op jit(solution)/shard_map/first_step/pallas_call | solution.py:476
  116.6 4.5 %collective-permute-start.32 = (bf16[96,640]{1,0:T(8,128)(2,1)}, bf16[96,640]{1,0:T(8,128)(2,1)S(1)}, u32[]{:S(2)}, u32[]{:S(2)}) collective-permute-start(bf16[96,640]{1,0:T(8,128)(2,1)} %get-tuple-element.88), channel_id=1, source_target_pairs={{0,4},{4,8},{8,12},{12,16},{16,20},{20,24},{24,28},{1,5},{5,9},{9,... | collective-permute-start | bytes 368648 | tf_op jit(solution)/shard_map/ppermute | solution.py:495
  121.1 2.2 %collective-permute-start.33 = (bf16[96,640]{1,0:T(8,128)(2,1)}, bf16[96,640]{1,0:T(8,128)(2,1)S(1)}, u32[]{:S(2)}, u32[]{:S(2)}) collective-permute-start(bf16[96,640]{1,0:T(8,128)(2,1)} %get-tuple-element.89), channel_id=1, source_target_pairs={{4,0},{8,4},{12,8},{16,12},{20,16},{24,20},{28,24},{5,1},{9,5},{13... | collective-permute-start | bytes 368648 | tf_op jit(solution)/shard_map/ppermute | solution.py:496
  123.3 1.1 collective-permute-done.32.above_ref
  124.5 3.6 %collective-permute-done.33.below_ref = bf16[96,640]{1,0:T(8,128)(2,1)S(1)} collective-permute-done((bf16[96,640]{1,0:T(8,128)(2,1)}, bf16[96,640]{1,0:T(8,128)(2,1)S(1)}, u32[]{:S(2)}, u32[]{:S(2)}) %collective-permute-start.33) | collective-permute-done | bytes 122912 | tf_op jit(solution)/shard_map/ppermute | solution.py:496
  128.1 0.6 copy-done.8
  128.8 3.6 %second_step.1 = f32[96,4,512]{2,1,0:T(4,128)} custom-call(f32[4,96,640]{2,1,0:T(8,128)} %get-tuple-element.87.tracer_ref, bf16[96,640]{1,0:T(8,128)(2,1)} %copy-done.7, bf16[96,640]{1,0:T(8,128)(2,1)} %copy-done.8, f32[4,96,640]{2,1,0:T(8,128)} %courant_x.1.x_ref, f32[4,96,640]{2,1,0:T(8,128)} %get-tuple-element.90.y_ref), custom_call_target="tpu_custom_call" | custom-call | flops 4000000 | bytes 4000000 | tf_op jit(solution)/shard_map/second_step/pallas_call | solution.py:476
  (131 shorter events, 0.3 us)
Async XLA Ops:
  24.3 11.9 %collective-permute-start.22 = (bf16[2,4,24,128]{3,2,1,0:T(8,128)(2,1)}, bf16[2,4,24,128]{3,2,1,0:T(8,128)(2,1)S(1)}, u32[]{:S(2)}, u32[]{:S(2)}) collective-permute-start(bf16[2,4,24,128]{3,2,1,0:T(8,128)(2,1)} %get-tuple-element.76), channel_id=1, source_target_pairs={{0,4},{4,0},{8,12},{12,8},{16,20},{20,16},{24,28},{28,24},{1,5},{5... | collective-permute-start | bytes 147464 | tf_op jit(solution)/shard_map/ppermute | solution.py:489
  25.9 12.9 %collective-permute-start = (bf16[2,4,24,128]{3,2,1,0:T(8,128)(2,1)}, bf16[2,4,24,128]{3,2,1,0:T(8,128)(2,1)S(1)}, u32[]{:S(2)}, u32[]{:S(2)}) collective-permute-start(bf16[2,4,24,128]{3,2,1,0:T(8,128)(2,1)} %get-tuple-element.49), channel_id=1, source_target_pairs={{0,4},{4,0},{8,12},{12,8},{16,20},{20,16},{24,28},{28,24},{1,5},{5... | collective-permute-start | bytes 147464 | tf_op jit(solution)/shard_map/ppermute | solution.py:489
  26.4 12.8 %collective-permute-start.1 = (bf16[2,4,24,128]{3,2,1,0:T(8,128)(2,1)}, bf16[2,4,24,128]{3,2,1,0:T(8,128)(2,1)S(1)}, u32[]{:S(2)}, u32[]{:S(2)}) collective-permute-start(bf16[2,4,24,128]{3,2,1,0:T(8,128)(2,1)} %get-tuple-element.50), channel_id=1, source_target_pairs={{0,8},{4,12},{8,0},{12,4},{16,24},{20,28},{24,16},{28,20},{1,9},{5... | collective-permute-start | bytes 147464 | tf_op jit(solution)/shard_map/ppermute | solution.py:489
  28.0 21.8 %collective-permute-start.2 = (bf16[2,4,24,128]{3,2,1,0:T(8,128)(2,1)}, bf16[2,4,24,128]{3,2,1,0:T(8,128)(2,1)S(1)}, u32[]{:S(2)}, u32[]{:S(2)}) collective-permute-start(bf16[2,4,24,128]{3,2,1,0:T(8,128)(2,1)} %get-tuple-element.51), channel_id=1, source_target_pairs={{0,12},{4,8},{8,4},{12,0},{16,28},{20,24},{24,20},{28,16},{1,13},{... | collective-permute-start | bytes 147464 | tf_op jit(solution)/shard_map/ppermute | solution.py:489
  29.4 23.9 %collective-permute-start.3 = (bf16[2,4,24,128]{3,2,1,0:T(8,128)(2,1)}, bf16[2,4,24,128]{3,2,1,0:T(8,128)(2,1)S(1)}, u32[]{:S(2)}, u32[]{:S(2)}) collective-permute-start(bf16[2,4,24,128]{3,2,1,0:T(8,128)(2,1)} %get-tuple-element.52), channel_id=1, source_target_pairs={{0,16},{4,20},{8,24},{12,28},{16,0},{20,4},{24,8},{28,12},{1,17},{... | collective-permute-start | bytes 147464 | tf_op jit(solution)/shard_map/ppermute | solution.py:489
  30.0 19.8 %copy-start.50 = (bf16[2,4,24,128]{3,2,1,0:T(8,128)(2,1)S(1)}, bf16[2,4,24,128]{3,2,1,0:T(8,128)(2,1)}, u32[]{:S(2)}) copy-start(bf16[2,4,24,128]{3,2,1,0:T(8,128)(2,1)} %get-tuple-element.77) | copy-start | bytes 147460
  30.0 23.2 %copy-start.49 = (bf16[2,4,24,128]{3,2,1,0:T(8,128)(2,1)S(1)}, bf16[2,4,24,128]{3,2,1,0:T(8,128)(2,1)}, u32[]{:S(2)}) copy-start(bf16[2,4,24,128]{3,2,1,0:T(8,128)(2,1)} %get-tuple-element.78) | copy-start | bytes 147460
  30.0 23.3 %copy-start.48 = (bf16[2,4,24,128]{3,2,1,0:T(8,128)(2,1)S(1)}, bf16[2,4,24,128]{3,2,1,0:T(8,128)(2,1)}, u32[]{:S(2)}) copy-start(bf16[2,4,24,128]{3,2,1,0:T(8,128)(2,1)} %get-tuple-element.64) | copy-start | bytes 147460
  30.0 24.9 %copy-start.47 = (bf16[2,4,24,128]{3,2,1,0:T(8,128)(2,1)S(1)}, bf16[2,4,24,128]{3,2,1,0:T(8,128)(2,1)}, u32[]{:S(2)}) copy-start(bf16[2,4,24,128]{3,2,1,0:T(8,128)(2,1)} %get-tuple-element.65) | copy-start | bytes 147460
  30.0 26.9 %copy-start.46 = (bf16[2,4,24,128]{3,2,1,0:T(8,128)(2,1)S(1)}, bf16[2,4,24,128]{3,2,1,0:T(8,128)(2,1)}, u32[]{:S(2)}) copy-start(bf16[2,4,24,128]{3,2,1,0:T(8,128)(2,1)} %get-tuple-element.66) | copy-start | bytes 147460
  36.2 26.2 %copy-start.14 = (bf16[2,4,24,128]{3,2,1,0:T(8,128)(2,1)}, bf16[2,4,24,128]{3,2,1,0:T(8,128)(2,1)S(1)}, u32[]{:S(2)}) copy-start(bf16[2,4,24,128]{3,2,1,0:T(8,128)(2,1)S(1)} %collective-permute-done.22.refs_1_) | copy-start | bytes 147460
  36.2 17.1 %collective-permute-start.4 = (bf16[2,4,24,128]{3,2,1,0:T(8,128)(2,1)}, bf16[2,4,24,128]{3,2,1,0:T(8,128)(2,1)S(1)}, u32[]{:S(2)}, u32[]{:S(2)}) collective-permute-start(bf16[2,4,24,128]{3,2,1,0:T(8,128)(2,1)} %get-tuple-element.53), channel_id=1, source_target_pairs={{0,20},{4,16},{8,28},{12,24},{16,4},{20,0},{24,12},{28,8},{1,21},{... | collective-permute-start | bytes 147464 | tf_op jit(solution)/shard_map/ppermute | solution.py:489
  38.8 18.3 %copy-start.17 = (bf16[2,4,24,128]{3,2,1,0:T(8,128)(2,1)}, bf16[2,4,24,128]{3,2,1,0:T(8,128)(2,1)S(1)}, u32[]{:S(2)}) copy-start(bf16[2,4,24,128]{3,2,1,0:T(8,128)(2,1)S(1)} %collective-permute-done.refs_1_) | copy-start | bytes 147460
  38.8 16.1 %collective-permute-start.5 = (bf16[2,4,24,128]{3,2,1,0:T(8,128)(2,1)}, bf16[2,4,24,128]{3,2,1,0:T(8,128)(2,1)S(1)}, u32[]{:S(2)}, u32[]{:S(2)}) collective-permute-start(bf16[2,4,24,128]{3,2,1,0:T(8,128)(2,1)} %get-tuple-element.54), channel_id=1, source_target_pairs={{0,24},{4,28},{8,16},{12,20},{16,8},{20,12},{24,0},{28,4},{1,25},{... | collective-permute-start | bytes 147464 | tf_op jit(solution)/shard_map/ppermute | solution.py:489
  39.2 17.8 %copy-start.19 = (bf16[2,4,24,128]{3,2,1,0:T(8,128)(2,1)}, bf16[2,4,24,128]{3,2,1,0:T(8,128)(2,1)S(1)}, u32[]{:S(2)}) copy-start(bf16[2,4,24,128]{3,2,1,0:T(8,128)(2,1)S(1)} %collective-permute-done.1.refs_2_) | copy-start | bytes 147460
  39.2 17.7 %collective-permute-start.6 = (bf16[2,4,24,128]{3,2,1,0:T(8,128)(2,1)}, bf16[2,4,24,128]{3,2,1,0:T(8,128)(2,1)S(1)}, u32[]{:S(2)}, u32[]{:S(2)}) collective-permute-start(bf16[2,4,24,128]{3,2,1,0:T(8,128)(2,1)} %get-tuple-element.55), channel_id=1, source_target_pairs={{0,28},{4,24},{8,20},{12,16},{16,12},{20,8},{24,4},{28,0},{1,29},{... | collective-permute-start | bytes 147464 | tf_op jit(solution)/shard_map/ppermute | solution.py:489
  42.3 20.1 %copy-start.45 = (bf16[2,4,24,128]{3,2,1,0:T(8,128)(2,1)S(1)}, bf16[2,4,24,128]{3,2,1,0:T(8,128)(2,1)}, u32[]{:S(2)}) copy-start(bf16[2,4,24,128]{3,2,1,0:T(8,128)(2,1)} %get-tuple-element.67) | copy-start | bytes 147460
  42.3 20.3 %copy-start.44 = (bf16[2,4,24,128]{3,2,1,0:T(8,128)(2,1)S(1)}, bf16[2,4,24,128]{3,2,1,0:T(8,128)(2,1)}, u32[]{:S(2)}) copy-start(bf16[2,4,24,128]{3,2,1,0:T(8,128)(2,1)} %get-tuple-element.68) | copy-start | bytes 147460
  42.4 23.6 %copy-start.43 = (bf16[2,4,24,128]{3,2,1,0:T(8,128)(2,1)S(1)}, bf16[2,4,24,128]{3,2,1,0:T(8,128)(2,1)}, u32[]{:S(2)}) copy-start(bf16[2,4,24,128]{3,2,1,0:T(8,128)(2,1)} %get-tuple-element.69) | copy-start | bytes 147460
  42.4 24.3 %copy-start.42 = (bf16[2,4,24,128]{3,2,1,0:T(8,128)(2,1)S(1)}, bf16[2,4,24,128]{3,2,1,0:T(8,128)(2,1)}, u32[]{:S(2)}) copy-start(bf16[2,4,24,128]{3,2,1,0:T(8,128)(2,1)} %get-tuple-element.70) | copy-start | bytes 147460
  42.4 26.3 %copy-start.41 = (bf16[2,4,24,128]{3,2,1,0:T(8,128)(2,1)S(1)}, bf16[2,4,24,128]{3,2,1,0:T(8,128)(2,1)}, u32[]{:S(2)}) copy-start(bf16[2,4,24,128]{3,2,1,0:T(8,128)(2,1)} %get-tuple-element.79) | copy-start | bytes 147460
  42.4 28.3 %copy-start.40 = (bf16[2,4,24,128]{3,2,1,0:T(8,128)(2,1)S(1)}, bf16[2,4,24,128]{3,2,1,0:T(8,128)(2,1)}, u32[]{:S(2)}) copy-start(bf16[2,4,24,128]{3,2,1,0:T(8,128)(2,1)} %get-tuple-element.80) | copy-start | bytes 147460
  42.4 29.8 %copy-start.39 = (bf16[2,4,24,128]{3,2,1,0:T(8,128)(2,1)S(1)}, bf16[2,4,24,128]{3,2,1,0:T(8,128)(2,1)}, u32[]{:S(2)}) copy-start(bf16[2,4,24,128]{3,2,1,0:T(8,128)(2,1)} %get-tuple-element.81) | copy-start | bytes 147460
  42.4 32.2 %copy-start.38 = (bf16[2,4,24,128]{3,2,1,0:T(8,128)(2,1)S(1)}, bf16[2,4,24,128]{3,2,1,0:T(8,128)(2,1)}, u32[]{:S(2)}) copy-start(bf16[2,4,24,128]{3,2,1,0:T(8,128)(2,1)} %get-tuple-element.82) | copy-start | bytes 147460
  49.8 7.3 %copy-start.20 = (bf16[2,4,24,128]{3,2,1,0:T(8,128)(2,1)}, bf16[2,4,24,128]{3,2,1,0:T(8,128)(2,1)S(1)}, u32[]{:S(2)}) copy-start(bf16[2,4,24,128]{3,2,1,0:T(8,128)(2,1)S(1)} %collective-permute-done.2.refs_3_) | copy-start | bytes 147460
  49.8 12.6 %collective-permute-start.23 = (bf16[2,4,24,128]{3,2,1,0:T(8,128)(2,1)S(1)}, bf16[2,4,24,128]{3,2,1,0:T(8,128)(2,1)S(1)}, u32[]{:S(2)}, u32[]{:S(2)}) collective-permute-start(bf16[2,4,24,128]{3,2,1,0:T(8,128)(2,1)S(1)} %copy-done.50), channel_id=1, source_target_pairs={{0,8},{4,12},{8,0},{12,4},{16,24},{20,28},{24,16},{28,20},{1,9},{5... | collective-permute-start | bytes 147464 | tf_op jit(solution)/shard_map/ppermute | solution.py:489
  53.2 9.4 %collective-permute-start.24 = (bf16[2,4,24,128]{3,2,1,0:T(8,128)(2,1)S(1)}, bf16[2,4,24,128]{3,2,1,0:T(8,128)(2,1)S(1)}, u32[]{:S(2)}, u32[]{:S(2)}) collective-permute-start(bf16[2,4,24,128]{3,2,1,0:T(8,128)(2,1)S(1)} %copy-done.49), channel_id=1, source_target_pairs={{0,12},{4,8},{8,4},{12,0},{16,28},{20,24},{24,20},{28,16},{1,13},{... | collective-permute-start | bytes 147464 | tf_op jit(solution)/shard_map/ppermute | solution.py:489
  53.3 12.6 %collective-permute-start.12 = (bf16[2,4,24,128]{3,2,1,0:T(8,128)(2,1)S(1)}, bf16[2,4,24,128]{3,2,1,0:T(8,128)(2,1)S(1)}, u32[]{:S(2)}, u32[]{:S(2)}) collective-permute-start(bf16[2,4,24,128]{3,2,1,0:T(8,128)(2,1)S(1)} %copy-done.48), channel_id=1, source_target_pairs={{0,4},{4,0},{8,12},{12,8},{16,20},{20,16},{24,28},{28,24},{1,5},{5... | collective-permute-start | bytes 147464 | tf_op jit(solution)/shard_map/ppermute | solution.py:489
  54.9 11.7 %collective-permute-start.13 = (bf16[2,4,24,128]{3,2,1,0:T(8,128)(2,1)S(1)}, bf16[2,4,24,128]{3,2,1,0:T(8,128)(2,1)S(1)}, u32[]{:S(2)}, u32[]{:S(2)}) collective-permute-start(bf16[2,4,24,128]{3,2,1,0:T(8,128)(2,1)S(1)} %copy-done.47), channel_id=1, source_target_pairs={{0,8},{4,12},{8,0},{12,4},{16,24},{20,28},{24,16},{28,20},{1,9},{5... | collective-permute-start | bytes 147464 | tf_op jit(solution)/shard_map/ppermute | solution.py:489
  56.9 11.6 %collective-permute-start.14 = (bf16[2,4,24,128]{3,2,1,0:T(8,128)(2,1)S(1)}, bf16[2,4,24,128]{3,2,1,0:T(8,128)(2,1)S(1)}, u32[]{:S(2)}, u32[]{:S(2)}) collective-permute-start(bf16[2,4,24,128]{3,2,1,0:T(8,128)(2,1)S(1)} %copy-done.46), channel_id=1, source_target_pairs={{0,12},{4,8},{8,4},{12,0},{16,28},{20,24},{24,20},{28,16},{1,13},{... | collective-permute-start | bytes 147464 | tf_op jit(solution)/shard_map/ppermute | solution.py:489
  57.6 27.3 %copy-start.35 = (f32[96,96]{1,0:T(8,128)S(1)}, f32[96,96]{1,0:T(8,128)}, u32[]{:S(2)}) copy-start(f32[96,96]{1,0:T(8,128)} %param.7) | copy-start | bytes 110596
  62.4 20.6 %copy-start.37 = (bf16[96,640]{1,0:T(8,128)(2,1)S(1)}, bf16[96,640]{1,0:T(8,128)(2,1)}, u32[]{:S(2)}) copy-start(bf16[96,640]{1,0:T(8,128)(2,1)} %get-tuple-element.58) | copy-start | bytes 368644
  62.4 22.1 %copy-start.36 = (bf16[96,640]{1,0:T(8,128)(2,1)S(1)}, bf16[96,640]{1,0:T(8,128)(2,1)}, u32[]{:S(2)}) copy-start(bf16[96,640]{1,0:T(8,128)(2,1)} %get-tuple-element.59) | copy-start | bytes 368644
  62.4 23.8 %copy-start.15 = (bf16[2,4,24,128]{3,2,1,0:T(8,128)(2,1)}, bf16[2,4,24,128]{3,2,1,0:T(8,128)(2,1)S(1)}, u32[]{:S(2)}) copy-start(bf16[2,4,24,128]{3,2,1,0:T(8,128)(2,1)S(1)} %collective-permute-done.23.refs_2_) | copy-start | bytes 147460
  62.5 6.1 %collective-permute-start.15 = (bf16[2,4,24,128]{3,2,1,0:T(8,128)(2,1)S(1)}, bf16[2,4,24,128]{3,2,1,0:T(8,128)(2,1)S(1)}, u32[]{:S(2)}, u32[]{:S(2)}) collective-permute-start(bf16[2,4,24,128]{3,2,1,0:T(8,128)(2,1)S(1)} %copy-done.45), channel_id=1, source_target_pairs={{0,16},{4,20},{8,24},{12,28},{16,0},{20,4},{24,8},{28,12},{1,17},{... | collective-permute-start | bytes 147464 | tf_op jit(solution)/shard_map/ppermute | solution.py:489
  62.7 23.5 %copy-start.16 = (bf16[2,4,24,128]{3,2,1,0:T(8,128)(2,1)}, bf16[2,4,24,128]{3,2,1,0:T(8,128)(2,1)S(1)}, u32[]{:S(2)}) copy-start(bf16[2,4,24,128]{3,2,1,0:T(8,128)(2,1)S(1)} %collective-permute-done.24.refs_3_) | copy-start | bytes 147460
  62.7 8.0 %collective-permute-start.16 = (bf16[2,4,24,128]{3,2,1,0:T(8,128)(2,1)S(1)}, bf16[2,4,24,128]{3,2,1,0:T(8,128)(2,1)S(1)}, u32[]{:S(2)}, u32[]{:S(2)}) collective-permute-start(bf16[2,4,24,128]{3,2,1,0:T(8,128)(2,1)S(1)} %copy-done.44), channel_id=1, source_target_pairs={{0,20},{4,16},{8,28},{12,24},{16,4},{20,0},{24,12},{28,8},{1,21},{... | collective-permute-start | bytes 147464 | tf_op jit(solution)/shard_map/ppermute | solution.py:489
  66.0 10.1 %copy-start.18 = (bf16[2,4,24,128]{3,2,1,0:T(8,128)(2,1)}, bf16[2,4,24,128]{3,2,1,0:T(8,128)(2,1)S(1)}, u32[]{:S(2)}) copy-start(bf16[2,4,24,128]{3,2,1,0:T(8,128)(2,1)S(1)} %collective-permute-done.12.refs_1_) | copy-start | bytes 147460
  66.0 6.2 %collective-permute-start.17 = (bf16[2,4,24,128]{3,2,1,0:T(8,128)(2,1)S(1)}, bf16[2,4,24,128]{3,2,1,0:T(8,128)(2,1)S(1)}, u32[]{:S(2)}, u32[]{:S(2)}) collective-permute-start(bf16[2,4,24,128]{3,2,1,0:T(8,128)(2,1)S(1)} %copy-done.43), channel_id=1, source_target_pairs={{0,24},{4,28},{8,16},{12,20},{16,8},{20,12},{24,0},{28,4},{1,25},{... | collective-permute-start | bytes 147464 | tf_op jit(solution)/shard_map/ppermute | solution.py:489
  66.6 9.4 %copy-start.22 = (bf16[2,4,24,128]{3,2,1,0:T(8,128)(2,1)}, bf16[2,4,24,128]{3,2,1,0:T(8,128)(2,1)S(1)}, u32[]{:S(2)}) copy-start(bf16[2,4,24,128]{3,2,1,0:T(8,128)(2,1)S(1)} %collective-permute-done.13.refs_2_) | copy-start | bytes 147460
  66.6 8.0 %collective-permute-start.18 = (bf16[2,4,24,128]{3,2,1,0:T(8,128)(2,1)S(1)}, bf16[2,4,24,128]{3,2,1,0:T(8,128)(2,1)S(1)}, u32[]{:S(2)}, u32[]{:S(2)}) collective-permute-start(bf16[2,4,24,128]{3,2,1,0:T(8,128)(2,1)S(1)} %copy-done.42), channel_id=1, source_target_pairs={{0,28},{4,24},{8,20},{12,16},{16,12},{20,8},{24,4},{28,0},{1,29},{... | collective-permute-start | bytes 147464 | tf_op jit(solution)/shard_map/ppermute | solution.py:489
  68.6 7.5 %copy-start.24 = (bf16[2,4,24,128]{3,2,1,0:T(8,128)(2,1)}, bf16[2,4,24,128]{3,2,1,0:T(8,128)(2,1)S(1)}, u32[]{:S(2)}) copy-start(bf16[2,4,24,128]{3,2,1,0:T(8,128)(2,1)S(1)} %collective-permute-done.14.refs_3_) | copy-start | bytes 147460
  68.6 16.0 %collective-permute-start.7 = (bf16[96,640]{1,0:T(8,128)(2,1)}, bf16[96,640]{1,0:T(8,128)(2,1)S(1)}, u32[]{:S(2)}, u32[]{:S(2)}) collective-permute-start(bf16[96,640]{1,0:T(8,128)(2,1)} %get-tuple-element.57), channel_id=1, source_target_pairs={{0,1},{1,0},{2,3},{3,2},{4,5},{5,4},{6,7},{7,6},{8,9},{9,8},{10,11... | collective-permute-start | bytes 368648 | tf_op jit(solution)/shard_map/ppermute | solution.py:489
  68.6 7.4 %copy-start.29 = (bf16[2,4,24,128]{3,2,1,0:T(8,128)(2,1)}, bf16[2,4,24,128]{3,2,1,0:T(8,128)(2,1)S(1)}, u32[]{:S(2)}) copy-start(bf16[2,4,24,128]{3,2,1,0:T(8,128)(2,1)S(1)} %collective-permute-done.15.refs_4_) | copy-start | bytes 147460
  68.6 12.4 %collective-permute-start.25 = (bf16[2,4,24,128]{3,2,1,0:T(8,128)(2,1)S(1)}, bf16[2,4,24,128]{3,2,1,0:T(8,128)(2,1)S(1)}, u32[]{:S(2)}, u32[]{:S(2)}) collective-permute-start(bf16[2,4,24,128]{3,2,1,0:T(8,128)(2,1)S(1)} %copy-done.41), channel_id=1, source_target_pairs={{0,16},{4,20},{8,24},{12,28},{16,0},{20,4},{24,8},{28,12},{1,17},{... | collective-permute-start | bytes 147464 | tf_op jit(solution)/shard_map/ppermute | solution.py:489
  70.7 5.4 %copy-start.31 = (bf16[2,4,24,128]{3,2,1,0:T(8,128)(2,1)}, bf16[2,4,24,128]{3,2,1,0:T(8,128)(2,1)S(1)}, u32[]{:S(2)}) copy-start(bf16[2,4,24,128]{3,2,1,0:T(8,128)(2,1)S(1)} %collective-permute-done.16.refs_5_) | copy-start | bytes 147460
  70.7 10.4 %collective-permute-start.26 = (bf16[2,4,24,128]{3,2,1,0:T(8,128)(2,1)S(1)}, bf16[2,4,24,128]{3,2,1,0:T(8,128)(2,1)S(1)}, u32[]{:S(2)}, u32[]{:S(2)}) collective-permute-start(bf16[2,4,24,128]{3,2,1,0:T(8,128)(2,1)S(1)} %copy-done.40), channel_id=1, source_target_pairs={{0,20},{4,16},{8,28},{12,24},{16,4},{20,0},{24,12},{28,8},{1,21},{... | collective-permute-start | bytes 147464 | tf_op jit(solution)/shard_map/ppermute | solution.py:489
  72.2 10.5 %collective-permute-start.27 = (bf16[2,4,24,128]{3,2,1,0:T(8,128)(2,1)S(1)}, bf16[2,4,24,128]{3,2,1,0:T(8,128)(2,1)S(1)}, u32[]{:S(2)}, u32[]{:S(2)}) collective-permute-start(bf16[2,4,24,128]{3,2,1,0:T(8,128)(2,1)S(1)} %copy-done.39), channel_id=1, source_target_pairs={{0,24},{4,28},{8,16},{12,20},{16,8},{20,12},{24,0},{28,4},{1,25},{... | collective-permute-start | bytes 147464 | tf_op jit(solution)/shard_map/ppermute | solution.py:489
  74.6 8.4 %collective-permute-start.28 = (bf16[2,4,24,128]{3,2,1,0:T(8,128)(2,1)S(1)}, bf16[2,4,24,128]{3,2,1,0:T(8,128)(2,1)S(1)}, u32[]{:S(2)}, u32[]{:S(2)}) collective-permute-start(bf16[2,4,24,128]{3,2,1,0:T(8,128)(2,1)S(1)} %copy-done.38), channel_id=1, source_target_pairs={{0,28},{4,24},{8,20},{12,16},{16,12},{20,8},{24,4},{28,0},{1,29},{... | collective-permute-start | bytes 147464 | tf_op jit(solution)/shard_map/ppermute | solution.py:489
  81.0 17.5 %collective-permute-start.19 = (bf16[96,640]{1,0:T(8,128)(2,1)}, bf16[96,640]{1,0:T(8,128)(2,1)S(1)}, u32[]{:S(2)}, u32[]{:S(2)}) collective-permute-start(bf16[96,640]{1,0:T(8,128)(2,1)} %get-tuple-element.72), channel_id=1, source_target_pairs={{0,1},{1,0},{2,3},{3,2},{4,5},{5,4},{6,7},{7,6},{8,9},{9,8},{10,11... | collective-permute-start | bytes 368648 | tf_op jit(solution)/shard_map/ppermute | solution.py:489
  81.1 18.1 %collective-permute-start.20 = (bf16[96,640]{1,0:T(8,128)(2,1)}, bf16[96,640]{1,0:T(8,128)(2,1)S(1)}, u32[]{:S(2)}, u32[]{:S(2)}) collective-permute-start(bf16[96,640]{1,0:T(8,128)(2,1)} %get-tuple-element.73), channel_id=1, source_target_pairs={{0,2},{1,3},{2,0},{3,1},{4,6},{5,7},{6,4},{7,5},{8,10},{9,11},{10,... | collective-permute-start | bytes 368648 | tf_op jit(solution)/shard_map/ppermute | solution.py:489
  82.7 18.5 %collective-permute-start.21 = (bf16[96,640]{1,0:T(8,128)(2,1)}, bf16[96,640]{1,0:T(8,128)(2,1)S(1)}, u32[]{:S(2)}, u32[]{:S(2)}) collective-permute-start(bf16[96,640]{1,0:T(8,128)(2,1)} %get-tuple-element.74), channel_id=1, source_target_pairs={{0,3},{1,2},{2,1},{3,0},{4,7},{5,6},{6,5},{7,4},{8,11},{9,10},{10,... | collective-permute-start | bytes 368648 | tf_op jit(solution)/shard_map/ppermute | solution.py:489
  83.0 9.9 %collective-permute-start.8 = (bf16[96,640]{1,0:T(8,128)(2,1)S(1)}, bf16[96,640]{1,0:T(8,128)(2,1)S(1)}, u32[]{:S(2)}, u32[]{:S(2)}) collective-permute-start(bf16[96,640]{1,0:T(8,128)(2,1)S(1)} %copy-done.37), channel_id=1, source_target_pairs={{0,2},{1,3},{2,0},{3,1},{4,6},{5,7},{6,4},{7,5},{8,10},{9,11},{10,... | collective-permute-start | bytes 368648 | tf_op jit(solution)/shard_map/ppermute | solution.py:489
  84.6 11.4 %copy-start.1 = (bf16[96,640]{1,0:T(8,128)(2,1)}, bf16[96,640]{1,0:T(8,128)(2,1)S(1)}, u32[]{:S(2)}) copy-start(bf16[96,640]{1,0:T(8,128)(2,1)S(1)} %collective-permute-done.7.refs_1_) | copy-start | bytes 368644
  84.6 9.8 %collective-permute-start.9 = (bf16[96,640]{1,0:T(8,128)(2,1)S(1)}, bf16[96,640]{1,0:T(8,128)(2,1)S(1)}, u32[]{:S(2)}, u32[]{:S(2)}) collective-permute-start(bf16[96,640]{1,0:T(8,128)(2,1)S(1)} %copy-done.36), channel_id=1, source_target_pairs={{0,3},{1,2},{2,1},{3,0},{4,7},{5,6},{6,5},{7,4},{8,11},{9,10},{10,... | collective-permute-start | bytes 368648 | tf_op jit(solution)/shard_map/ppermute | solution.py:489
  92.9 15.7 %collective-permute-start.29 = (bf16[96,640]{1,0:T(8,128)(2,1)}, bf16[96,640]{1,0:T(8,128)(2,1)S(1)}, u32[]{:S(2)}, u32[]{:S(2)}) collective-permute-start(bf16[96,640]{1,0:T(8,128)(2,1)} %get-tuple-element.84), channel_id=1, source_target_pairs={{0,1},{1,0},{2,3},{3,2},{4,5},{5,4},{6,7},{7,6},{8,9},{9,8},{10,11... | collective-permute-start | bytes 368648 | tf_op jit(solution)/shard_map/ppermute | solution.py:489
  94.4 14.2 %collective-permute-start.30 = (bf16[96,640]{1,0:T(8,128)(2,1)}, bf16[96,640]{1,0:T(8,128)(2,1)S(1)}, u32[]{:S(2)}, u32[]{:S(2)}) collective-permute-start(bf16[96,640]{1,0:T(8,128)(2,1)} %get-tuple-element.85), channel_id=1, source_target_pairs={{0,2},{1,3},{2,0},{3,1},{4,6},{5,7},{6,4},{7,5},{8,10},{9,11},{10,... | collective-permute-start | bytes 368648 | tf_op jit(solution)/shard_map/ppermute | solution.py:489
  98.5 7.4 %copy-start.2 = (bf16[96,640]{1,0:T(8,128)(2,1)}, bf16[96,640]{1,0:T(8,128)(2,1)S(1)}, u32[]{:S(2)}) copy-start(bf16[96,640]{1,0:T(8,128)(2,1)S(1)} %collective-permute-done.19.refs_1_) | copy-start | bytes 368644
  98.5 10.1 %collective-permute-start.31 = (bf16[96,640]{1,0:T(8,128)(2,1)}, bf16[96,640]{1,0:T(8,128)(2,1)S(1)}, u32[]{:S(2)}, u32[]{:S(2)}) collective-permute-start(bf16[96,640]{1,0:T(8,128)(2,1)} %get-tuple-element.86), channel_id=1, source_target_pairs={{0,3},{1,2},{2,1},{3,0},{4,7},{5,6},{6,5},{7,4},{8,11},{9,10},{10,... | collective-permute-start | bytes 368648 | tf_op jit(solution)/shard_map/ppermute | solution.py:489
  99.2 6.8 %copy-start.3 = (bf16[96,640]{1,0:T(8,128)(2,1)}, bf16[96,640]{1,0:T(8,128)(2,1)S(1)}, u32[]{:S(2)}) copy-start(bf16[96,640]{1,0:T(8,128)(2,1)S(1)} %collective-permute-done.20.refs_2_) | copy-start | bytes 368644
  99.2 9.4 %collective-permute-start.10 = (bf16[96,640]{1,0:T(8,128)(2,1)}, bf16[96,640]{1,0:T(8,128)(2,1)S(1)}, u32[]{:S(2)}, u32[]{:S(2)}) collective-permute-start(bf16[96,640]{1,0:T(8,128)(2,1)} %get-tuple-element.61), channel_id=1, source_target_pairs={{0,4},{4,8},{8,12},{12,16},{16,20},{20,24},{24,28},{1,5},{5,9},{9,... | collective-permute-start | bytes 368648 | tf_op jit(solution)/shard_map/ppermute | solution.py:495
  101.2 10.6 %collective-permute-start.11 = (bf16[96,640]{1,0:T(8,128)(2,1)}, bf16[96,640]{1,0:T(8,128)(2,1)S(1)}, u32[]{:S(2)}, u32[]{:S(2)}) collective-permute-start(bf16[96,640]{1,0:T(8,128)(2,1)} %get-tuple-element.62), channel_id=1, source_target_pairs={{4,0},{8,4},{12,8},{16,12},{20,16},{24,20},{28,24},{5,1},{9,5},{13... | collective-permute-start | bytes 368648 | tf_op jit(solution)/shard_map/ppermute | solution.py:496
  116.6 7.9 %collective-permute-start.32 = (bf16[96,640]{1,0:T(8,128)(2,1)}, bf16[96,640]{1,0:T(8,128)(2,1)S(1)}, u32[]{:S(2)}, u32[]{:S(2)}) collective-permute-start(bf16[96,640]{1,0:T(8,128)(2,1)} %get-tuple-element.88), channel_id=1, source_target_pairs={{0,4},{4,8},{8,12},{12,16},{16,20},{20,24},{24,28},{1,5},{5,9},{9,... | collective-permute-start | bytes 368648 | tf_op jit(solution)/shard_map/ppermute | solution.py:495
  121.1 7.0 %collective-permute-start.33 = (bf16[96,640]{1,0:T(8,128)(2,1)}, bf16[96,640]{1,0:T(8,128)(2,1)S(1)}, u32[]{:S(2)}, u32[]{:S(2)}) collective-permute-start(bf16[96,640]{1,0:T(8,128)(2,1)} %get-tuple-element.89), channel_id=1, source_target_pairs={{4,0},{8,4},{12,8},{16,12},{20,16},{24,20},{28,24},{5,1},{9,5},{13... | collective-permute-start | bytes 368648 | tf_op jit(solution)/shard_map/ppermute | solution.py:496
  (21 other events, 60.8 us)

commit v2 on v1

--- a/solution.py
+++ b/solution.py
@@ -14,6 +14,7 @@
 LANES = 128
 CHUNK = 256
 TILE = 256
+PAIRS = 4
 
 courant_max = 0.45
 
@@ -126,33 +127,30 @@
     outs, (held, sums, arrived) = refs[:-3], refs[-3:]
     half = legendre_ref.shape[1]
     degrees = legendre_ref.shape[2]
-    rows = spectrum_ref.shape[1]
-    slots = spectrum_ref.shape[0]
+    slots, rows, _ = spectrum_ref.shape
     chunks = degrees // CHUNK + 1
     step, steps = pl.program_id(0), pl.num_programs(0)
-
-    def plan(pair):
-        first = degrees - numbers_ref[2 * pair]
-        second = degrees - numbers_ref[2 * pair + 1]
-        return first, second, (first + CHUNK - 1) // CHUNK
-
-    def copy(group, slot, pair, t):
-        index = group * pairs + pair
-        _, _, edge = plan(index)
-        inside = t < edge
-        source = 2 * index + jnp.where(inside, 0, 1)
-        block = jnp.where(inside, t, t - edge)
-        start = pl.multiple_of(block * CHUNK, CHUNK)
-        return pltpu.make_async_copy(
-            spectrum_ref.at[source, :, pl.ds(start, CHUNK)],
-            held.at[slot, pair, :, pl.ds(t * CHUNK, CHUNK)],
-            arrived.at[slot],
-        )
+    place = place_ref[0]
+
+    def plan(index):
+        first = degrees - numbers_ref[place * slots + 2 * index]
+        second = degrees - numbers_ref[place * slots + 2 * index + 1]
+        return first, second, lax.shift_right_logical(first + (CHUNK - 1), CHUNK.bit_length() - 1)
 
     def fetch(group, slot):
         for pair in range(pairs):
+            index = group * pairs + pair
+            _, _, edge = plan(index)
             for t in range(chunks):
-                copy(group, slot, pair, t).start()
+                inside = t < edge
+                source = jnp.where(inside, 2 * index, 2 * index + 1)
+                block = jnp.where(inside, t, t - edge)
+                start = pl.multiple_of(block * CHUNK, CHUNK)
+                pltpu.make_async_copy(
+                    spectrum_ref.at[source, :, pl.ds(start, CHUNK)],
+                    held.at[slot, pair, :, pl.ds(t * CHUNK, CHUNK)],
+                    arrived.at[slot],
+                ).start()
 
     @pl.when(step == 0)
     def _():
@@ -164,9 +162,7 @@
     def _():
         fetch(step + 1, 1 - now)
 
-    for pair in range(pairs):
-        for t in range(chunks):
-            copy(step, now, pair, t).wait()
+    pltpu.make_async_copy(held.at[now], held.at[now], arrived.at[now]).wait()
 
     lane = lax.broadcasted_iota(jnp.int32, (half, CHUNK), 1)
     sign = jnp.where(lane % 2 == 0, 1.0, -1.0)
@@ -176,14 +172,13 @@
         columns = []
         for t in range(chunks):
             inside = t < edge
-            local = 2 * pair + jnp.where(inside, 0, 1)
+            local = jnp.where(inside, 2 * pair, 2 * pair + 1)
             block = jnp.where(inside, t, t - edge)
             start = pl.multiple_of(block * CHUNK, CHUNK)
             length = jnp.where(inside, first, second) - start
             values = legendre_ref[local, :, pl.ds(start, CHUNK)].astype(jnp.float32)
             values = jnp.where(lane < length, values, 0.0)
-            own = jnp.where(inside, 1.0, 0.0)
-            north_first = values * own
+            north_first = values * jnp.where(inside, 1.0, 0.0)
             north_second = values - north_first
             columns.append(
                 jnp.concatenate(
@@ -213,7 +208,6 @@
 
     @pl.when(step == steps - 1)
     def _():
-        place = place_ref[0]
         for d in range(waves):
             for l in range(lats):
                 lat = (place ^ d) * lats + l
@@ -227,19 +221,19 @@
                 for f in range(FIELDS):
                     for p in range(PARTS):
                         base = (f * PARTS + p) * modes
-                        outs[f * waves + d][p, l] = whole[base : base + modes]
-
-
-def legendre_stage(spectrum, legendre, own_numbers, place, waves):
+                        outs[d][f, p, l] = whole[base : base + modes]
+
+
+def legendre_stage(spectrum, legendre, numbers, place, waves):
     slots, degrees, modes, _ = spectrum.shape
     half = legendre.shape[2]
     lats = 2 * half // waves
     rows = modes * FIELDS * PARTS
     turned = jnp.transpose(spectrum, (0, 3, 2, 1)).reshape(slots, rows, degrees)
     basis = jnp.transpose(legendre, (0, 2, 1))
-    pairs = 4
+    pairs = PAIRS
     chunks = degrees // CHUNK + 1
-    outs = [jax.ShapeDtypeStruct((PARTS, lats, modes, slots), jnp.bfloat16)] * (FIELDS * waves)
+    outs = [jax.ShapeDtypeStruct((FIELDS, PARTS, lats, modes, slots), jnp.bfloat16)] * waves
     tiles = -(-rows // LANES)
     return pl.pallas_call(
         functools.partial(legendre_kernel, waves, lats, modes, pairs),
@@ -251,137 +245,116 @@
                 pl.BlockSpec(memory_space=pl.ANY),
                 pl.BlockSpec((2 * pairs, half, degrees), lambda i, *_: (i, 0, 0)),
             ],
-            out_specs=[
-                pl.BlockSpec((PARTS, lats, modes, slots), lambda i, *_: (0, 0, 0, 0))
-                for _ in outs
-            ],
+            out_specs=[pl.BlockSpec(out.shape, lambda i, *_: (0,) * 5) for out in outs],
             scratch_shapes=[
                 pltpu.VMEM((2, pairs, rows, chunks * CHUNK), jnp.bfloat16),
                 pltpu.VMEM((tiles, 2 * half * slots, LANES), jnp.float32),
                 pltpu.SemaphoreType.DMA((2,)),
             ],
         ),
-        compiler_params=pltpu.CompilerParams(dimension_semantics=("arbitrary",)),
+        compiler_params=pltpu.CompilerParams(
+            dimension_semantics=("arbitrary",), vmem_limit_bytes=24 << 20
+        ),
         cost_estimate=cost(slots * rows * degrees * 2 * half, slots * rows * degrees),
         name="legendre_sums",
-    )(own_numbers, place, turned, basis)
-
-
-def twiddle_kernel(low_cos_ref, low_sin_ref, high_cos_ref, high_sin_ref, out_ref):
-    low_cos, low_sin = low_cos_ref[0], low_sin_ref[0]
+    )(numbers, place, turned, basis)
+
+
+def twiddle_kernel(low_cos_ref, low_sin_ref, turn_cos_ref, turn_sin_ref, out_ref):
+    slots = low_cos_ref.shape[1]
+    shape = (LANES, slots)
+    turn_cos = jnp.broadcast_to(turn_cos_ref[0], shape).T
+    turn_sin = jnp.broadcast_to(turn_sin_ref[0], shape).T
+    cos, sin = low_cos_ref[0], low_sin_ref[0]
     for block in range(out_ref.shape[3] // LANES):
-        high_cos = high_cos_ref[0, :, block : block + 1]
-        high_sin = high_sin_ref[0, :, block : block + 1]
         lanes = pl.ds(block * LANES, LANES)
-        out_ref[0, 0, :, lanes] = (high_cos * low_cos - high_sin * low_sin).astype(jnp.bfloat16)
-        out_ref[0, 1, :, lanes] = -(high_sin * low_cos + high_cos * low_sin).astype(jnp.bfloat16)
+        out_ref[0, 0, :, lanes] = cos.astype(jnp.bfloat16)
+        out_ref[0, 1, :, lanes] = (-sin).astype(jnp.bfloat16)
+        cos, sin = cos * turn_cos - sin * turn_sin, sin * turn_cos + cos * turn_sin
 
 
 def twiddle_stage(numbers):
     waves, slots = numbers.shape
     count = NLON // 2
-    blocks = count // LANES
-
-    def angles(steps):
-        residue = numbers[:, :, None] * steps[None, None, :] % NLON
-        return residue.astype(jnp.float32) * (2.0 * math.pi / NLON)
-
-    low = angles(jnp.arange(LANES, dtype=jnp.int32))
-    high = angles(jnp.arange(blocks, dtype=jnp.int32) * LANES)
+
+    def angles(residue):
+        return (residue % NLON).astype(jnp.float32) * (2.0 * math.pi / NLON)
+
+    low = angles(numbers[:, :, None] * jnp.arange(LANES, dtype=jnp.int32)[None, None, :])
+    turn = angles(numbers * LANES)[:, None, :]
     weight = jnp.where(numbers == 0, 1.0, 2.0).astype(jnp.float32)[:, :, None]
 
-    def spec(last):
-        return pl.BlockSpec((1, slots, last), lambda i: (i, 0, 0))
+    def spec(rows, last):
+        return pl.BlockSpec((1, rows, last), lambda i: (i, 0, 0))
 
     return pl.pallas_call(
         twiddle_kernel,
         out_shape=jax.ShapeDtypeStruct((waves, PARTS, slots, count), jnp.bfloat16),
         grid=(waves,),
-        in_specs=[spec(LANES), spec(LANES), spec(blocks), spec(blocks)],
+        in_specs=[spec(slots, LANES), spec(slots, LANES), spec(1, slots), spec(1, slots)],
         out_specs=pl.BlockSpec((1, PARTS, slots, count), lambda i: (i, 0, 0, 0)),
+        compiler_params=pltpu.CompilerParams(vmem_limit_bytes=8 << 20),
         cost_estimate=cost(8 * waves * slots * count, 4 * waves * slots * count),
         name="twiddles",
-    )(jnp.cos(low), jnp.sin(low), weight * jnp.cos(high), weight * jnp.sin(high))
-
-
-def synthesis_kernel(waves, levs, place_ref, *refs):
+    )(weight * jnp.cos(low), weight * jnp.sin(low), jnp.cos(turn), jnp.sin(turn))
+
+
+def synthesis_kernel(waves, levs, field, place_ref, *refs):
     blocks, (sign_ref, twiddle_ref) = refs[:waves], refs[waves : waves + 2]
     outs, (left, grid) = refs[waves + 2 : -2], refs[-2:]
-    _, lats, modes, slots = blocks[0].shape
+    _, _, lats, modes, slots = blocks[0].shape
     rows = lats * modes
-    step, steps = pl.program_id(0), pl.num_programs(0)
-
-    @pl.when(step == 0)
-    def _():
-        for d in range(waves):
-            sign = sign_ref[d]
-            for p in range(PARTS):
-                values = blocks[d][p].reshape(rows, slots)
-                lanes = pl.ds((d * PARTS + p) * slots, slots)
-                left[:rows, lanes] = values
-                left[rows:, lanes] = values * sign
-
-    right = twiddle_ref[...].reshape(waves * PARTS * slots, TILE)
-    result = jnp.dot(left[...], right, preferred_element_type=jnp.float32).astype(jnp.bfloat16)
+    for d in range(waves):
+        sign = sign_ref[d]
+        for p in range(PARTS):
+            values = blocks[d][field, p].reshape(rows, slots)
+            lanes = pl.ds((d * PARTS + p) * slots, slots)
+            left[:rows, lanes] = values
+            left[rows:, lanes] = values * sign
+
     width = NLON // levs
     ratio = width // TILE
+    steps = twiddle_ref.shape[3] // TILE
     lane = lax.broadcasted_iota(jnp.int32, (rows, LANES), 1)
-    for which in range(2):
-        values = result[which * rows : (which + 1) * rows]
-        block = step + which * steps
-        owner = block // ratio
-        inner = lax.rem(block, ratio)
-        start = pl.multiple_of(inner * TILE, TILE)
-        grid[owner, :, pl.ds(start, TILE)] = values
-
-        @pl.when(inner == 0)
-        def _():
-            west = lax.rem(owner + levs - 1, levs)
-            grid[west, :, pl.ds(width, LANES)] = jnp.where(
-                lane < LANES // 2, values[:, :LANES], grid[west, :, pl.ds(width, LANES)]
-            )
-
-        @pl.when(inner == ratio - 1)
-        def _():
-            east = lax.rem(owner + 1, levs)
-            grid[east, :, pl.ds(width, LANES)] = jnp.where(
-                lane < LANES // 2, grid[east, :, pl.ds(width, LANES)], values[:, -LANES:]
-            )
-
-    @pl.when(step == steps - 1)
-    def _():
-        place = place_ref[0]
-        for e in range(levs):
-            outs[e][...] = grid[place ^ e]
-
-
-def synthesis_stage(blocks, sign, twiddle, place, levs):
+    half = {}
+    for step in range(steps):
+        right = twiddle_ref[:, :, :, pl.ds(step * TILE, TILE)]
+        right = right.reshape(waves * PARTS * slots, TILE)
+        result = jnp.dot(left[...], right, preferred_element_type=jnp.float32)
+        result = result.astype(jnp.bfloat16)
+        for which in range(2):
+            values = result[which * rows : (which + 1) * rows]
+            owner, inner = divmod(step + which * steps, ratio)
+            grid[owner, :, pl.ds(inner * TILE, TILE)] = values
+            if inner == 0:
+                half[owner, 0] = values[:, :LANES]
+            if inner == ratio - 1:
+                half[owner, 1] = values[:, -LANES:]
+    for owner in range(levs):
+        grid[owner, :, pl.ds(width, LANES)] = jnp.where(
+            lane < LANES // 2, half[(owner + 1) % levs, 0], half[(owner - 1) % levs, 1]
+        )
+    place = place_ref[0]
+    for e in range(levs):
+        outs[e][...] = grid[place ^ e]
+
+
+def synthesis_stage(blocks, sign, twiddle, place, levs, field):
     waves, _, slots, count = twiddle.shape
-    _, lats, modes, _ = blocks[0].shape
+    _, _, lats, modes, _ = blocks[0].shape
     rows = lats * modes
     width = NLON // levs + LANES
     depth = waves * PARTS * slots
     return pl.pallas_call(
-        functools.partial(synthesis_kernel, waves, levs),
+        functools.partial(synthesis_kernel, waves, levs, field),
         out_shape=[jax.ShapeDtypeStruct((rows, width), jnp.bfloat16)] * levs,
-        grid_spec=pltpu.PrefetchScalarGridSpec(
-            num_scalar_prefetch=1,
-            grid=(count // TILE,),
-            in_specs=[
-                pl.BlockSpec((PARTS, lats, modes, slots), lambda i, *_: (0, 0, 0, 0))
-                for _ in blocks
-            ]
-            + [
-                pl.BlockSpec((waves, 1, slots), lambda i, *_: (0, 0, 0)),
-                pl.BlockSpec((waves, PARTS, slots, TILE), lambda i, *_: (0, 0, 0, i)),
-            ],
-            out_specs=[pl.BlockSpec((rows, width), lambda i, *_: (0, 0))] * levs,
-            scratch_shapes=[
-                pltpu.VMEM((2 * rows, depth), jnp.bfloat16),
-                pltpu.VMEM((levs, rows, width), jnp.bfloat16),
-            ],
-        ),
-        compiler_params=pltpu.CompilerParams(dimension_semantics=("arbitrary",)),
+        in_specs=[pl.BlockSpec(memory_space=pltpu.SMEM)] + [vmem()] * (waves + 2),
+        out_specs=[vmem()] * levs,
+        scratch_shapes=[
+            pltpu.VMEM((2 * rows, depth), jnp.bfloat16),
+            pltpu.VMEM((levs, rows, width), jnp.bfloat16),
+        ],
+        compiler_params=pltpu.CompilerParams(vmem_limit_bytes=16 << 20),
         cost_estimate=cost(4 * rows * depth * count, 2 * depth * count),
         name="synthesis",
     )(place, *blocks, sign, twiddle)
@@ -404,17 +377,29 @@
     return result[:count] + (result[count : 2 * count] + result[2 * count :])
 
 
-def tracer_kernel(modes, vertical_ref, *refs):
-    blocks, (field_ref, north_ref, south_ref) = refs[:-3], refs[-3:]
+def keep_edges(lat, lats, values, odd, pair_ref, diagonal_ref):
+    edge = values.astype(jnp.bfloat16)
+    if 0 < lat < lats - 1:
+        return
+    takes_pair = 1 if lat == 0 else 0
+
+    @pl.when(odd == takes_pair)
+    def _():
+        pair_ref[...] = edge
+
+    @pl.when(odd != takes_pair)
+    def _():
+        diagonal_ref[...] = edge
+
+
+def tracer_kernel(modes, odd_ref, vertical_ref, *refs):
+    blocks, (field_ref, pair_ref, diagonal_ref) = refs[:-3], refs[-3:]
     terms = three_terms(vertical_ref[...])
     lats = field_ref.shape[0]
     for lat in range(lats):
         values = levels_of(terms, blocks, lat, modes)
         field_ref[lat] = values
-        if lat == 0:
-            north_ref[...] = values.astype(jnp.bfloat16)
-        if lat == lats - 1:
-            south_ref[...] = values.astype(jnp.bfloat16)
+        keep_edges(lat, lats, values, odd_ref[0], pair_ref, diagonal_ref)
 
 
 def courant_kernel(modes, vertical_ref, *refs):
@@ -434,11 +419,17 @@
     )
 
 
-def stepped(lat, tracer_ref, above_ref, below_ref, courant_x, courant_y):
+def stepped(lat, odd, tracer_ref, pair_ref, diagonal_ref, courant_x, courant_y):
     lats, _, width = tracer_ref.shape
     center = tracer_ref[lat]
-    northern = tracer_ref[lat - 1] if lat > 0 else above_ref[...].astype(jnp.float32)
-    southern = tracer_ref[lat + 1] if lat < lats - 1 else below_ref[...].astype(jnp.float32)
+
+    def outside(takes_pair):
+        pair = pair_ref[...].astype(jnp.float32)
+        diagonal = diagonal_ref[...].astype(jnp.float32)
+        return jnp.where(odd == takes_pair, pair, diagonal)
+
+    northern = tracer_ref[lat - 1] if lat > 0 else outside(1)
+    southern = tracer_ref[lat + 1] if lat < lats - 1 else outside(0)
     return upwind(
         center,
         pltpu.roll(center, 1, 1),
@@ -450,34 +441,36 @@
     )
 
 
-def first_step_kernel(modes, vertical_ref, tracer_ref, above_ref, below_ref, x_ref, *refs):
-    blocks, (y_ref, out_ref, north_ref, south_ref) = refs[:-4], refs[-4:]
+def first_step_kernel(modes, odd_ref, vertical_ref, tracer_ref, pair_ref, diagonal_ref, x_ref, *refs):
+    blocks, (y_ref, out_ref, next_pair_ref, next_diagonal_ref) = refs[:-4], refs[-4:]
     terms = three_terms(vertical_ref[...])
     lats = tracer_ref.shape[0]
-    for lat in range(lats):
+    odd = odd_ref[0]
+    for lat in (0, lats - 1, *range(1, lats - 1)):
         courant_y = courant_max * jnp.tanh(levels_of(terms, blocks, lat, modes))
         y_ref[lat] = courant_y
-        values = stepped(lat, tracer_ref, above_ref, below_ref, x_ref[lat], courant_y)
+        values = stepped(lat, odd, tracer_ref, pair_ref, diagonal_ref, x_ref[lat], courant_y)
         out_ref[lat] = values
-        if lat == 0:
-            north_ref[...] = values.astype(jnp.bfloat16)
-        if lat == lats - 1:
-            south_ref[...] = values.astype(jnp.bfloat16)
-
-
-def second_step_kernel(tracer_ref, above_ref, below_ref, x_ref, y_ref, out_ref):
+        keep_edges(lat, lats, values, odd, next_pair_ref, next_diagonal_ref)
+
+
+def second_step_kernel(odd_ref, tracer_ref, pair_ref, diagonal_ref, x_ref, y_ref, out_ref):
     width = out_ref.shape[2]
     for lat in range(tracer_ref.shape[0]):
-        values = stepped(lat, tracer_ref, above_ref, below_ref, x_ref[lat], y_ref[lat])
+        values = stepped(
+            lat, odd_ref[0], tracer_ref, pair_ref, diagonal_ref, x_ref[lat], y_ref[lat]
+        )
         out_ref[:, lat, :] = values[:, :width]
 
 
 def local_call(kernel, outs, name, *operands):
+    smem = pl.BlockSpec(memory_space=pltpu.SMEM)
     return pl.pallas_call(
         kernel,
         out_shape=outs,
-        in_specs=[vmem() for _ in operands],
+        in_specs=[smem if operand.dtype == jnp.int32 else vmem() for operand in operands],
         out_specs=jax.tree.map(lambda _: vmem(), outs),
+        compiler_params=pltpu.CompilerParams(vmem_limit_bytes=16 << 20),
         cost_estimate=cost(4_000_000, 4_000_000),
         name=name,
     )(*operands)
@@ -490,11 +483,12 @@
     ]
 
 
-def edges(north, south):
+def edges(pair, diagonal):
     count = lax.axis_size("wave")
-    above = lax.ppermute(south, "wave", [(i, i + 1) for i in range(count - 1)])
-    below = lax.ppermute(north, "wave", [(i + 1, i) for i in range(count - 1)])
-    return above, below
+    steps = [(i, i + 1) for i in range(1, count - 1, 2)]
+    diagonal = lax.ppermute(diagonal, "wave", steps + [(b, a) for a, b in steps])
+    pair = lax.ppermute(pair, "wave", [(i, i ^ 1) for i in range(count)])
+    return pair, diagonal
 
 
 def tiled_body(spectrum, legendre, wave_numbers, vertical):
@@ -504,47 +498,55 @@
     lats = 2 * legendre.shape[2] // waves
     width = NLON // levs
     wave_place, lev_place = lax.axis_index("wave"), lax.axis_index("lev")
+    odd = lax.rem(wave_place, 2)[None]
+
+    fourier = legendre_stage(spectrum, legendre, wave_numbers, wave_place[None], waves)
     by_wave = wave_numbers.reshape(waves, slots)[wave_place ^ jnp.arange(waves)]
     by_lev = vertical.reshape(levels, levs, modes)[:, lev_place ^ jnp.arange(levs)]
     by_lev = by_lev.reshape(levels, levs * modes)
     sign = jnp.where(by_wave % 2 == 0, 1.0, -1.0).astype(jnp.bfloat16)[:, None, :]
-
-    fourier = legendre_stage(spectrum, legendre, by_wave[0], wave_place[None], waves)
     twiddle = twiddle_stage(by_wave)
+    received = exchange(fourier, "wave")
     columns = {}
     for field in (2, 0, 1):
-        received = exchange(fourier[field * waves : (field + 1) * waves], "wave")
-        grid = synthesis_stage(received, sign, twiddle, lev_place[None], levs)
+        grid = synthesis_stage(received, sign, twiddle, lev_place[None], levs, field)
         columns[field] = exchange(grid, "lev")
 
     whole = jax.ShapeDtypeStruct((lats, levels, width + LANES), jnp.float32)
     row = jax.ShapeDtypeStruct((levels, width + LANES), jnp.bfloat16)
-    tracer, north, south = local_call(
-        functools.partial(tracer_kernel, modes), (whole, row, row), "tracer", by_lev, *columns[2]
-    )
-    above, below = edges(north, south)
+    tracer, pair, diagonal = local_call(
+        functools.partial(tracer_kernel, modes),
+        (whole, row, row),
+        "tracer",
+        odd,
+        by_lev,
+        *columns[2],
+    )
+    pair, diagonal = edges(pair, diagonal)
     courant_x = local_call(
         functools.partial(courant_kernel, modes), whole, "courant_x", by_lev, *columns[0]
     )
-    courant_y, tracer, north, south = local_call(
+    courant_y, tracer, next_pair, next_diagonal = local_call(
         functools.partial(first_step_kernel, modes),
         (whole, whole, row, row),
         "first_step",
+        odd,
         by_lev,
         tracer,
-        above,
-        below,
+        pair,
+        diagonal,
         courant_x,
         *columns[1],
     )
-    above, below = edges(north, south)
+    pair, diagonal = edges(next_pair, next_diagonal)
     return local_call(
         second_step_kernel,
         jax.ShapeDtypeStruct((levels, lats, width), jnp.float32),
         "second_step",
+        odd,
         tracer,
-        above,
-        below,
+        pair,
+        diagonal,
         courant_x,
         courant_y,
     )
@@ -561,6 +563,7 @@
         and levs & (levs - 1) == 0
         and NLON // levs % TILE == 0
         and levs % 2 == 0
+        and 2 * legendre.shape[2] // waves >= 2
     )
     form = tiled_body if tiled else plain_body
     return form(spectrum, legendre, wave_numbers, vertical)

time: 134 us -> 94.8 us (0.71)
  starting transfers between devices: 51 us -> 20.6 us
  Pallas kernels: 57.4 us -> 29 us
  waiting for transfers between devices: 11.3 us -> 35.1 us
  other arithmetic: 6.86 us -> 2.33 us
    ppermute x30 -> x16, starting transfers between devices: 37.5 us -> 14.1 us  [exchange(): lax.ppermute(blocks[d], axis, [(i, i ^ d) for i in range(count)])]
    ppermute x30 -> x16, waiting for transfers between devices: 3.31 us -> 26.3 us  [exchange(): lax.ppermute(blocks[d], axis, [(i, i ^ d) for i in range(count)])]
    pallas_call x7, Pallas kernels: 27.5 us -> 7.64 us  [the longest x4 4.47 us: local_call(): pl.pallas_call(kernel, out_shape=outs, in_specs=[smem if operand.dtype ==...]
    ppermute x4, starting transfers between devices: 13.5 us -> 6.53 us  [the longest x2 4.41 us: edges(): lax.ppermute(diagonal, 'wave', steps + [(b, a) for a, b in steps])]
    pallas_call x1, Pallas kernels: 7.38 us -> 1.79 us  [twiddle_stage(): pl.pallas_call(twiddle_kernel, out_shape=jax.ShapeDtypeStruct((waves, PAR...]
    sin x1, other arithmetic: 3.23 us -> 0.16 us  [twiddle_stage(): jnp.sin(turn)]
    pallas_call x1, Pallas kernels: 22.5 us -> 19.6 us  [legendre_stage(): pl.pallas_call(functools.partial(legendre_kernel, waves, lats, modes, pai...]
    unnamed x103 -> x13, local copies, waits for them, and re-layouts: 2.7 us -> 5.15 us
  transfers between devices with their start and end apart: 34 -> 20, of which waited for: 5 -> 11; matrix products, arithmetic and copies ran while one was open for 6% -> 4% of each run, Pallas kernels for 21% -> 6%
where the time goes in v2:
time: 94.8 us; the launch traced here: 93.8 us
  waiting for transfers between devices  35.1 us (37%)
  Pallas kernels  29 us (31%)
  starting transfers between devices  20.6 us (22%)
  local copies, waits for them, and re-layouts  6.47 us (7%)
  other arithmetic  2.33 us (2%)
    ppermute x16, waiting for transfers between devices, exchange(): lax.ppermute(blocks[d], axis, [(i, i ^ d) for i in range(count)])  26.3 us
    pallas_call x1, Pallas kernels, legendre_stage(): pl.pallas_call(functools.partial(legendre_kernel, waves, lats, modes, pai...  19.6 us
    ppermute x16, starting transfers between devices, exchange(): lax.ppermute(blocks[d], axis, [(i, i ^ d) for i in range(count)])  14.1 us
    ppermute x2, waiting for transfers between devices, edges(): lax.ppermute(diagonal, 'wave', steps + [(b, a) for a, b in steps])  7.32 us
    unnamed x13, local copies, waits for them, and re-layouts  5.15 us
    pallas_call x4, Pallas kernels, local_call(): pl.pallas_call(kernel, out_shape=outs, in_specs=[smem if operand.dtype ==...  4.47 us
    ppermute x2, starting transfers between devices, edges(): lax.ppermute(diagonal, 'wave', steps + [(b, a) for a, b in steps])  4.41 us
    pallas_call x3, Pallas kernels, synthesis_stage(): pl.pallas_call(functools.partial(synthesis_kernel, waves, levs, field), o...  3.18 us
  transfers between devices with their start and end apart: 20, of which 11 were waited for; matrix products, arithmetic and copies ran while one was open for 4% of the time, Pallas kernels for 6%

profile of v2, /device:TPU:16, one launch (start us, length us, event | category | flops | bytes accessed | tf_op | source)
XLA Modules:
  0.0 93.8 jit_solution(6823891281180641939)
XLA Ops:
  0.0 2.2 %copy-done.2 = bf16[128,1024,16]{1,2,0:T(8,128)(2,1)S(1)} copy-done((bf16[128,1024,16]{1,2,0:T(8,128)(2,1)S(1)}, bf16[128,1024,16]{1,2,0:T(8,128)(2,1)}, u32[]{:S(2)}) %copy-start.2) | copy-done | bytes 4194328
  2.2 0.7 copy-done.3
  2.9 19.6 %legendre_sums.1 = (bf16[3,2,4,24,128]{4,3,2,1,0:T(8,128)(2,1)S(1)}, bf16[3,2,4,24,128]{4,3,2,1,0:T(8,128)(2,1)S(1)}, bf16[3,2,4,24,128]{4,3,2,1,0:T(8,128)(2,1)...) custom-call(s32[1024]{0:T(1024)S(1)} %copy-done.3, ...), custom_call_target="tpu_custom_call" | custom-call | flops 603979776 | bytes 18874368 | tf_op jit(solution)/shard_map/legendre_sums/pallas_call | solution.py:238
  22.5 1.6 %collective-permute-start = (bf16[3,2,4,24,128]{4,3,2,1,0:T(8,128)(2,1)S(1)}, bf16[3,2,4,24,128]{4,3,2,1,0:T(8,128)(2,1)S(1)}, u32[]{:S(2)}, u32[]{:S(2)}) collective-permute-start(bf16[3,2,4,24,128]{4,3,2,1,0:T(8,128)(2,1)S(1)} %get-tuple-element.33), channel_id=1, source_target_pairs={{0,4},{4,0},{8,12},{12,8},{16,20},{20,16},{24,28},{28,24},{1,5},{5... | collective-permute-start | bytes 442376 | tf_op jit(solution)/shard_map/ppermute | solution.py:482
  24.0 1.6 %collective-permute-start.1 = (bf16[3,2,4,24,128]{4,3,2,1,0:T(8,128)(2,1)S(1)}, bf16[3,2,4,24,128]{4,3,2,1,0:T(8,128)(2,1)S(1)}, u32[]{:S(2)}, u32[]{:S(2)}) collective-permute-start(bf16[3,2,4,24,128]{4,3,2,1,0:T(8,128)(2,1)S(1)} %get-tuple-element.34), channel_id=1, source_target_pairs={{0,8},{4,12},{8,0},{12,4},{16,24},{20,28},{24,16},{28,20},{1,9},{5... | collective-permute-start | bytes 442376 | tf_op jit(solution)/shard_map/ppermute | solution.py:482
  25.6 0.4 collective-permute-start.2
  26.0 0.0 collective-permute-start.3
  26.1 3.8 %collective-permute-start.4 = (bf16[3,2,4,24,128]{4,3,2,1,0:T(8,128)(2,1)S(1)}, bf16[3,2,4,24,128]{4,3,2,1,0:T(8,128)(2,1)S(1)}, u32[]{:S(2)}, u32[]{:S(2)}) collective-permute-start(bf16[3,2,4,24,128]{4,3,2,1,0:T(8,128)(2,1)S(1)} %get-tuple-element.37), channel_id=1, source_target_pairs={{0,20},{4,16},{8,28},{12,24},{16,4},{20,0},{24,12},{28,8},{1,21},{... | collective-permute-start | bytes 442376 | tf_op jit(solution)/shard_map/ppermute | solution.py:482
  29.9 0.0 copy-done.4
  29.9 0.6 gather_fusion.1
  30.5 0.2 fusion.13
  30.6 0.1 cos.7.turn_cos_ref
  30.8 0.0 collective-permute-done.refs_1_
  30.8 0.5 collective-permute-start.5
  31.3 2.2 %collective-permute-done.1.refs_2_ = bf16[3,2,4,24,128]{4,3,2,1,0:T(8,128)(2,1)S(1)} collective-permute-done((bf16[3,2,4,24,128]{4,3,2,1,0:T(8,128)(2,1)S(1)}, bf16[3,2,4,24,128]{4,3,2,1,0:T(8,128)(2,1)S(1)}, u32[]{:S(2)}, u32[]{:S(2)}) %collective-permute-start.1) | collective-permute-done | bytes 147488 | tf_op jit(solution)/shard_map/ppermute | solution.py:482
  33.5 0.0 collective-permute-start.6
  33.5 2.1 %sine_multiply_fusion = (f32[8,128,128]{2,1,0:T(8,128)S(1)}, f32[8,128,128]{2,1,0:T(8,128)S(1)}) fusion(s32[8,128]{1,0:T(8,128)S(1)} %gather_fusion.1, f32[8,128]{1,0:T(8,128)S(1)} %compare_select_fusion.5), kind=kLoop, calls=%fused_computation.8 | loop fusion | flops 2097152 | bytes 1056768 | tf_op jit(solution)/shard_map/mul | solution.py:299
  35.7 1.8 %twiddles.1.refs_9_ = bf16[8,2,128,1024]{3,2,1,0:T(8,128)(2,1)S(1)} custom-call(f32[8,128,128]{2,1,0:T(8,128)S(1)} %get-tuple-element.62.low_cos_ref, f32[8,128,128]{2,1,0:T(8,128)S(1)} %get-tuple-element.61.low_sin_ref, f32[8,1,128]{2,1,0:T(1,128)S(1)} %cos.7.turn_cos_ref, f32[8,1,128]{2,1,0:T(1,128)S(1)} %get-tuple-element.59.turn_sin_ref), custom_call_target="tpu_custom_call" | custom-call | flops 8388608 | bytes 4194304 | tf_op jit(solution)/shard_map/twiddles/pallas_call | solution.py:290
  37.5 0.0 copy-start
  37.5 0.0 collective-permute-done.2.refs_3_
  37.5 0.0 collective-permute-done.3.refs_4_
  37.5 8.8 %collective-permute-done.4.refs_5_ = bf16[3,2,4,24,128]{4,3,2,1,0:T(8,128)(2,1)S(1)} collective-permute-done((bf16[3,2,4,24,128]{4,3,2,1,0:T(8,128)(2,1)S(1)}, bf16[3,2,4,24,128]{4,3,2,1,0:T(8,128)(2,1)S(1)}, u32[]{:S(2)}, u32[]{:S(2)}) %collective-permute-start.4) | collective-permute-done | bytes 147488 | tf_op jit(solution)/shard_map/ppermute | solution.py:482
  46.3 6.1 %collective-permute-done.5.refs_6_ = bf16[3,2,4,24,128]{4,3,2,1,0:T(8,128)(2,1)S(1)} collective-permute-done((bf16[3,2,4,24,128]{4,3,2,1,0:T(8,128)(2,1)S(1)}, bf16[3,2,4,24,128]{4,3,2,1,0:T(8,128)(2,1)S(1)}, u32[]{:S(2)}, u32[]{:S(2)}) %collective-permute-start.5) | collective-permute-done | bytes 147488 | tf_op jit(solution)/shard_map/ppermute | solution.py:482
  52.4 2.5 %collective-permute-done.6.refs_7_ = bf16[3,2,4,24,128]{4,3,2,1,0:T(8,128)(2,1)S(1)} collective-permute-done((bf16[3,2,4,24,128]{4,3,2,1,0:T(8,128)(2,1)S(1)}, bf16[3,2,4,24,128]{4,3,2,1,0:T(8,128)(2,1)S(1)}, u32[]{:S(2)}, u32[]{:S(2)}) %collective-permute-start.6) | collective-permute-done | bytes 147488 | tf_op jit(solution)/shard_map/ppermute | solution.py:482
  54.9 1.1 %synthesis.3 = (bf16[96,640]{1,0:T(8,128)(2,1)S(1)}, bf16[96,640]{1,0:T(8,128)(2,1)S(1)}, bf16[96,640]{1,0:T(8,128)(2,1)S(1)}, bf16[96,640]{1,0:T(8,128)(2,1)S(1)}) custom-call(s32[1]{0:T(128)} %bitcast.5.place_ref, bf16[3,2,4,24,128]{4,3,2,1,0:T(8,128)(2,1)S(1)} %get-tuple-element.32.refs_0_, bf16[3,2,4,24,128]{4,3,2,1,0:T(8,128)(2,1)S(1)} %collective-permute-done.refs_1_, ...), custom_call_target="tpu_custom_call" | custom-call | flops 805306368 | bytes 4194304 | tf_op jit(solution)/shard_map/synthesis/pallas_call | solution.py:348
  56.0 0.1 collective-permute-start.7
  56.1 1.1 %synthesis.4 = (bf16[96,640]{1,0:T(8,128)(2,1)S(1)}, bf16[96,640]{1,0:T(8,128)(2,1)S(1)}, bf16[96,640]{1,0:T(8,128)(2,1)S(1)}, bf16[96,640]{1,0:T(8,128)(2,1)S(1)}) custom-call(s32[1]{0:T(128)} %bitcast.5.place_ref, bf16[3,2,4,24,128]{4,3,2,1,0:T(8,128)(2,1)S(1)} %get-tuple-element.32.refs_0_, bf16[3,2,4,24,128]{4,3,2,1,0:T(8,128)(2,1)S(1)} %collective-permute-done.refs_1_, ...), custom_call_target="tpu_custom_call" | custom-call | flops 805306368 | bytes 4194304 | tf_op jit(solution)/shard_map/synthesis/pallas_call | solution.py:348
  57.1 0.0 copy-done
  57.1 0.6 collective-permute-start.12
  57.7 1.5 %collective-permute-start.13 = (bf16[96,640]{1,0:T(8,128)(2,1)S(1)}, bf16[96,640]{1,0:T(8,128)(2,1)S(1)}, u32[]{:S(2)}, u32[]{:S(2)}) collective-permute-start(bf16[96,640]{1,0:T(8,128)(2,1)S(1)} %get-tuple-element.49), channel_id=1, source_target_pairs={{0,2},{1,3},{2,0},{3,1},{4,6},{5,7},{6,4},{7,5},{8,10},{9,11},{10,... | collective-permute-start | bytes 368648 | tf_op jit(solution)/shard_map/ppermute | solution.py:482
  59.2 0.0 collective-permute-start.14
  59.2 1.4 %collective-permute-start.8 = (bf16[96,640]{1,0:T(8,128)(2,1)S(1)}, bf16[96,640]{1,0:T(8,128)(2,1)S(1)}, u32[]{:S(2)}, u32[]{:S(2)}) collective-permute-start(bf16[96,640]{1,0:T(8,128)(2,1)S(1)} %get-tuple-element.42), channel_id=1, source_target_pairs={{0,2},{1,3},{2,0},{3,1},{4,6},{5,7},{6,4},{7,5},{8,10},{9,11},{10,... | collective-permute-start | bytes 368648 | tf_op jit(solution)/shard_map/ppermute | solution.py:482
  60.7 0.0 collective-permute-done.7.refs_1_
  60.7 0.5 collective-permute-start.9
  61.2 0.0 copy-done.5
  61.2 0.1 copy.9
  61.3 0.6 gather_fusion
  61.9 0.1 copy.12.vertical_ref
  61.9 0.0 copy-start.1
  62.0 2.2 %copy-done.1 = bf16[8,2,128,1024]{3,2,1,0:T(8,128)(2,1)S(1)} copy-done((bf16[8,2,128,1024]{3,2,1,0:T(8,128)(2,1)S(1)}, bf16[8,2,128,1024]{3,2,1,0:T(8,128)(2,1)}, u32[]{:S(2)}) %copy-start.1) | copy-done | bytes 4194328
  64.1 1.0 %synthesis.5 = (bf16[96,640]{1,0:T(8,128)(2,1)S(1)}, bf16[96,640]{1,0:T(8,128)(2,1)S(1)}, bf16[96,640]{1,0:T(8,128)(2,1)S(1)}, bf16[96,640]{1,0:T(8,128)(2,1)S(1)}) custom-call(s32[1]{0:T(128)} %bitcast.5.place_ref, bf16[3,2,4,24,128]{4,3,2,1,0:T(8,128)(2,1)S(1)} %get-tuple-element.32.refs_0_, bf16[3,2,4,24,128]{4,3,2,1,0:T(8,128)(2,1)S(1)} %collective-permute-done.refs_1_, ...), custom_call_target="tpu_custom_call" | custom-call | flops 805306368 | bytes 4194304 | tf_op jit(solution)/shard_map/synthesis/pallas_call | solution.py:348
  65.2 3.9 %collective-permute-done.8.refs_2_ = bf16[96,640]{1,0:T(8,128)(2,1)S(1)} collective-permute-done((bf16[96,640]{1,0:T(8,128)(2,1)S(1)}, bf16[96,640]{1,0:T(8,128)(2,1)S(1)}, u32[]{:S(2)}, u32[]{:S(2)}) %collective-permute-start.8) | collective-permute-done | bytes 122912 | tf_op jit(solution)/shard_map/ppermute | solution.py:482
  69.1 0.0 collective-permute-start.15
  69.1 1.1 %collective-permute-done.9.refs_3_ = bf16[96,640]{1,0:T(8,128)(2,1)S(1)} collective-permute-done((bf16[96,640]{1,0:T(8,128)(2,1)S(1)}, bf16[96,640]{1,0:T(8,128)(2,1)S(1)}, u32[]{:S(2)}, u32[]{:S(2)}) %collective-permute-start.9) | collective-permute-done | bytes 122912 | tf_op jit(solution)/shard_map/ppermute | solution.py:482
  70.1 1.4 %collective-permute-start.16 = (bf16[96,640]{1,0:T(8,128)(2,1)S(1)}, bf16[96,640]{1,0:T(8,128)(2,1)S(1)}, u32[]{:S(2)}, u32[]{:S(2)}) collective-permute-start(bf16[96,640]{1,0:T(8,128)(2,1)S(1)} %get-tuple-element.53), channel_id=1, source_target_pairs={{0,2},{1,3},{2,0},{3,1},{4,6},{5,7},{6,4},{7,5},{8,10},{9,11},{10,... | collective-permute-start | bytes 368648 | tf_op jit(solution)/shard_map/ppermute | solution.py:482
  71.5 0.7 tracer.1
  72.3 0.0 collective-permute-done.12.refs_1_
  72.3 0.6 collective-permute-start.17
  72.9 0.0 collective-permute-done.13.refs_2_
  72.9 0.5 collective-permute-start.10
  73.4 0.0 collective-permute-done.14.refs_3_
  73.4 2.5 %collective-permute-start.11 = (bf16[96,640]{1,0:T(8,128)(2,1)S(1)}, bf16[96,640]{1,0:T(8,128)(2,1)S(1)}, u32[]{:S(2)}, u32[]{:S(2)}) collective-permute-start(bf16[96,640]{1,0:T(8,128)(2,1)S(1)} %get-tuple-element.46), channel_id=1, source_target_pairs={{4,8},{12,16},{20,24},{8,4},{16,12},{24,20},{5,9},{13,17},{21,25},... | collective-permute-start | bytes 368648 | tf_op jit(solution)/shard_map/ppermute | solution.py:489
  75.9 0.5 courant_x.1.x_ref
  76.5 0.0 collective-permute-done.15.refs_1_
  76.5 0.0 collective-permute-done.16.refs_2_
  76.5 1.7 %collective-permute-done.17.refs_3_ = bf16[96,640]{1,0:T(8,128)(2,1)S(1)} collective-permute-done((bf16[96,640]{1,0:T(8,128)(2,1)S(1)}, bf16[96,640]{1,0:T(8,128)(2,1)S(1)}, u32[]{:S(2)}, u32[]{:S(2)}) %collective-permute-start.17) | collective-permute-done | bytes 122912 | tf_op jit(solution)/shard_map/ppermute | solution.py:482
  78.2 0.1 collective-permute-done.10.pair_ref
  78.3 3.0 %collective-permute-done.11.diagonal_ref = bf16[96,640]{1,0:T(8,128)(2,1)S(1)} collective-permute-done((bf16[96,640]{1,0:T(8,128)(2,1)S(1)}, bf16[96,640]{1,0:T(8,128)(2,1)S(1)}, u32[]{:S(2)}, u32[]{:S(2)}) %collective-permute-start.11) | collective-permute-done | bytes 122912 | tf_op jit(solution)/shard_map/ppermute | solution.py:489
  81.3 1.4 %first_step.1 = (f32[4,96,640]{2,1,0:T(8,128)S(1)}, f32[4,96,640]{2,1,0:T(8,128)S(1)}, bf16[96,640]{1,0:T(8,128)(2,1)S(1)}, bf16[96,640]{1,0:T(8,128)(2,1)S(1)}) custom-call(s32[1]{0:T(128)} %bitcast.odd_ref, f32[96,96]{1,0:T(8,128)S(1)} %copy.12.vertical_ref, f32[4,96,640]{2,1,0:T(8,128)S(1)} %get-tuple-element.44.tracer_ref, ...), custom_call_target="tpu_custom_call" | custom-call | flops 4000000 | bytes 4000000 | tf_op jit(solution)/shard_map/first_step/pallas_call | solution.py:468
  82.7 1.6 %collective-permute-start.18 = (bf16[96,640]{1,0:T(8,128)(2,1)S(1)}, bf16[96,640]{1,0:T(8,128)(2,1)S(1)}, u32[]{:S(2)}, u32[]{:S(2)}) collective-permute-start(bf16[96,640]{1,0:T(8,128)(2,1)S(1)} %get-tuple-element.56), channel_id=1, source_target_pairs={{0,4},{4,0},{8,12},{12,8},{16,20},{20,16},{24,28},{28,24},{1,5},{5... | collective-permute-start | bytes 368648 | tf_op jit(solution)/shard_map/ppermute | solution.py:490
  84.3 1.9 %collective-permute-start.19 = (bf16[96,640]{1,0:T(8,128)(2,1)S(1)}, bf16[96,640]{1,0:T(8,128)(2,1)S(1)}, u32[]{:S(2)}, u32[]{:S(2)}) collective-permute-start(bf16[96,640]{1,0:T(8,128)(2,1)S(1)} %get-tuple-element.57), channel_id=1, source_target_pairs={{4,8},{12,16},{20,24},{8,4},{16,12},{24,20},{5,9},{13,17},{21,25},... | collective-permute-start | bytes 368648 | tf_op jit(solution)/shard_map/ppermute | solution.py:489
  86.2 1.4 %collective-permute-done.18.pair_ref = bf16[96,640]{1,0:T(8,128)(2,1)S(1)} collective-permute-done((bf16[96,640]{1,0:T(8,128)(2,1)S(1)}, bf16[96,640]{1,0:T(8,128)(2,1)S(1)}, u32[]{:S(2)}, u32[]{:S(2)}) %collective-permute-start.18) | collective-permute-done | bytes 122912 | tf_op jit(solution)/shard_map/ppermute | solution.py:490
  87.7 4.3 %collective-permute-done.19.diagonal_ref = bf16[96,640]{1,0:T(8,128)(2,1)S(1)} collective-permute-done((bf16[96,640]{1,0:T(8,128)(2,1)S(1)}, bf16[96,640]{1,0:T(8,128)(2,1)S(1)}, u32[]{:S(2)}, u32[]{:S(2)}) %collective-permute-start.19) | collective-permute-done | bytes 122912 | tf_op jit(solution)/shard_map/ppermute | solution.py:489
  92.0 1.8 %second_step.1 = f32[96,4,512]{2,1,0:T(4,128)} custom-call(s32[1]{0:T(128)} %bitcast.odd_ref, f32[4,96,640]{2,1,0:T(8,128)S(1)} %get-tuple-element.55.tracer_ref, bf16[96,640]{1,0:T(8,128)(2,1)S(1)} %collective-permute-done.18.pair_ref, bf16[96,640]{1,0:T(8,128)(2,1)S(1)} %collective-permute-done.19.diagonal_ref, f32[4,96,640]{2,1,0:T(8,128)S(1)} %courant_x.1.x_ref, ...), custom_call_target="tpu_custom_call" | custom-call | flops 4000000 | bytes 4000000 | tf_op jit(solution)/shard_map/second_step/pallas_call | solution.py:468
  (9 shorter events, 0.0 us)
Async XLA Ops:
  0.0 2.2 %copy-start.2 = (bf16[128,1024,16]{1,2,0:T(8,128)(2,1)S(1)}, bf16[128,1024,16]{1,2,0:T(8,128)(2,1)}, u32[]{:S(2)}) copy-start(bf16[128,1024,16]{1,2,0:T(8,128)(2,1)} %param.5) | copy-start | bytes 12582916
  2.2 0.7 copy-start.3
  2.9 27.0 %copy-start.4 = (s32[1024]{0:T(1024)S(1)}, s32[1024]{0:T(1024)}, u32[]{:S(2)}) copy-start(s32[1024]{0:T(1024)} %numbers_ref.1) | copy-start | bytes 12292
  22.5 8.3 %collective-permute-start = (bf16[3,2,4,24,128]{4,3,2,1,0:T(8,128)(2,1)S(1)}, bf16[3,2,4,24,128]{4,3,2,1,0:T(8,128)(2,1)S(1)}, u32[]{:S(2)}, u32[]{:S(2)}) collective-permute-start(bf16[3,2,4,24,128]{4,3,2,1,0:T(8,128)(2,1)S(1)} %get-tuple-element.33), channel_id=1, source_target_pairs={{0,4},{4,0},{8,12},{12,8},{16,20},{20,16},{24,28},{28,24},{1,5},{5... | collective-permute-start | bytes 442376 | tf_op jit(solution)/shard_map/ppermute | solution.py:482
  24.0 9.5 %collective-permute-start.1 = (bf16[3,2,4,24,128]{4,3,2,1,0:T(8,128)(2,1)S(1)}, bf16[3,2,4,24,128]{4,3,2,1,0:T(8,128)(2,1)S(1)}, u32[]{:S(2)}, u32[]{:S(2)}) collective-permute-start(bf16[3,2,4,24,128]{4,3,2,1,0:T(8,128)(2,1)S(1)} %get-tuple-element.34), channel_id=1, source_target_pairs={{0,8},{4,12},{8,0},{12,4},{16,24},{20,28},{24,16},{28,20},{1,9},{5... | collective-permute-start | bytes 442376 | tf_op jit(solution)/shard_map/ppermute | solution.py:482
  25.6 11.9 %collective-permute-start.2 = (bf16[3,2,4,24,128]{4,3,2,1,0:T(8,128)(2,1)S(1)}, bf16[3,2,4,24,128]{4,3,2,1,0:T(8,128)(2,1)S(1)}, u32[]{:S(2)}, u32[]{:S(2)}) collective-permute-start(bf16[3,2,4,24,128]{4,3,2,1,0:T(8,128)(2,1)S(1)} %get-tuple-element.35), channel_id=1, source_target_pairs={{0,12},{4,8},{8,4},{12,0},{16,28},{20,24},{24,20},{28,16},{1,13},{... | collective-permute-start | bytes 442376 | tf_op jit(solution)/shard_map/ppermute | solution.py:482
  26.0 11.5 %collective-permute-start.3 = (bf16[3,2,4,24,128]{4,3,2,1,0:T(8,128)(2,1)S(1)}, bf16[3,2,4,24,128]{4,3,2,1,0:T(8,128)(2,1)S(1)}, u32[]{:S(2)}, u32[]{:S(2)}) collective-permute-start(bf16[3,2,4,24,128]{4,3,2,1,0:T(8,128)(2,1)S(1)} %get-tuple-element.36), channel_id=1, source_target_pairs={{0,16},{4,20},{8,24},{12,28},{16,0},{20,4},{24,8},{28,12},{1,17},{... | collective-permute-start | bytes 442376 | tf_op jit(solution)/shard_map/ppermute | solution.py:482
  26.1 20.3 %collective-permute-start.4 = (bf16[3,2,4,24,128]{4,3,2,1,0:T(8,128)(2,1)S(1)}, bf16[3,2,4,24,128]{4,3,2,1,0:T(8,128)(2,1)S(1)}, u32[]{:S(2)}, u32[]{:S(2)}) collective-permute-start(bf16[3,2,4,24,128]{4,3,2,1,0:T(8,128)(2,1)S(1)} %get-tuple-element.37), channel_id=1, source_target_pairs={{0,20},{4,16},{8,28},{12,24},{16,4},{20,0},{24,12},{28,8},{1,21},{... | collective-permute-start | bytes 442376 | tf_op jit(solution)/shard_map/ppermute | solution.py:482
  30.8 21.6 %collective-permute-start.5 = (bf16[3,2,4,24,128]{4,3,2,1,0:T(8,128)(2,1)S(1)}, bf16[3,2,4,24,128]{4,3,2,1,0:T(8,128)(2,1)S(1)}, u32[]{:S(2)}, u32[]{:S(2)}) collective-permute-start(bf16[3,2,4,24,128]{4,3,2,1,0:T(8,128)(2,1)S(1)} %get-tuple-element.38), channel_id=1, source_target_pairs={{0,24},{4,28},{8,16},{12,20},{16,8},{20,12},{24,0},{28,4},{1,25},{... | collective-permute-start | bytes 442376 | tf_op jit(solution)/shard_map/ppermute | solution.py:482
  33.5 21.4 %collective-permute-start.6 = (bf16[3,2,4,24,128]{4,3,2,1,0:T(8,128)(2,1)S(1)}, bf16[3,2,4,24,128]{4,3,2,1,0:T(8,128)(2,1)S(1)}, u32[]{:S(2)}, u32[]{:S(2)}) collective-permute-start(bf16[3,2,4,24,128]{4,3,2,1,0:T(8,128)(2,1)S(1)} %get-tuple-element.39), channel_id=1, source_target_pairs={{0,28},{4,24},{8,20},{12,16},{16,12},{20,8},{24,4},{28,0},{1,29},{... | collective-permute-start | bytes 442376 | tf_op jit(solution)/shard_map/ppermute | solution.py:482
  37.5 19.7 %copy-start = (bf16[8,2,128,1024]{3,2,1,0:T(8,128)(2,1)}, bf16[8,2,128,1024]{3,2,1,0:T(8,128)(2,1)S(1)}, u32[]{:S(2)}) copy-start(bf16[8,2,128,1024]{3,2,1,0:T(8,128)(2,1)S(1)} %twiddles.1.refs_9_) | copy-start | bytes 12582916
  54.9 6.3 %copy-start.5 = (f32[96,96]{1,0:T(8,128)S(1)}, f32[96,96]{1,0:T(8,128)}, u32[]{:S(2)}) copy-start(f32[96,96]{1,0:T(8,128)} %param.7) | copy-start | bytes 110596
  56.0 4.7 %collective-permute-start.7 = (bf16[96,640]{1,0:T(8,128)(2,1)S(1)}, bf16[96,640]{1,0:T(8,128)(2,1)S(1)}, u32[]{:S(2)}, u32[]{:S(2)}) collective-permute-start(bf16[96,640]{1,0:T(8,128)(2,1)S(1)} %get-tuple-element.41), channel_id=1, source_target_pairs={{0,1},{1,0},{2,3},{3,2},{4,5},{5,4},{6,7},{7,6},{8,9},{9,8},{10,11... | collective-permute-start | bytes 368648 | tf_op jit(solution)/shard_map/ppermute | solution.py:482
  57.1 15.1 %collective-permute-start.12 = (bf16[96,640]{1,0:T(8,128)(2,1)S(1)}, bf16[96,640]{1,0:T(8,128)(2,1)S(1)}, u32[]{:S(2)}, u32[]{:S(2)}) collective-permute-start(bf16[96,640]{1,0:T(8,128)(2,1)S(1)} %get-tuple-element.48), channel_id=1, source_target_pairs={{0,1},{1,0},{2,3},{3,2},{4,5},{5,4},{6,7},{7,6},{8,9},{9,8},{10,11... | collective-permute-start | bytes 368648 | tf_op jit(solution)/shard_map/ppermute | solution.py:482
  57.7 15.2 %collective-permute-start.13 = (bf16[96,640]{1,0:T(8,128)(2,1)S(1)}, bf16[96,640]{1,0:T(8,128)(2,1)S(1)}, u32[]{:S(2)}, u32[]{:S(2)}) collective-permute-start(bf16[96,640]{1,0:T(8,128)(2,1)S(1)} %get-tuple-element.49), channel_id=1, source_target_pairs={{0,2},{1,3},{2,0},{3,1},{4,6},{5,7},{6,4},{7,5},{8,10},{9,11},{10,... | collective-permute-start | bytes 368648 | tf_op jit(solution)/shard_map/ppermute | solution.py:482
  59.2 14.2 %collective-permute-start.14 = (bf16[96,640]{1,0:T(8,128)(2,1)S(1)}, bf16[96,640]{1,0:T(8,128)(2,1)S(1)}, u32[]{:S(2)}, u32[]{:S(2)}) collective-permute-start(bf16[96,640]{1,0:T(8,128)(2,1)S(1)} %get-tuple-element.50), channel_id=1, source_target_pairs={{0,3},{1,2},{2,1},{3,0},{4,7},{5,6},{6,5},{7,4},{8,11},{9,10},{10,... | collective-permute-start | bytes 368648 | tf_op jit(solution)/shard_map/ppermute | solution.py:482
  59.2 9.8 %collective-permute-start.8 = (bf16[96,640]{1,0:T(8,128)(2,1)S(1)}, bf16[96,640]{1,0:T(8,128)(2,1)S(1)}, u32[]{:S(2)}, u32[]{:S(2)}) collective-permute-start(bf16[96,640]{1,0:T(8,128)(2,1)S(1)} %get-tuple-element.42), channel_id=1, source_target_pairs={{0,2},{1,3},{2,0},{3,1},{4,6},{5,7},{6,4},{7,5},{8,10},{9,11},{10,... | collective-permute-start | bytes 368648 | tf_op jit(solution)/shard_map/ppermute | solution.py:482
  60.7 9.5 %collective-permute-start.9 = (bf16[96,640]{1,0:T(8,128)(2,1)S(1)}, bf16[96,640]{1,0:T(8,128)(2,1)S(1)}, u32[]{:S(2)}, u32[]{:S(2)}) collective-permute-start(bf16[96,640]{1,0:T(8,128)(2,1)S(1)} %get-tuple-element.43), channel_id=1, source_target_pairs={{0,3},{1,2},{2,1},{3,0},{4,7},{5,6},{6,5},{7,4},{8,11},{9,10},{10,... | collective-permute-start | bytes 368648 | tf_op jit(solution)/shard_map/ppermute | solution.py:482
  61.9 2.2 %copy-start.1 = (bf16[8,2,128,1024]{3,2,1,0:T(8,128)(2,1)S(1)}, bf16[8,2,128,1024]{3,2,1,0:T(8,128)(2,1)}, u32[]{:S(2)}) copy-start(bf16[8,2,128,1024]{3,2,1,0:T(8,128)(2,1)} %copy-done) | copy-start | bytes 12582916
  69.1 7.4 %collective-permute-start.15 = (bf16[96,640]{1,0:T(8,128)(2,1)S(1)}, bf16[96,640]{1,0:T(8,128)(2,1)S(1)}, u32[]{:S(2)}, u32[]{:S(2)}) collective-permute-start(bf16[96,640]{1,0:T(8,128)(2,1)S(1)} %get-tuple-element.52), channel_id=1, source_target_pairs={{0,1},{1,0},{2,3},{3,2},{4,5},{5,4},{6,7},{7,6},{8,9},{9,8},{10,11... | collective-permute-start | bytes 368648 | tf_op jit(solution)/shard_map/ppermute | solution.py:482
  70.1 6.4 %collective-permute-start.16 = (bf16[96,640]{1,0:T(8,128)(2,1)S(1)}, bf16[96,640]{1,0:T(8,128)(2,1)S(1)}, u32[]{:S(2)}, u32[]{:S(2)}) collective-permute-start(bf16[96,640]{1,0:T(8,128)(2,1)S(1)} %get-tuple-element.53), channel_id=1, source_target_pairs={{0,2},{1,3},{2,0},{3,1},{4,6},{5,7},{6,4},{7,5},{8,10},{9,11},{10,... | collective-permute-start | bytes 368648 | tf_op jit(solution)/shard_map/ppermute | solution.py:482
  72.3 5.9 %collective-permute-start.17 = (bf16[96,640]{1,0:T(8,128)(2,1)S(1)}, bf16[96,640]{1,0:T(8,128)(2,1)S(1)}, u32[]{:S(2)}, u32[]{:S(2)}) collective-permute-start(bf16[96,640]{1,0:T(8,128)(2,1)S(1)} %get-tuple-element.54), channel_id=1, source_target_pairs={{0,3},{1,2},{2,1},{3,0},{4,7},{5,6},{6,5},{7,4},{8,11},{9,10},{10,... | collective-permute-start | bytes 368648 | tf_op jit(solution)/shard_map/ppermute | solution.py:482
  72.9 5.4 %collective-permute-start.10 = (bf16[96,640]{1,0:T(8,128)(2,1)S(1)}, bf16[96,640]{1,0:T(8,128)(2,1)S(1)}, u32[]{:S(2)}, u32[]{:S(2)}) collective-permute-start(bf16[96,640]{1,0:T(8,128)(2,1)S(1)} %get-tuple-element.45), channel_id=1, source_target_pairs={{0,4},{4,0},{8,12},{12,8},{16,20},{20,16},{24,28},{28,24},{1,5},{5... | collective-permute-start | bytes 368648 | tf_op jit(solution)/shard_map/ppermute | solution.py:490
  73.4 7.9 %collective-permute-start.11 = (bf16[96,640]{1,0:T(8,128)(2,1)S(1)}, bf16[96,640]{1,0:T(8,128)(2,1)S(1)}, u32[]{:S(2)}, u32[]{:S(2)}) collective-permute-start(bf16[96,640]{1,0:T(8,128)(2,1)S(1)} %get-tuple-element.46), channel_id=1, source_target_pairs={{4,8},{12,16},{20,24},{8,4},{16,12},{24,20},{5,9},{13,17},{21,25},... | collective-permute-start | bytes 368648 | tf_op jit(solution)/shard_map/ppermute | solution.py:489
  82.7 4.9 %collective-permute-start.18 = (bf16[96,640]{1,0:T(8,128)(2,1)S(1)}, bf16[96,640]{1,0:T(8,128)(2,1)S(1)}, u32[]{:S(2)}, u32[]{:S(2)}) collective-permute-start(bf16[96,640]{1,0:T(8,128)(2,1)S(1)} %get-tuple-element.56), channel_id=1, source_target_pairs={{0,4},{4,0},{8,12},{12,8},{16,20},{20,16},{24,28},{28,24},{1,5},{5... | collective-permute-start | bytes 368648 | tf_op jit(solution)/shard_map/ppermute | solution.py:490
  84.3 7.7 %collective-permute-start.19 = (bf16[96,640]{1,0:T(8,128)(2,1)S(1)}, bf16[96,640]{1,0:T(8,128)(2,1)S(1)}, u32[]{:S(2)}, u32[]{:S(2)}) collective-permute-start(bf16[96,640]{1,0:T(8,128)(2,1)S(1)} %get-tuple-element.57), channel_id=1, source_target_pairs={{4,8},{12,16},{20,24},{8,4},{16,12},{24,20},{5,9},{13,17},{21,25},... | collective-permute-start | bytes 368648 | tf_op jit(solution)/shard_map/ppermute | solution.py:489

commit v3 on v2

v3 whole, which is shorter than its diff:
```python
import functools
import math

import jax
import jax.numpy as jnp
from jax import lax
from jax.experimental import pallas as pl
from jax.experimental.pallas import tpu as pltpu
from jax.sharding import PartitionSpec as P

NLON = 2048
FIELDS = 3
PARTS = 2
LANES = 128
CHUNK = 256
TILE = 256
PAIRS = 8
GROUP = 4
AHEAD = 2

courant_max = 0.45


def padded(block, sides, width, periodic):
    for axis, dim in sides:
        count = lax.axis_size(axis)
        forward = [(i, i + 1) for i in range(count - 1)]
        if periodic:
            forward.append((count - 1, 0))
        backward = [(target, source) for source, target in forward]
        low = lax.ppermute(
            lax.slice_in_dim(block, block.shape[dim] - width, None, axis=dim), axis, forward
        )
        high = lax.ppermute(lax.slice_in_dim(block, 0, width, axis=dim), axis, backward)
        block = jnp.concatenate([low, block, high], axis=dim)
    return block


def twiddles(numbers):
    longitude = jnp.arange(NLON, dtype=jnp.int32)
    residue = numbers[:, None] * longitude[None, :] % NLON
    angles = residue.astype(jnp.float32) * (2.0 * math.pi / NLON)
    weight = jnp.where(numbers == 0, 1.0, 2.0).astype(jnp.float32)[:, None]
    return jnp.stack([weight * jnp.cos(angles), -weight * jnp.sin(angles)]).astype(jnp.bfloat16)


def parity_columns(coefficient, degree, lengths):
    counted = degree < lengths[:, None]
    even_mask = counted & (degree % 2 == 0)
    odd_mask = counted & (degree % 2 == 1)
    return jnp.concatenate(
        [
            jnp.where(even_mask[:, :, None], coefficient, 0),
            jnp.where(odd_mask[:, :, None], coefficient, 0),
        ],
        axis=2,
    )


def padded_sums(coefficient, basis, own_numbers):
    degree_count = coefficient.shape[1]
    degree = jnp.arange(degree_count, dtype=jnp.int32)[None, :]
    masked = parity_columns(coefficient, degree, degree_count - own_numbers)
    return jnp.einsum("skc,ski->sci", masked, basis, preferred_element_type=jnp.float32)


def upwind_core(extended, courant_x, courant_y):
    center = extended[:, 1:-1, 1:-1]
    western = extended[:, 1:-1, :-2]
    eastern = extended[:, 1:-1, 2:]
    northern = extended[:, :-2, 1:-1]
    southern = extended[:, 2:, 1:-1]
    return (
        center
        - jnp.maximum(courant_x, 0.0) * (center - western)
        - jnp.minimum(courant_x, 0.0) * (eastern - center)
        - jnp.maximum(courant_y, 0.0) * (center - northern)
        - jnp.minimum(courant_y, 0.0) * (southern - center)
    )


def plain_body(spectrum, legendre, wave_numbers, vertical):
    slot_count, degree_count, level_count, part_count = spectrum.shape
    columns = level_count * part_count
    coefficient = spectrum.reshape(slot_count, degree_count, columns)
    first_slot = lax.axis_index("wave") * slot_count
    own_numbers = lax.dynamic_slice_in_dim(wave_numbers, first_slot, slot_count)
    partial_sums = padded_sums(coefficient, legendre, own_numbers)
    even_sums = partial_sums[:, :columns]
    odd_sums = partial_sums[:, columns:]
    northern = even_sums + odd_sums
    southern = jnp.flip(even_sums - odd_sums, axis=2)
    fourier = jnp.concatenate([northern, southern], axis=2).astype(jnp.bfloat16)
    received = lax.all_to_all(fourier, "wave", split_axis=2, concat_axis=0, tiled=True)
    lat_count = received.shape[2]
    received = received.reshape(received.shape[0], level_count, FIELDS, PARTS, lat_count)
    twiddle = twiddles(wave_numbers)
    grid_values = jnp.einsum(
        "smfrl,rsj->lmfj", received, twiddle, preferred_element_type=jnp.float32
    ).astype(jnp.bfloat16)
    column_values = lax.all_to_all(grid_values, "lev", split_axis=3, concat_axis=1, tiled=True)
    fields = jnp.einsum(
        "vm,lmfj->fvlj",
        vertical,
        column_values.astype(jnp.float32),
        precision=lax.Precision.HIGHEST,
    )
    courant_x = courant_max * jnp.tanh(fields[0])
    courant_y = courant_max * jnp.tanh(fields[1])
    tracer = fields[2]
    for sweep in range(2):
        extended = padded(tracer, (("wave", 1),), 1, False)
        extended = padded(extended, (("lev", 2),), 1, True)
        tracer = upwind_core(extended, courant_x, courant_y)
    return tracer


def vmem():
    return pl.BlockSpec(memory_space=pltpu.VMEM)


def cost(flops, count_bytes):
    return pl.CostEstimate(flops=flops, bytes_accessed=count_bytes, transcendentals=0)


def legendre_kernel(numbers_ref, place_ref, spectrum_ref, legendre_ref, *refs):
    outs, (held, basis_held, order, sums, arrived) = refs[:-5], refs[-5:]
    waves = len(outs)
    _, _, lats, modes, _ = outs[0].shape
    buffers, pairs, rows, _ = held.shape
    slots, half, degrees = legendre_ref.shape
    chunks = degrees // CHUNK + 1
    steps = slots // (2 * pairs)
    ahead = buffers - 1
    place = place_ref[0]
    many = 2 * GROUP

    def plan(index):
        first = degrees - numbers_ref[place * slots + 2 * index]
        second = degrees - numbers_ref[place * slots + 2 * index + 1]
        return first, second, lax.shift_right_logical(first + (CHUNK - 1), CHUNK.bit_length() - 1)

    def fetch(group, slot):
        pltpu.make_async_copy(
            legendre_ref.at[pl.ds(group * 2 * pairs, 2 * pairs)],
            basis_held.at[slot],
            arrived.at[slot],
        ).start()
        for pair in range(pairs):
            index = group * pairs + pair
            _, _, edge = plan(index)
            for t in range(chunks):
                inside = t < edge
                source = jnp.where(inside, 2 * index, 2 * index + 1)
                block = jnp.where(inside, t, t - edge)
                start = pl.multiple_of(block * CHUNK, CHUNK)
                pltpu.make_async_copy(
                    spectrum_ref.at[source, :, pl.ds(start, CHUNK)],
                    held.at[slot, pair, :, pl.ds(t * CHUNK, CHUNK)],
                    arrived.at[slot],
                ).start()

    for group in range(min(ahead, steps)):
        fetch(group, group)

    row = lax.broadcasted_iota(jnp.int32, order.shape, 0)
    column = lax.broadcasted_iota(jnp.int32, order.shape, 1)
    wanted = lax.rem(row, many) * (2 * half) + lax.div(row, many)
    order[...] = jnp.where(column == wanted, 1.0, 0.0).astype(jnp.bfloat16)

    def work(step, fetches):
        now = lax.rem(step, buffers)
        for buffer in (held, basis_held):
            pltpu.make_async_copy(buffer.at[now], buffer.at[now], arrived.at[now]).wait()
        if fetches:
            fetch(step + ahead, lax.rem(step + ahead, buffers))
        lane = lax.broadcasted_iota(jnp.int32, (half, CHUNK), 1)
        sign = jnp.where(lane % 2 == 0, 1.0, -1.0)
        results = []
        for pair in range(pairs):
            index = step * pairs + pair
            first, second, edge = plan(index)
            columns = []
            for t in range(chunks):
                inside = t < edge
                local = jnp.where(inside, 2 * pair, 2 * pair + 1)
                block = jnp.where(inside, t, t - edge)
                start = pl.multiple_of(block * CHUNK, CHUNK)
                length = jnp.where(inside, first, second) - start
                values = basis_held[now, local, :, pl.ds(start, CHUNK)].astype(jnp.float32)
                values = jnp.where(lane < length, values, 0.0)
                north_first = values * jnp.where(inside, 1.0, 0.0)
                north_second = values - north_first
                parts = [north_first, north_first * sign, north_second, north_second * sign]
                columns.append(jnp.concatenate(parts, axis=0).astype(jnp.bfloat16))
            result = lax.dot_general(
                jnp.concatenate(columns, axis=1),
                held[now, pair],
                (((1,), (1,)), ((), ())),
                preferred_element_type=jnp.float32,
            )
            results.append(result.astype(jnp.bfloat16))
            if len(results) == GROUP:
                slot = pl.multiple_of(2 * (index - (GROUP - 1)), many)
                ordered = jnp.dot(
                    order[...], jnp.concatenate(results, axis=0), preferred_element_type=jnp.float32
                )
                results = []
                for low in range(0, rows, LANES):
                    width = min(LANES, rows - low)
                    part = ordered[:, low : low + width].reshape(2 * half, many, width)
                    sums[low // LANES, :, pl.ds(slot, many), :width] = part

    lax.fori_loop(0, steps - ahead, lambda step, _: work(step, True), None)
    lax.fori_loop(steps - ahead, steps, lambda step, _: work(step, False), None)

    for d in range(waves):
        for l in range(lats):
            lat = (place ^ d) * lats + l
            row = jnp.where(lat < half, lat, 3 * half - 1 - lat)
            turned = [
                sums[low // LANES, row].T.astype(jnp.bfloat16) for low in range(0, rows, LANES)
            ]
            whole = jnp.concatenate(turned, axis=0)
            for f in range(FIELDS):
                for p in range(PARTS):
                    base = (f * PARTS + p) * modes
                    outs[d][f, p, l] = whole[base : base + modes]


def legendre_stage(spectrum, legendre, numbers, place, waves):
    slots, degrees, modes, _ = spectrum.shape
    half = legendre.shape[2]
    lats = 2 * half // waves
    rows = modes * FIELDS * PARTS
    turned = jnp.transpose(spectrum, (0, 3, 2, 1)).reshape(slots, rows, degrees)
    basis = jnp.transpose(legendre, (0, 2, 1))
    chunks = degrees // CHUNK + 1
    tiles = -(-rows // LANES)
    smem = pl.BlockSpec(memory_space=pltpu.SMEM)
    away = pl.BlockSpec(memory_space=pl.ANY)
    return pl.pallas_call(
        legendre_kernel,
        out_shape=[jax.ShapeDtypeStruct((FIELDS, PARTS, lats, modes, slots), jnp.bfloat16)] * waves,
        in_specs=[smem, smem, away, away],
        out_specs=[vmem()] * waves,
        scratch_shapes=[
            pltpu.VMEM((AHEAD + 1, PAIRS, rows, chunks * CHUNK), jnp.bfloat16),
            pltpu.VMEM((AHEAD + 1, 2 * PAIRS, half, degrees), jnp.bfloat16),
            pltpu.VMEM((GROUP * 4 * half, GROUP * 4 * half), jnp.bfloat16),
            pltpu.VMEM((tiles, 2 * half, slots, LANES), jnp.float32),
            pltpu.SemaphoreType.DMA((AHEAD + 1,)),
        ],
        compiler_params=pltpu.CompilerParams(vmem_limit_bytes=58 << 20),
        cost_estimate=cost(slots * rows * degrees * 2 * half, slots * rows * degrees),
        name="legendre_sums",
    )(numbers, place, turned, basis)


def twiddle_kernel(place_ref, low_cos_ref, low_sin_ref, turn_cos_ref, turn_sin_ref, out_ref):
    slots = low_cos_ref.shape[1]
    shape = (LANES, slots)
    turn_cos = jnp.broadcast_to(turn_cos_ref[0], shape).T
    turn_sin = jnp.broadcast_to(turn_sin_ref[0], shape).T
    cos, sin = low_cos_ref[0], low_sin_ref[0]
    for block in range(out_ref.shape[3] // LANES):
        lanes = pl.ds(block * LANES, LANES)
        out_ref[0, 0, :, lanes] = cos.astype(jnp.bfloat16)
        out_ref[0, 1, :, lanes] = (-sin).astype(jnp.bfloat16)
        cos, sin = cos * turn_cos - sin * turn_sin, sin * turn_cos + cos * turn_sin


def twiddle_stage(numbers, place):
    waves, slots = numbers.shape
    count = NLON // 2

    def angles(residue):
        return (residue % NLON).astype(jnp.float32) * (2.0 * math.pi / NLON)

    low = angles(numbers[:, :, None] * jnp.arange(LANES, dtype=jnp.int32)[None, None, :])
    turn = angles(numbers * LANES)[:, None, :]
    weight = jnp.where(numbers == 0, 1.0, 2.0).astype(jnp.float32)[:, :, None]

    def spec(rows, last):
        return pl.BlockSpec((1, rows, last), lambda i, place_ref: (place_ref[0] ^ i, 0, 0))

    return pl.pallas_call(
        twiddle_kernel,
        out_shape=jax.ShapeDtypeStruct((waves, PARTS, slots, count), jnp.bfloat16),
        grid_spec=pltpu.PrefetchScalarGridSpec(
            num_scalar_prefetch=1,
            grid=(waves,),
            in_specs=[spec(slots, LANES), spec(slots, LANES), spec(1, slots), spec(1, slots)],
            out_specs=pl.BlockSpec((1, PARTS, slots, count), lambda i, _: (i, 0, 0, 0)),
        ),
        compiler_params=pltpu.CompilerParams(vmem_limit_bytes=8 << 20),
        cost_estimate=cost(8 * waves * slots * count, 4 * waves * slots * count),
        name="twiddles",
    )(place, weight * jnp.cos(low), weight * jnp.sin(low), jnp.cos(turn), jnp.sin(turn))


def synthesis_kernel(waves, levs, fields, wave_ref, lev_ref, *refs):
    blocks, (sign_ref, twiddle_ref) = refs[:waves], refs[waves : waves + 2]
    outs, (left, grid) = refs[waves + 2 : -2], refs[-2:]
    _, _, lats, modes, slots = blocks[0].shape
    each = lats * modes
    rows = each * len(fields)
    for d in range(waves):
        sign = sign_ref[wave_ref[0] ^ d]
        for p in range(PARTS):
            lanes = pl.ds((d * PARTS + p) * slots, slots)
            for place, field in enumerate(fields):
                values = blocks[d][field, p].reshape(each, slots)
                left[place * each : (place + 1) * each, lanes] = values
                left[rows + place * each : rows + (place + 1) * each, lanes] = values * sign

    width = NLON // levs
    ratio = width // TILE
    steps = twiddle_ref.shape[3] // TILE
    lane = lax.broadcasted_iota(jnp.int32, (rows, LANES), 1)
    for step in range(steps):
        right = twiddle_ref[:, :, :, pl.ds(step * TILE, TILE)]
        right = right.reshape(waves * PARTS * slots, TILE)
        result = jnp.dot(left[...], right, preferred_element_type=jnp.float32)
        result = result.astype(jnp.bfloat16)
        for which in range(2):
            owner, inner = divmod(step + which * steps, ratio)
            grid[owner, :, pl.ds(inner * TILE, TILE)] = result[which * rows : (which + 1) * rows]
    for owner in range(levs):
        grid[owner, :, pl.ds(width, LANES)] = jnp.where(
            lane < LANES // 2,
            grid[(owner + 1) % levs, :, :LANES],
            grid[(owner - 1) % levs, :, pl.ds(width - LANES, LANES)],
        )
    place = lev_ref[0]
    for e in range(levs):
        outs[e][...] = grid[place ^ e]


def synthesis_stage(blocks, sign, twiddle, wave_place, lev_place, levs, fields):
    waves, _, slots, count = twiddle.shape
    _, _, lats, modes, _ = blocks[0].shape
    rows = lats * modes * len(fields)
    width = NLON // levs + LANES
    depth = waves * PARTS * slots
    return pl.pallas_call(
        functools.partial(synthesis_kernel, waves, levs, fields),
        out_shape=[jax.ShapeDtypeStruct((rows, width), jnp.bfloat16)] * levs,
        in_specs=[pl.BlockSpec(memory_space=pltpu.SMEM)] * 2 + [vmem()] * (waves + 2),
        out_specs=[vmem()] * levs,
        scratch_shapes=[
            pltpu.VMEM((2 * rows, depth), jnp.bfloat16),
            pltpu.VMEM((levs, rows, width), jnp.bfloat16),
        ],
        compiler_params=pltpu.CompilerParams(vmem_limit_bytes=12 << 20),
        cost_estimate=cost(4 * rows * depth * count, 2 * depth * count),
        name="synthesis",
    )(wave_place, lev_place, *blocks, sign, twiddle)


def three_terms(matrix):
    high = matrix.astype(jnp.bfloat16)
    rest = matrix - high.astype(jnp.float32)
    middle = rest.astype(jnp.bfloat16)
    low = (rest - middle.astype(jnp.float32)).astype(jnp.bfloat16)
    return jnp.concatenate([high, middle, low], axis=0)


def levels_of(terms, place, blocks, gathered, base, modes):
    count = terms.shape[0] // 3
    for e, block in enumerate(blocks):
        start = pl.multiple_of((place ^ e) * modes, modes)
        gathered[pl.ds(start, modes)] = block[base : base + modes].astype(jnp.float32)
    rows = gathered[...].astype(jnp.bfloat16)
    result = jnp.dot(terms, rows, preferred_element_type=jnp.float32)
    return result[:count] + (result[count : 2 * count] + result[2 * count :])


def keep_edges(lat, lats, values, odd, pair_ref, diagonal_ref):
    edge = values.astype(jnp.bfloat16)
    if 0 < lat < lats - 1:
        return
    takes_pair = 1 if lat == 0 else 0

    @pl.when(odd == takes_pair)
    def _():
        pair_ref[...] = edge

    @pl.when(odd != takes_pair)
    def _():
        diagonal_ref[...] = edge


def tracer_kernel(modes, odd_ref, lev_ref, vertical_ref, *refs):
    blocks, (field_ref, pair_ref, diagonal_ref, gathered) = refs[:-4], refs[-4:]
    terms = three_terms(vertical_ref[...])
    lats = field_ref.shape[0]
    for lat in range(lats):
        values = levels_of(terms, lev_ref[0], blocks, gathered, lat * modes, modes)
        field_ref[lat] = values
        keep_edges(lat, lats, values, odd_ref[0], pair_ref, diagonal_ref)


def upwind(center, western, eastern, northern, southern, courant_x, courant_y):
    return (
        center
        - jnp.maximum(courant_x, 0.0) * (center - western)
        - jnp.minimum(courant_x, 0.0) * (eastern - center)
        - jnp.maximum(courant_y, 0.0) * (center - northern)
        - jnp.minimum(courant_y, 0.0) * (southern - center)
    )


def stepped(lat, odd_ref, end_ref, tracer_ref, pair_ref, diagonal_ref, courant_x, courant_y):
    lats, _, width = tracer_ref.shape
    center = tracer_ref[lat]

    def outside(takes_pair):
        pair = pair_ref[...].astype(jnp.float32)
        diagonal = jnp.where(end_ref[0] == 1, 0.0, diagonal_ref[...].astype(jnp.float32))
        return jnp.where(odd_ref[0] == takes_pair, pair, diagonal)

    northern = tracer_ref[lat - 1] if lat > 0 else outside(1)
    southern = tracer_ref[lat + 1] if lat < lats - 1 else outside(0)
    return upwind(
        center,
        pltpu.roll(center, 1, 1),
        pltpu.roll(center, width - 1, 1),
        northern,
        southern,
        courant_x,
        courant_y,
    )


def first_step_kernel(
    modes, odd_ref, end_ref, lev_ref, vertical_ref, tracer_ref, pair_ref, diagonal_ref, *refs
):
    blocks, (x_ref, y_ref, out_ref, next_pair_ref, next_diagonal_ref, gathered) = refs[:-6], refs[-6:]
    terms = three_terms(vertical_ref[...])
    lats = tracer_ref.shape[0]

    def courant(field, lat):
        base = (field * lats + lat) * modes
        velocity = levels_of(terms, lev_ref[0], blocks, gathered.at[field], base, modes)
        return courant_max * jnp.tanh(velocity)

    for lat in (0, lats - 1, *range(1, lats - 1)):
        courant_x, courant_y = courant(0, lat), courant(1, lat)
        x_ref[lat] = courant_x
        y_ref[lat] = courant_y
        values = stepped(
            lat, odd_ref, end_ref, tracer_ref, pair_ref, diagonal_ref, courant_x, courant_y
        )
        out_ref[lat] = values
        keep_edges(lat, lats, values, odd_ref[0], next_pair_ref, next_diagonal_ref)


def second_step_kernel(odd_ref, end_ref, tracer_ref, pair_ref, diagonal_ref, x_ref, y_ref, out_ref):
    width = out_ref.shape[2]
    for lat in range(tracer_ref.shape[0]):
        values = stepped(
            lat, odd_ref, end_ref, tracer_ref, pair_ref, diagonal_ref, x_ref[lat], y_ref[lat]
        )
        out_ref[:, lat, :] = values[:, :width]


def local_call(kernel, outs, scratch, name, *operands):
    smem = pl.BlockSpec(memory_space=pltpu.SMEM)
    return pl.pallas_call(
        kernel,
        out_shape=outs,
        in_specs=[smem if operand.dtype == jnp.int32 else vmem() for operand in operands],
        out_specs=jax.tree.map(lambda _: vmem(), outs),
        scratch_shapes=scratch,
        compiler_params=pltpu.CompilerParams(vmem_limit_bytes=16 << 20),
        cost_estimate=cost(4_000_000, 4_000_000),
        name=name,
    )(*operands)


def exchange(blocks, axis):
    count = lax.axis_size(axis)
    return [blocks[0]] + [
        lax.ppermute(blocks[d], axis, [(i, i ^ d) for i in range(count)]) for d in range(1, count)
    ]


def edges(pair, diagonal):
    count = lax.axis_size("wave")
    steps = [(i, i + 1) for i in range(1, count - 1, 2)] + [(0, 0)]
    steps = steps + [(b, a) for a, b in steps[:-1]] + [(count - 1, count - 1)]
    diagonal = lax.ppermute(diagonal, "wave", steps)
    pair = lax.ppermute(pair, "wave", [(i, i ^ 1) for i in range(count)])
    return pair, diagonal


def tiled_body(spectrum, legendre, wave_numbers, vertical):
    waves, levs = lax.axis_size("wave"), lax.axis_size("lev")
    slots, degrees, modes, _ = spectrum.shape
    levels = vertical.shape[0]
    lats = 2 * legendre.shape[2] // waves
    width = NLON // levs
    wave_place, lev_place = lax.axis_index("wave"), lax.axis_index("lev")
    at_end = (wave_place == 0) | (wave_place == waves - 1)
    odd, at_end = lax.rem(wave_place, 2)[None], at_end.astype(jnp.int32)[None]
    wave_place, lev_place = wave_place[None], lev_place[None]

    fourier = legendre_stage(spectrum, legendre, wave_numbers, wave_place, waves)
    by_wave = wave_numbers.reshape(waves, slots)
    sign = jnp.where(by_wave % 2 == 0, 1.0, -1.0).astype(jnp.bfloat16)[:, None, :]
    twiddle = twiddle_stage(by_wave, wave_place)
    received = exchange(fourier, "wave")
    columns = [
        exchange(
            synthesis_stage(received, sign, twiddle, wave_place, lev_place, levs, fields), "lev"
        )
        for fields in ((2,), (0, 1))
    ]

    whole = jax.ShapeDtypeStruct((lats, levels, width + LANES), jnp.float32)
    row = jax.ShapeDtypeStruct((levels, width + LANES), jnp.bfloat16)
    gathered = (levs * modes, width + LANES)
    tracer, pair, diagonal = local_call(
        functools.partial(tracer_kernel, modes),
        (whole, row, row),
        [pltpu.VMEM(gathered, jnp.float32)],
        "tracer",
        odd,
        lev_place,
        vertical,
        *columns[0],
    )
    pair, diagonal = edges(pair, diagonal)
    courant_x, courant_y, tracer, next_pair, next_diagonal = local_call(
        functools.partial(first_step_kernel, modes),
        (whole, whole, whole, row, row),
        [pltpu.VMEM((2, *gathered), jnp.float32)],
        "first_step",
        odd,
        at_end,
        lev_place,
        vertical,
        tracer,
        pair,
        diagonal,
        *columns[1],
    )
    pair, diagonal = edges(next_pair, next_diagonal)
    return local_call(
        second_step_kernel,
        jax.ShapeDtypeStruct((levels, lats, width), jnp.float32),
        [],
        "second_step",
        odd,
        at_end,
        tracer,
        pair,
        diagonal,
        courant_x,
        courant_y,
    )


def body(spectrum, legendre, wave_numbers, vertical):
    waves, levs = lax.axis_size("wave"), lax.axis_size("lev")
    slots, degrees, modes, _ = spectrum.shape
    tiled = (
        slots % LANES == 0
        and slots % (2 * PAIRS) == 0
        and slots > 2 * PAIRS * AHEAD
        and legendre.shape[2] % 16 == 0
        and modes % 8 == 0
        and degrees % CHUNK == 0
        and waves & (waves - 1) == 0
        and levs & (levs - 1) == 0
        and NLON // levs % TILE == 0
        and levs % 2 == 0
        and 2 * legendre.shape[2] // waves >= 2
    )
    form = tiled_body if tiled else plain_body
    return form(spectrum, legendre, wave_numbers, vertical)


def solution(mesh):
    in_specs = (P("wave", None, "lev", None), P("wave", None, None), P(), P())
    out_specs = P(None, "wave", "lev")
    return jax.shard_map(body, mesh=mesh, in_specs=in_specs, out_specs=out_specs, check_vma=False)
```

time: 94.8 us -> 81.1 us (0.86)
  local copies, waits for them, and re-layouts: 6.47 us -> 0.14 us
  Pallas kernels: 29 us -> 25.4 us
  starting transfers between devices: 20.6 us -> 18 us
    unnamed x13 -> x6, local copies, waits for them, and re-layouts: 5.15 us -> 0.02 us
    ppermute x2, waiting for transfers between devices: 7.32 us -> 3.22 us  [edges(): diagonal = lax.ppermute(diagonal, 'wave', steps)]
    pallas_call x4 -> x3, Pallas kernels: 22.8 us -> 19.3 us  [the longest x1 16.2 us: legendre_stage(): pl.pallas_call(legendre_kernel, out_shape=[jax.ShapeDtypeStruct((FIELDS,...]
    ppermute x16 -> x13, waiting for transfers between devices: 26.3 us -> 29 us  [exchange(): lax.ppermute(blocks[d], axis, [(i, i ^ d) for i in range(count)])]
    ppermute x16 -> x13, starting transfers between devices: 14.1 us -> 11.8 us  [exchange(): lax.ppermute(blocks[d], axis, [(i, i ^ d) for i in range(count)])]
    gather x2 -> x0, local copies, waits for them, and re-layouts: 1.11 us -> none  [the longest x1 0.56 us: tiled_body(): vertical.reshape(levels, levs, modes)[:, lev_place ^ jnp.arange(levs)]]
    ppermute x2, waiting for transfers between devices: 1.53 us -> 2.56 us  [edges(): pair = lax.ppermute(pair, 'wave', [(i, i ^ 1) for i in range(count)])]
    pallas_call x4 -> x3, Pallas kernels: 4.47 us -> 4.31 us  [local_call(): pl.pallas_call(kernel, out_shape=outs, in_specs=[smem if operand.dtype ==...]
  transfers between devices with their start and end apart: 20 -> 17, of which waited for: 11 -> 10; matrix products, arithmetic and copies ran while one was open for 4% -> 3% of each run, Pallas kernels for 6% -> 6%
where the time goes in v3:
time: 81.1 us; the launch traced here: 80.9 us
  waiting for transfers between devices  34.8 us (43%)
  Pallas kernels  25.4 us (31%)
  starting transfers between devices  18 us (22%)
  other arithmetic  2.3 us (3%)
    ppermute x13, waiting for transfers between devices, exchange(): lax.ppermute(blocks[d], axis, [(i, i ^ d) for i in range(count)])  29 us
    pallas_call x1, Pallas kernels, legendre_stage(): pl.pallas_call(legendre_kernel, out_shape=[jax.ShapeDtypeStruct((FIELDS,...  16.2 us
    ppermute x13, starting transfers between devices, exchange(): lax.ppermute(blocks[d], axis, [(i, i ^ d) for i in range(count)])  11.8 us
    ppermute x2, starting transfers between devices, edges(): diagonal = lax.ppermute(diagonal, 'wave', steps)  4.58 us
    pallas_call x3, Pallas kernels, local_call(): pl.pallas_call(kernel, out_shape=outs, in_specs=[smem if operand.dtype ==...  4.31 us
    ppermute x2, waiting for transfers between devices, edges(): diagonal = lax.ppermute(diagonal, 'wave', steps)  3.22 us
    pallas_call x2, Pallas kernels, synthesis_stage(): pl.pallas_call(functools.partial(synthesis_kernel, waves, levs, fields),...  3.07 us
    ppermute x2, waiting for transfers between devices, edges(): pair = lax.ppermute(pair, 'wave', [(i, i ^ 1) for i in range(count)])  2.56 us
  transfers between devices with their start and end apart: 17, of which 10 were waited for; matrix products, arithmetic and copies ran while one was open for 3% of the time, Pallas kernels for 6%

profile of v3, /device:TPU:16, one launch (start us, length us, event | category | flops | bytes accessed | tf_op | source)
XLA Modules:
  0.0 80.9 jit_solution(8059781623004123270)
XLA Ops:
  0.0 0.0 copy-start.2
  0.0 16.2 %legendre_sums.1 = (bf16[3,2,4,24,128]{4,3,2,1,0:T(8,128)(2,1)}, bf16[3,2,4,24,128]{4,3,2,1,0:T(8,128)(2,1)}, bf16[3,2,4,24,128]{4,3,2,1,0:T(8,128)(2,1)}, bf16[...) custom-call(s32[1024]{0:T(1024)} %numbers_ref.1, ...), custom_call_target="tpu_custom_call" | custom-call | flops 603979776 | bytes 18874368 | tf_op jit(solution)/shard_map/legendre_sums/pallas_call | solution.py:242
  16.2 0.0 copy-start.1
  16.2 1.5 %collective-permute-start = (bf16[3,2,4,24,128]{4,3,2,1,0:T(8,128)(2,1)}, bf16[3,2,4,24,128]{4,3,2,1,0:T(8,128)(2,1)S(1)}, u32[]{:S(2)}, u32[]{:S(2)}) collective-permute-start(bf16[3,2,4,24,128]{4,3,2,1,0:T(8,128)(2,1)} %get-tuple-element.30), channel_id=1, source_target_pairs={{0,4},{4,0},{8,12},{12,8},{16,20},{20,16},{24,28},{28,24},{1,5},{5... | collective-permute-start | bytes 442376 | tf_op jit(solution)/shard_map/ppermute | solution.py:485
  17.8 1.6 %collective-permute-start.1 = (bf16[3,2,4,24,128]{4,3,2,1,0:T(8,128)(2,1)}, bf16[3,2,4,24,128]{4,3,2,1,0:T(8,128)(2,1)S(1)}, u32[]{:S(2)}, u32[]{:S(2)}) collective-permute-start(bf16[3,2,4,24,128]{4,3,2,1,0:T(8,128)(2,1)} %get-tuple-element.31), channel_id=1, source_target_pairs={{0,8},{4,12},{8,0},{12,4},{16,24},{20,28},{24,16},{28,20},{1,9},{5... | collective-permute-start | bytes 442376 | tf_op jit(solution)/shard_map/ppermute | solution.py:485
  19.4 0.4 collective-permute-start.2
  19.8 0.0 collective-permute-start.3
  19.8 3.8 %collective-permute-start.4 = (bf16[3,2,4,24,128]{4,3,2,1,0:T(8,128)(2,1)}, bf16[3,2,4,24,128]{4,3,2,1,0:T(8,128)(2,1)S(1)}, u32[]{:S(2)}, u32[]{:S(2)}) collective-permute-start(bf16[3,2,4,24,128]{4,3,2,1,0:T(8,128)(2,1)} %get-tuple-element.34), channel_id=1, source_target_pairs={{0,20},{4,16},{8,28},{12,24},{16,4},{20,0},{24,12},{28,8},{1,21},{... | collective-permute-start | bytes 442376 | tf_op jit(solution)/shard_map/ppermute | solution.py:485
  23.6 0.0 copy-done.2
  23.7 0.2 fusion.11
  23.8 0.1 cos.7.turn_cos_ref
  23.9 0.0 collective-permute-done.refs_1_
  24.0 0.5 collective-permute-start.5
  24.5 3.1 %collective-permute-done.1.refs_2_ = bf16[3,2,4,24,128]{4,3,2,1,0:T(8,128)(2,1)S(1)} collective-permute-done((bf16[3,2,4,24,128]{4,3,2,1,0:T(8,128)(2,1)}, bf16[3,2,4,24,128]{4,3,2,1,0:T(8,128)(2,1)S(1)}, u32[]{:S(2)}, u32[]{:S(2)}) %collective-permute-start.1) | collective-permute-done | bytes 147488 | tf_op jit(solution)/shard_map/ppermute | solution.py:485
  27.6 0.0 collective-permute-start.6
  27.6 2.1 %sine_multiply_fusion = (f32[8,128,128]{2,1,0:T(8,128)S(1)}, f32[8,128,128]{2,1,0:T(8,128)S(1)}) fusion(s32[8,128]{1,0:T(8,128)S(1)} %bitcast.14, f32[8,128]{1,0:T(8,128)S(1)} %compare_select_fusion.5), kind=kLoop, calls=%fused_computation.6 | loop fusion | flops 2097152 | bytes 1056768 | tf_op jit(solution)/shard_map/mul | solution.py:299
  29.8 1.8 %twiddles.1.refs_9_ = bf16[8,2,128,1024]{3,2,1,0:T(8,128)(2,1)S(1)} custom-call(s32[1]{0:T(128)} %bitcast.3.place_ref.wave_ref, f32[8,128,128]{2,1,0:T(8,128)S(1)} %get-tuple-element.56.low_cos_ref, f32[8,128,128]{2,1,0:T(8,128)S(1)} %get-tuple-element.55.low_sin_ref, f32[8,1,128]{2,1,0:T(1,128)S(1)} %cos.7.turn_cos_ref, ...), custom_call_target="tpu_custom_call" | custom-call | flops 8388608 | bytes 4194304 | tf_op jit(solution)/shard_map/twiddles/pallas_call | solution.py:287
  31.6 0.0 collective-permute-done.2.refs_3_
  31.6 0.0 collective-permute-done.3.refs_4_
  31.6 8.8 %collective-permute-done.4.refs_5_ = bf16[3,2,4,24,128]{4,3,2,1,0:T(8,128)(2,1)S(1)} collective-permute-done((bf16[3,2,4,24,128]{4,3,2,1,0:T(8,128)(2,1)}, bf16[3,2,4,24,128]{4,3,2,1,0:T(8,128)(2,1)S(1)}, u32[]{:S(2)}, u32[]{:S(2)}) %collective-permute-start.4) | collective-permute-done | bytes 147488 | tf_op jit(solution)/shard_map/ppermute | solution.py:485
  40.4 6.0 %collective-permute-done.5.refs_6_ = bf16[3,2,4,24,128]{4,3,2,1,0:T(8,128)(2,1)S(1)} collective-permute-done((bf16[3,2,4,24,128]{4,3,2,1,0:T(8,128)(2,1)}, bf16[3,2,4,24,128]{4,3,2,1,0:T(8,128)(2,1)S(1)}, u32[]{:S(2)}, u32[]{:S(2)}) %collective-permute-start.5) | collective-permute-done | bytes 147488 | tf_op jit(solution)/shard_map/ppermute | solution.py:485
  46.4 2.5 %collective-permute-done.6.refs_7_ = bf16[3,2,4,24,128]{4,3,2,1,0:T(8,128)(2,1)S(1)} collective-permute-done((bf16[3,2,4,24,128]{4,3,2,1,0:T(8,128)(2,1)}, bf16[3,2,4,24,128]{4,3,2,1,0:T(8,128)(2,1)S(1)}, u32[]{:S(2)}, u32[]{:S(2)}) %collective-permute-start.6) | collective-permute-done | bytes 147488 | tf_op jit(solution)/shard_map/ppermute | solution.py:485
  48.9 0.0 copy-done.1
  48.9 1.1 %synthesis.2 = (bf16[96,640]{1,0:T(8,128)(2,1)S(1)}, bf16[96,640]{1,0:T(8,128)(2,1)S(1)}, bf16[96,640]{1,0:T(8,128)(2,1)S(1)}, bf16[96,640]{1,0:T(8,128)(2,1)S(1)}) custom-call(s32[1]{0:T(128)} %bitcast.3.place_ref.wave_ref, s32[1]{0:T(128)} %bitcast.2.lev_ref, bf16[3,2,4,24,128]{4,3,2,1,0:T(8,128)(2,1)S(1)} %copy-done.1, ...), custom_call_target="tpu_custom_call" | custom-call | flops 805306368 | bytes 4194304 | tf_op jit(solution)/shard_map/synthesis/pallas_call | solution.py:346
  50.0 0.0 copy-start
  50.0 0.1 collective-permute-start.7
  50.1 1.6 %collective-permute-start.8 = (bf16[96,640]{1,0:T(8,128)(2,1)S(1)}, bf16[96,640]{1,0:T(8,128)(2,1)S(1)}, u32[]{:S(2)}, u32[]{:S(2)}) collective-permute-start(bf16[96,640]{1,0:T(8,128)(2,1)S(1)} %get-tuple-element.39), channel_id=1, source_target_pairs={{0,2},{1,3},{2,0},{3,1},{4,6},{5,7},{6,4},{7,5},{8,10},{9,11},{10,... | collective-permute-start | bytes 368648 | tf_op jit(solution)/shard_map/ppermute | solution.py:485
  51.7 0.3 collective-permute-start.9
  51.9 2.0 %synthesis.3 = (bf16[192,640]{1,0:T(8,128)(2,1)S(1)}, bf16[192,640]{1,0:T(8,128)(2,1)S(1)}, bf16[192,640]{1,0:T(8,128)(2,1)S(1)}, bf16[192,640]{1,0:T(8,128)(2,1)S(1)}) custom-call(s32[1]{0:T(128)} %bitcast.3.place_ref.wave_ref, s32[1]{0:T(128)} %bitcast.2.lev_ref, bf16[3,2,4,24,128]{4,3,2,1,0:T(8,128)(2,1)S(1)} %copy-done.1, ...), custom_call_target="tpu_custom_call" | custom-call | flops 1610612736 | bytes 4194304 | tf_op jit(solution)/shard_map/synthesis/pallas_call | solution.py:346
  53.9 0.4 collective-permute-start.12
  54.3 1.5 %collective-permute-start.13 = (bf16[192,640]{1,0:T(8,128)(2,1)S(1)}, bf16[192,640]{1,0:T(8,128)(2,1)S(1)}, u32[]{:S(2)}, u32[]{:S(2)}) collective-permute-start(bf16[192,640]{1,0:T(8,128)(2,1)S(1)} %get-tuple-element.46), channel_id=1, source_target_pairs={{0,2},{1,3},{2,0},{3,1},{4,6},{5,7},{6,4},{7,5},{8,10},{9,11},{10,... | collective-permute-start | bytes 737288 | tf_op jit(solution)/shard_map/ppermute | solution.py:485
  55.8 0.0 collective-permute-done.7.refs_1_
  55.8 0.0 collective-permute-start.14
  55.8 0.5 collective-permute-done.8.refs_2_
  56.3 1.7 %collective-permute-done.9.refs_3_ = bf16[96,640]{1,0:T(8,128)(2,1)S(1)} collective-permute-done((bf16[96,640]{1,0:T(8,128)(2,1)S(1)}, bf16[96,640]{1,0:T(8,128)(2,1)S(1)}, u32[]{:S(2)}, u32[]{:S(2)}) %collective-permute-start.9) | collective-permute-done | bytes 122912 | tf_op jit(solution)/shard_map/ppermute | solution.py:485
  58.0 0.0 copy-done
  58.0 0.8 tracer.1
  58.8 0.6 collective-permute-start.10
  59.4 2.5 %collective-permute-start.11 = (bf16[96,640]{1,0:T(8,128)(2,1)S(1)}, bf16[96,640]{1,0:T(8,128)(2,1)S(1)}, u32[]{:S(2)}, u32[]{:S(2)}) collective-permute-start(bf16[96,640]{1,0:T(8,128)(2,1)S(1)} %get-tuple-element.43), channel_id=1, source_target_pairs={{4,8},{12,16},{20,24},{0,0},{8,4},{16,12},{24,20},{28,28},{5,9},{1... | collective-permute-start | bytes 368648 | tf_op jit(solution)/shard_map/ppermute | solution.py:493
  61.9 0.0 collective-permute-done.12.refs_1_
  61.9 2.3 %collective-permute-done.13.refs_2_ = bf16[192,640]{1,0:T(8,128)(2,1)S(1)} collective-permute-done((bf16[192,640]{1,0:T(8,128)(2,1)S(1)}, bf16[192,640]{1,0:T(8,128)(2,1)S(1)}, u32[]{:S(2)}, u32[]{:S(2)}) %collective-permute-start.13) | collective-permute-done | bytes 245792 | tf_op jit(solution)/shard_map/ppermute | solution.py:485
  64.2 4.2 %collective-permute-done.14.refs_3_ = bf16[192,640]{1,0:T(8,128)(2,1)S(1)} collective-permute-done((bf16[192,640]{1,0:T(8,128)(2,1)S(1)}, bf16[192,640]{1,0:T(8,128)(2,1)S(1)}, u32[]{:S(2)}, u32[]{:S(2)}) %collective-permute-start.14) | collective-permute-done | bytes 245792 | tf_op jit(solution)/shard_map/ppermute | solution.py:485
  68.4 0.0 collective-permute-done.10.pair_ref
  68.4 0.0 collective-permute-done.11.diagonal_ref
  68.4 1.7 %first_step.1 = (f32[4,96,640]{2,1,0:T(8,128)S(1)}, f32[4,96,640]{2,1,0:T(8,128)S(1)}, f32[4,96,640]{2,1,0:T(8,128)S(1)}, bf16[96,640]{1,0:T(8,128)(2,1)S(1)}, bf16[96,640]{1,0:T(8,128)(2,1)S(1)}) custom-call(s32[1]{0:T(128)} %bitcast.odd_ref, s32[1]{0:T(128)} %bitcast.1.end_ref, s32[1]{0:T(128)} %bitcast.2.lev_ref, f32[96,96]{1,0:T(8,128)S(1)} %copy-done, ...), custom_call_target="tpu_custom_call" | custom-call | flops 4000000 | bytes 4000000 | tf_op jit(solution)/shard_map/first_step/pallas_call | solution.py:470
  70.2 1.0 %collective-permute-start.15 = (bf16[96,640]{1,0:T(8,128)(2,1)S(1)}, bf16[96,640]{1,0:T(8,128)(2,1)S(1)}, u32[]{:S(2)}, u32[]{:S(2)}) collective-permute-start(bf16[96,640]{1,0:T(8,128)(2,1)S(1)} %get-tuple-element.49), channel_id=1, source_target_pairs={{0,4},{4,0},{8,12},{12,8},{16,20},{20,16},{24,28},{28,24},{1,5},{5... | collective-permute-start | bytes 368648 | tf_op jit(solution)/shard_map/ppermute | solution.py:494
  71.2 2.1 %collective-permute-start.16 = (bf16[96,640]{1,0:T(8,128)(2,1)S(1)}, bf16[96,640]{1,0:T(8,128)(2,1)S(1)}, u32[]{:S(2)}, u32[]{:S(2)}) collective-permute-start(bf16[96,640]{1,0:T(8,128)(2,1)S(1)} %get-tuple-element.50), channel_id=1, source_target_pairs={{4,8},{12,16},{20,24},{0,0},{8,4},{16,12},{24,20},{28,28},{5,9},{1... | collective-permute-start | bytes 368648 | tf_op jit(solution)/shard_map/ppermute | solution.py:493
  73.3 2.6 %collective-permute-done.15.pair_ref = bf16[96,640]{1,0:T(8,128)(2,1)S(1)} collective-permute-done((bf16[96,640]{1,0:T(8,128)(2,1)S(1)}, bf16[96,640]{1,0:T(8,128)(2,1)S(1)}, u32[]{:S(2)}, u32[]{:S(2)}) %collective-permute-start.15) | collective-permute-done | bytes 122912 | tf_op jit(solution)/shard_map/ppermute | solution.py:494
  75.8 3.2 %collective-permute-done.16.diagonal_ref = bf16[96,640]{1,0:T(8,128)(2,1)S(1)} collective-permute-done((bf16[96,640]{1,0:T(8,128)(2,1)S(1)}, bf16[96,640]{1,0:T(8,128)(2,1)S(1)}, u32[]{:S(2)}, u32[]{:S(2)}) %collective-permute-start.16) | collective-permute-done | bytes 122912 | tf_op jit(solution)/shard_map/ppermute | solution.py:493
  79.0 1.8 %second_step.1 = f32[96,4,512]{2,1,0:T(4,128)} custom-call(s32[1]{0:T(128)} %bitcast.odd_ref, s32[1]{0:T(128)} %bitcast.1.end_ref, f32[4,96,640]{2,1,0:T(8,128)S(1)} %get-tuple-element.48.tracer_ref, bf16[96,640]{1,0:T(8,128)(2,1)S(1)} %collective-permute-done.15.pair_ref, bf16[96,640]{1,0:T(8,128)(2,1)S(1)} %collective-permute-done.16.diagonal_ref, ...), custom_call_target="tpu_custom_call" | custom-call | flops 4000000 | bytes 4000000 | tf_op jit(solution)/shard_map/second_step/pallas_call | solution.py:470
  (1 shorter events, 0.0 us)
Async XLA Ops:
  0.0 23.6 %copy-start.2 = (s32[1024]{0:T(1024)S(1)}, s32[1024]{0:T(1024)}, u32[]{:S(2)}) copy-start(s32[1024]{0:T(1024)} %numbers_ref.1) | copy-start | bytes 12292
  16.2 32.6 %copy-start.1 = (bf16[3,2,4,24,128]{4,3,2,1,0:T(8,128)(2,1)S(1)}, bf16[3,2,4,24,128]{4,3,2,1,0:T(8,128)(2,1)}, u32[]{:S(2)}) copy-start(bf16[3,2,4,24,128]{4,3,2,1,0:T(8,128)(2,1)} %get-tuple-element.29.refs_0_) | copy-start | bytes 442372
  16.2 7.7 %collective-permute-start = (bf16[3,2,4,24,128]{4,3,2,1,0:T(8,128)(2,1)}, bf16[3,2,4,24,128]{4,3,2,1,0:T(8,128)(2,1)S(1)}, u32[]{:S(2)}, u32[]{:S(2)}) collective-permute-start(bf16[3,2,4,24,128]{4,3,2,1,0:T(8,128)(2,1)} %get-tuple-element.30), channel_id=1, source_target_pairs={{0,4},{4,0},{8,12},{12,8},{16,20},{20,16},{24,28},{28,24},{1,5},{5... | collective-permute-start | bytes 442376 | tf_op jit(solution)/shard_map/ppermute | solution.py:485
  17.8 9.8 %collective-permute-start.1 = (bf16[3,2,4,24,128]{4,3,2,1,0:T(8,128)(2,1)}, bf16[3,2,4,24,128]{4,3,2,1,0:T(8,128)(2,1)S(1)}, u32[]{:S(2)}, u32[]{:S(2)}) collective-permute-start(bf16[3,2,4,24,128]{4,3,2,1,0:T(8,128)(2,1)} %get-tuple-element.31), channel_id=1, source_target_pairs={{0,8},{4,12},{8,0},{12,4},{16,24},{20,28},{24,16},{28,20},{1,9},{5... | collective-permute-start | bytes 442376 | tf_op jit(solution)/shard_map/ppermute | solution.py:485
  19.4 12.2 %collective-permute-start.2 = (bf16[3,2,4,24,128]{4,3,2,1,0:T(8,128)(2,1)}, bf16[3,2,4,24,128]{4,3,2,1,0:T(8,128)(2,1)S(1)}, u32[]{:S(2)}, u32[]{:S(2)}) collective-permute-start(bf16[3,2,4,24,128]{4,3,2,1,0:T(8,128)(2,1)} %get-tuple-element.32), channel_id=1, source_target_pairs={{0,12},{4,8},{8,4},{12,0},{16,28},{20,24},{24,20},{28,16},{1,13},{... | collective-permute-start | bytes 442376 | tf_op jit(solution)/shard_map/ppermute | solution.py:485
  19.8 11.8 %collective-permute-start.3 = (bf16[3,2,4,24,128]{4,3,2,1,0:T(8,128)(2,1)}, bf16[3,2,4,24,128]{4,3,2,1,0:T(8,128)(2,1)S(1)}, u32[]{:S(2)}, u32[]{:S(2)}) collective-permute-start(bf16[3,2,4,24,128]{4,3,2,1,0:T(8,128)(2,1)} %get-tuple-element.33), channel_id=1, source_target_pairs={{0,16},{4,20},{8,24},{12,28},{16,0},{20,4},{24,8},{28,12},{1,17},{... | collective-permute-start | bytes 442376 | tf_op jit(solution)/shard_map/ppermute | solution.py:485
  19.8 20.6 %collective-permute-start.4 = (bf16[3,2,4,24,128]{4,3,2,1,0:T(8,128)(2,1)}, bf16[3,2,4,24,128]{4,3,2,1,0:T(8,128)(2,1)S(1)}, u32[]{:S(2)}, u32[]{:S(2)}) collective-permute-start(bf16[3,2,4,24,128]{4,3,2,1,0:T(8,128)(2,1)} %get-tuple-element.34), channel_id=1, source_target_pairs={{0,20},{4,16},{8,28},{12,24},{16,4},{20,0},{24,12},{28,8},{1,21},{... | collective-permute-start | bytes 442376 | tf_op jit(solution)/shard_map/ppermute | solution.py:485
  24.0 22.4 %collective-permute-start.5 = (bf16[3,2,4,24,128]{4,3,2,1,0:T(8,128)(2,1)}, bf16[3,2,4,24,128]{4,3,2,1,0:T(8,128)(2,1)S(1)}, u32[]{:S(2)}, u32[]{:S(2)}) collective-permute-start(bf16[3,2,4,24,128]{4,3,2,1,0:T(8,128)(2,1)} %get-tuple-element.35), channel_id=1, source_target_pairs={{0,24},{4,28},{8,16},{12,20},{16,8},{20,12},{24,0},{28,4},{1,25},{... | collective-permute-start | bytes 442376 | tf_op jit(solution)/shard_map/ppermute | solution.py:485
  27.6 21.2 %collective-permute-start.6 = (bf16[3,2,4,24,128]{4,3,2,1,0:T(8,128)(2,1)}, bf16[3,2,4,24,128]{4,3,2,1,0:T(8,128)(2,1)S(1)}, u32[]{:S(2)}, u32[]{:S(2)}) collective-permute-start(bf16[3,2,4,24,128]{4,3,2,1,0:T(8,128)(2,1)} %get-tuple-element.36), channel_id=1, source_target_pairs={{0,28},{4,24},{8,20},{12,16},{16,12},{20,8},{24,4},{28,0},{1,29},{... | collective-permute-start | bytes 442376 | tf_op jit(solution)/shard_map/ppermute | solution.py:485
  50.0 8.0 %copy-start = (f32[96,96]{1,0:T(8,128)S(1)}, f32[96,96]{1,0:T(8,128)}, u32[]{:S(2)}) copy-start(f32[96,96]{1,0:T(8,128)} %vertical_ref.3) | copy-start | bytes 110596
  50.0 5.8 %collective-permute-start.7 = (bf16[96,640]{1,0:T(8,128)(2,1)S(1)}, bf16[96,640]{1,0:T(8,128)(2,1)S(1)}, u32[]{:S(2)}, u32[]{:S(2)}) collective-permute-start(bf16[96,640]{1,0:T(8,128)(2,1)S(1)} %get-tuple-element.38), channel_id=1, source_target_pairs={{0,1},{1,0},{2,3},{3,2},{4,5},{5,4},{6,7},{7,6},{8,9},{9,8},{10,11... | collective-permute-start | bytes 368648 | tf_op jit(solution)/shard_map/ppermute | solution.py:485
  50.1 6.3 %collective-permute-start.8 = (bf16[96,640]{1,0:T(8,128)(2,1)S(1)}, bf16[96,640]{1,0:T(8,128)(2,1)S(1)}, u32[]{:S(2)}, u32[]{:S(2)}) collective-permute-start(bf16[96,640]{1,0:T(8,128)(2,1)S(1)} %get-tuple-element.39), channel_id=1, source_target_pairs={{0,2},{1,3},{2,0},{3,1},{4,6},{5,7},{6,4},{7,5},{8,10},{9,11},{10,... | collective-permute-start | bytes 368648 | tf_op jit(solution)/shard_map/ppermute | solution.py:485
  51.7 6.3 %collective-permute-start.9 = (bf16[96,640]{1,0:T(8,128)(2,1)S(1)}, bf16[96,640]{1,0:T(8,128)(2,1)S(1)}, u32[]{:S(2)}, u32[]{:S(2)}) collective-permute-start(bf16[96,640]{1,0:T(8,128)(2,1)S(1)} %get-tuple-element.40), channel_id=1, source_target_pairs={{0,3},{1,2},{2,1},{3,0},{4,7},{5,6},{6,5},{7,4},{8,11},{9,10},{10,... | collective-permute-start | bytes 368648 | tf_op jit(solution)/shard_map/ppermute | solution.py:485
  53.9 8.0 %collective-permute-start.12 = (bf16[192,640]{1,0:T(8,128)(2,1)S(1)}, bf16[192,640]{1,0:T(8,128)(2,1)S(1)}, u32[]{:S(2)}, u32[]{:S(2)}) collective-permute-start(bf16[192,640]{1,0:T(8,128)(2,1)S(1)} %get-tuple-element.45), channel_id=1, source_target_pairs={{0,1},{1,0},{2,3},{3,2},{4,5},{5,4},{6,7},{7,6},{8,9},{9,8},{10,11... | collective-permute-start | bytes 737288 | tf_op jit(solution)/shard_map/ppermute | solution.py:485
  54.3 9.9 %collective-permute-start.13 = (bf16[192,640]{1,0:T(8,128)(2,1)S(1)}, bf16[192,640]{1,0:T(8,128)(2,1)S(1)}, u32[]{:S(2)}, u32[]{:S(2)}) collective-permute-start(bf16[192,640]{1,0:T(8,128)(2,1)S(1)} %get-tuple-element.46), channel_id=1, source_target_pairs={{0,2},{1,3},{2,0},{3,1},{4,6},{5,7},{6,4},{7,5},{8,10},{9,11},{10,... | collective-permute-start | bytes 737288 | tf_op jit(solution)/shard_map/ppermute | solution.py:485
  55.8 12.6 %collective-permute-start.14 = (bf16[192,640]{1,0:T(8,128)(2,1)S(1)}, bf16[192,640]{1,0:T(8,128)(2,1)S(1)}, u32[]{:S(2)}, u32[]{:S(2)}) collective-permute-start(bf16[192,640]{1,0:T(8,128)(2,1)S(1)} %get-tuple-element.47), channel_id=1, source_target_pairs={{0,3},{1,2},{2,1},{3,0},{4,7},{5,6},{6,5},{7,4},{8,11},{9,10},{10,... | collective-permute-start | bytes 737288 | tf_op jit(solution)/shard_map/ppermute | solution.py:485
  58.8 9.6 %collective-permute-start.10 = (bf16[96,640]{1,0:T(8,128)(2,1)S(1)}, bf16[96,640]{1,0:T(8,128)(2,1)S(1)}, u32[]{:S(2)}, u32[]{:S(2)}) collective-permute-start(bf16[96,640]{1,0:T(8,128)(2,1)S(1)} %get-tuple-element.42), channel_id=1, source_target_pairs={{0,4},{4,0},{8,12},{12,8},{16,20},{20,16},{24,28},{28,24},{1,5},{5... | collective-permute-start | bytes 368648 | tf_op jit(solution)/shard_map/ppermute | solution.py:494
  59.4 9.0 %collective-permute-start.11 = (bf16[96,640]{1,0:T(8,128)(2,1)S(1)}, bf16[96,640]{1,0:T(8,128)(2,1)S(1)}, u32[]{:S(2)}, u32[]{:S(2)}) collective-permute-start(bf16[96,640]{1,0:T(8,128)(2,1)S(1)} %get-tuple-element.43), channel_id=1, source_target_pairs={{4,8},{12,16},{20,24},{0,0},{8,4},{16,12},{24,20},{28,28},{5,9},{1... | collective-permute-start | bytes 368648 | tf_op jit(solution)/shard_map/ppermute | solution.py:493
  70.2 5.7 %collective-permute-start.15 = (bf16[96,640]{1,0:T(8,128)(2,1)S(1)}, bf16[96,640]{1,0:T(8,128)(2,1)S(1)}, u32[]{:S(2)}, u32[]{:S(2)}) collective-permute-start(bf16[96,640]{1,0:T(8,128)(2,1)S(1)} %get-tuple-element.49), channel_id=1, source_target_pairs={{0,4},{4,0},{8,12},{12,8},{16,20},{20,16},{24,28},{28,24},{1,5},{5... | collective-permute-start | bytes 368648 | tf_op jit(solution)/shard_map/ppermute | solution.py:494
  71.2 7.8 %collective-permute-start.16 = (bf16[96,640]{1,0:T(8,128)(2,1)S(1)}, bf16[96,640]{1,0:T(8,128)(2,1)S(1)}, u32[]{:S(2)}, u32[]{:S(2)}) collective-permute-start(bf16[96,640]{1,0:T(8,128)(2,1)S(1)} %get-tuple-element.50), channel_id=1, source_target_pairs={{4,8},{12,16},{20,24},{0,0},{8,4},{16,12},{24,20},{28,28},{5,9},{1... | collective-permute-start | bytes 368648 | tf_op jit(solution)/shard_map/ppermute | solution.py:493

commit v4 on v3

--- a/solution.py
+++ b/solution.py
@@ -108,7 +108,7 @@
     courant_x = courant_max * jnp.tanh(fields[0])
     courant_y = courant_max * jnp.tanh(fields[1])
     tracer = fields[2]
-    for sweep in range(2):
+    for _ in range(2):
         extended = padded(tracer, (("wave", 1),), 1, False)
         extended = padded(extended, (("lev", 2),), 1, True)
         tracer = upwind_core(extended, courant_x, courant_y)
@@ -465,7 +465,7 @@
         out_ref[:, lat, :] = values[:, :width]
 
 
-def local_call(kernel, outs, scratch, name, *operands):
+def local_call(kernel, outs, scratch, *operands):
     smem = pl.BlockSpec(memory_space=pltpu.SMEM)
     return pl.pallas_call(
         kernel,
@@ -475,15 +475,15 @@
         scratch_shapes=scratch,
         compiler_params=pltpu.CompilerParams(vmem_limit_bytes=16 << 20),
         cost_estimate=cost(4_000_000, 4_000_000),
-        name=name,
     )(*operands)
 
 
 def exchange(blocks, axis):
     count = lax.axis_size(axis)
-    return [blocks[0]] + [
-        lax.ppermute(blocks[d], axis, [(i, i ^ d) for i in range(count)]) for d in range(1, count)
-    ]
+    moved = [blocks[0]]
+    for d in range(1, count):
+        moved.append(lax.ppermute(blocks[d], axis, [(i, i ^ d) for i in range(count)]))
+    return moved
 
 
 def edges(pair, diagonal):
@@ -497,7 +497,7 @@
 
 def tiled_body(spectrum, legendre, wave_numbers, vertical):
     waves, levs = lax.axis_size("wave"), lax.axis_size("lev")
-    slots, degrees, modes, _ = spectrum.shape
+    slots, _, modes, _ = spectrum.shape
     levels = vertical.shape[0]
     lats = 2 * legendre.shape[2] // waves
     width = NLON // levs
@@ -525,7 +525,6 @@
         functools.partial(tracer_kernel, modes),
         (whole, row, row),
         [pltpu.VMEM(gathered, jnp.float32)],
-        "tracer",
         odd,
         lev_place,
         vertical,
@@ -536,7 +535,6 @@
         functools.partial(first_step_kernel, modes),
         (whole, whole, whole, row, row),
         [pltpu.VMEM((2, *gathered), jnp.float32)],
-        "first_step",
         odd,
         at_end,
         lev_place,
@@ -551,7 +549,6 @@
         second_step_kernel,
         jax.ShapeDtypeStruct((levels, lats, width), jnp.float32),
         [],
-        "second_step",
         odd,
         at_end,
         tracer,

time: 81.1 us -> 81.1 us (level)
  no operation moved by 1% of the time
where the time goes in v4:
time: 81.1 us; the launch traced here: 80.8 us
  waiting for transfers between devices  34.8 us (43%)
  Pallas kernels  25.4 us (31%)
  starting transfers between devices  18 us (22%)
  other arithmetic  2.3 us (3%)
    ppermute x13, waiting for transfers between devices, exchange(): lax.ppermute(blocks[d], axis, [(i, i ^ d) for i in range(count)])  29 us
    pallas_call x1, Pallas kernels, legendre_stage(): pl.pallas_call(legendre_kernel, out_shape=[jax.ShapeDtypeStruct((FIELDS,...  16.2 us
    ppermute x13, starting transfers between devices, exchange(): lax.ppermute(blocks[d], axis, [(i, i ^ d) for i in range(count)])  11.8 us
    ppermute x2, starting transfers between devices, edges(): diagonal = lax.ppermute(diagonal, 'wave', steps)  4.59 us
    pallas_call x3, Pallas kernels, local_call(): pl.pallas_call(kernel, out_shape=outs, in_specs=[smem if operand.dtype ==...  4.32 us
    ppermute x2, waiting for transfers between devices, edges(): diagonal = lax.ppermute(diagonal, 'wave', steps)  3.24 us
    pallas_call x2, Pallas kernels, synthesis_stage(): pl.pallas_call(functools.partial(synthesis_kernel, waves, levs, fields),...  3.07 us
    ppermute x2, waiting for transfers between devices, edges(): pair = lax.ppermute(pair, 'wave', [(i, i ^ 1) for i in range(count)])  2.53 us
  transfers between devices with their start and end apart: 17, of which 10 were waited for; matrix products, arithmetic and copies ran while one was open for 3% of the time, Pallas kernels for 6%

profile of v4, /device:TPU:16, one launch (start us, length us, event | category | flops | bytes accessed | tf_op | source)
XLA Modules:
  0.0 80.8 jit_solution(8059781623004123270)
XLA Ops:
  0.0 0.0 copy-start.2
  0.0 16.2 %legendre_sums.1 = (bf16[3,2,4,24,128]{4,3,2,1,0:T(8,128)(2,1)}, bf16[3,2,4,24,128]{4,3,2,1,0:T(8,128)(2,1)}, bf16[3,2,4,24,128]{4,3,2,1,0:T(8,128)(2,1)}, bf16[...) custom-call(s32[1024]{0:T(1024)} %numbers_ref.1, ...), custom_call_target="tpu_custom_call" | custom-call | flops 603979776 | bytes 18874368 | tf_op jit(solution)/shard_map/legendre_sums/pallas_call | solution.py:242
  16.2 0.0 copy-start.1
  16.2 1.5 %collective-permute-start = (bf16[3,2,4,24,128]{4,3,2,1,0:T(8,128)(2,1)}, bf16[3,2,4,24,128]{4,3,2,1,0:T(8,128)(2,1)S(1)}, u32[]{:S(2)}, u32[]{:S(2)}) collective-permute-start(bf16[3,2,4,24,128]{4,3,2,1,0:T(8,128)(2,1)} %get-tuple-element.30), channel_id=1, source_target_pairs={{0,4},{4,0},{8,12},{12,8},{16,20},{20,16},{24,28},{28,24},{1,5},{5... | collective-permute-start | bytes 442376 | tf_op jit(solution)/shard_map/ppermute | solution.py:485
  17.8 1.6 %collective-permute-start.1 = (bf16[3,2,4,24,128]{4,3,2,1,0:T(8,128)(2,1)}, bf16[3,2,4,24,128]{4,3,2,1,0:T(8,128)(2,1)S(1)}, u32[]{:S(2)}, u32[]{:S(2)}) collective-permute-start(bf16[3,2,4,24,128]{4,3,2,1,0:T(8,128)(2,1)} %get-tuple-element.31), channel_id=1, source_target_pairs={{0,8},{4,12},{8,0},{12,4},{16,24},{20,28},{24,16},{28,20},{1,9},{5... | collective-permute-start | bytes 442376 | tf_op jit(solution)/shard_map/ppermute | solution.py:485
  19.4 0.4 collective-permute-start.2
  19.8 0.0 collective-permute-start.3
  19.8 3.8 %collective-permute-start.4 = (bf16[3,2,4,24,128]{4,3,2,1,0:T(8,128)(2,1)}, bf16[3,2,4,24,128]{4,3,2,1,0:T(8,128)(2,1)S(1)}, u32[]{:S(2)}, u32[]{:S(2)}) collective-permute-start(bf16[3,2,4,24,128]{4,3,2,1,0:T(8,128)(2,1)} %get-tuple-element.34), channel_id=1, source_target_pairs={{0,20},{4,16},{8,28},{12,24},{16,4},{20,0},{24,12},{28,8},{1,21},{... | collective-permute-start | bytes 442376 | tf_op jit(solution)/shard_map/ppermute | solution.py:485
  23.6 0.0 copy-done.2
  23.7 0.2 fusion.11
  23.8 0.1 cos.7.turn_cos_ref
  23.9 0.0 collective-permute-done.refs_1_
  24.0 0.5 collective-permute-start.5
  24.5 3.1 %collective-permute-done.1.refs_2_ = bf16[3,2,4,24,128]{4,3,2,1,0:T(8,128)(2,1)S(1)} collective-permute-done((bf16[3,2,4,24,128]{4,3,2,1,0:T(8,128)(2,1)}, bf16[3,2,4,24,128]{4,3,2,1,0:T(8,128)(2,1)S(1)}, u32[]{:S(2)}, u32[]{:S(2)}) %collective-permute-start.1) | collective-permute-done | bytes 147488 | tf_op jit(solution)/shard_map/ppermute | solution.py:485
  27.6 0.0 collective-permute-start.6
  27.6 2.1 %sine_multiply_fusion = (f32[8,128,128]{2,1,0:T(8,128)S(1)}, f32[8,128,128]{2,1,0:T(8,128)S(1)}) fusion(s32[8,128]{1,0:T(8,128)S(1)} %bitcast.14, f32[8,128]{1,0:T(8,128)S(1)} %compare_select_fusion.5), kind=kLoop, calls=%fused_computation.6 | loop fusion | flops 2097152 | bytes 1056768 | tf_op jit(solution)/shard_map/mul | solution.py:299
  29.8 1.8 %twiddles.1.refs_9_ = bf16[8,2,128,1024]{3,2,1,0:T(8,128)(2,1)S(1)} custom-call(s32[1]{0:T(128)} %bitcast.3.place_ref.wave_ref, f32[8,128,128]{2,1,0:T(8,128)S(1)} %get-tuple-element.56.low_cos_ref, f32[8,128,128]{2,1,0:T(8,128)S(1)} %get-tuple-element.55.low_sin_ref, f32[8,1,128]{2,1,0:T(1,128)S(1)} %cos.7.turn_cos_ref, ...), custom_call_target="tpu_custom_call" | custom-call | flops 8388608 | bytes 4194304 | tf_op jit(solution)/shard_map/twiddles/pallas_call | solution.py:287
  31.6 0.0 collective-permute-done.2.refs_3_
  31.6 0.0 collective-permute-done.3.refs_4_
  31.6 8.8 %collective-permute-done.4.refs_5_ = bf16[3,2,4,24,128]{4,3,2,1,0:T(8,128)(2,1)S(1)} collective-permute-done((bf16[3,2,4,24,128]{4,3,2,1,0:T(8,128)(2,1)}, bf16[3,2,4,24,128]{4,3,2,1,0:T(8,128)(2,1)S(1)}, u32[]{:S(2)}, u32[]{:S(2)}) %collective-permute-start.4) | collective-permute-done | bytes 147488 | tf_op jit(solution)/shard_map/ppermute | solution.py:485
  40.4 6.0 %collective-permute-done.5.refs_6_ = bf16[3,2,4,24,128]{4,3,2,1,0:T(8,128)(2,1)S(1)} collective-permute-done((bf16[3,2,4,24,128]{4,3,2,1,0:T(8,128)(2,1)}, bf16[3,2,4,24,128]{4,3,2,1,0:T(8,128)(2,1)S(1)}, u32[]{:S(2)}, u32[]{:S(2)}) %collective-permute-start.5) | collective-permute-done | bytes 147488 | tf_op jit(solution)/shard_map/ppermute | solution.py:485
  46.4 2.5 %collective-permute-done.6.refs_7_ = bf16[3,2,4,24,128]{4,3,2,1,0:T(8,128)(2,1)S(1)} collective-permute-done((bf16[3,2,4,24,128]{4,3,2,1,0:T(8,128)(2,1)}, bf16[3,2,4,24,128]{4,3,2,1,0:T(8,128)(2,1)S(1)}, u32[]{:S(2)}, u32[]{:S(2)}) %collective-permute-start.6) | collective-permute-done | bytes 147488 | tf_op jit(solution)/shard_map/ppermute | solution.py:485
  48.9 0.0 copy-done.1
  48.9 1.1 %synthesis.2 = (bf16[96,640]{1,0:T(8,128)(2,1)S(1)}, bf16[96,640]{1,0:T(8,128)(2,1)S(1)}, bf16[96,640]{1,0:T(8,128)(2,1)S(1)}, bf16[96,640]{1,0:T(8,128)(2,1)S(1)}) custom-call(s32[1]{0:T(128)} %bitcast.3.place_ref.wave_ref, s32[1]{0:T(128)} %bitcast.2.lev_ref, bf16[3,2,4,24,128]{4,3,2,1,0:T(8,128)(2,1)S(1)} %copy-done.1, ...), custom_call_target="tpu_custom_call" | custom-call | flops 805306368 | bytes 4194304 | tf_op jit(solution)/shard_map/synthesis/pallas_call | solution.py:346
  50.0 0.0 copy-start
  50.0 0.1 collective-permute-start.7
  50.1 1.6 %collective-permute-start.8 = (bf16[96,640]{1,0:T(8,128)(2,1)S(1)}, bf16[96,640]{1,0:T(8,128)(2,1)S(1)}, u32[]{:S(2)}, u32[]{:S(2)}) collective-permute-start(bf16[96,640]{1,0:T(8,128)(2,1)S(1)} %get-tuple-element.39), channel_id=1, source_target_pairs={{0,2},{1,3},{2,0},{3,1},{4,6},{5,7},{6,4},{7,5},{8,10},{9,11},{10,... | collective-permute-start | bytes 368648 | tf_op jit(solution)/shard_map/ppermute | solution.py:485
  51.7 0.3 collective-permute-start.9
  51.9 2.0 %synthesis.3 = (bf16[192,640]{1,0:T(8,128)(2,1)S(1)}, bf16[192,640]{1,0:T(8,128)(2,1)S(1)}, bf16[192,640]{1,0:T(8,128)(2,1)S(1)}, bf16[192,640]{1,0:T(8,128)(2,1)S(1)}) custom-call(s32[1]{0:T(128)} %bitcast.3.place_ref.wave_ref, s32[1]{0:T(128)} %bitcast.2.lev_ref, bf16[3,2,4,24,128]{4,3,2,1,0:T(8,128)(2,1)S(1)} %copy-done.1, ...), custom_call_target="tpu_custom_call" | custom-call | flops 1610612736 | bytes 4194304 | tf_op jit(solution)/shard_map/synthesis/pallas_call | solution.py:346
  53.9 0.4 collective-permute-start.12
  54.3 1.5 %collective-permute-start.13 = (bf16[192,640]{1,0:T(8,128)(2,1)S(1)}, bf16[192,640]{1,0:T(8,128)(2,1)S(1)}, u32[]{:S(2)}, u32[]{:S(2)}) collective-permute-start(bf16[192,640]{1,0:T(8,128)(2,1)S(1)} %get-tuple-element.46), channel_id=1, source_target_pairs={{0,2},{1,3},{2,0},{3,1},{4,6},{5,7},{6,4},{7,5},{8,10},{9,11},{10,... | collective-permute-start | bytes 737288 | tf_op jit(solution)/shard_map/ppermute | solution.py:485
  55.8 0.0 collective-permute-done.7.refs_1_
  55.8 0.0 collective-permute-start.14
  55.8 0.5 collective-permute-done.8.refs_2_
  56.3 1.7 %collective-permute-done.9.refs_3_ = bf16[96,640]{1,0:T(8,128)(2,1)S(1)} collective-permute-done((bf16[96,640]{1,0:T(8,128)(2,1)S(1)}, bf16[96,640]{1,0:T(8,128)(2,1)S(1)}, u32[]{:S(2)}, u32[]{:S(2)}) %collective-permute-start.9) | collective-permute-done | bytes 122912 | tf_op jit(solution)/shard_map/ppermute | solution.py:485
  58.0 0.0 copy-done
  58.0 0.8 shard_map.46
  58.8 0.6 collective-permute-start.10
  59.4 2.5 %collective-permute-start.11 = (bf16[96,640]{1,0:T(8,128)(2,1)S(1)}, bf16[96,640]{1,0:T(8,128)(2,1)S(1)}, u32[]{:S(2)}, u32[]{:S(2)}) collective-permute-start(bf16[96,640]{1,0:T(8,128)(2,1)S(1)} %get-tuple-element.43), channel_id=1, source_target_pairs={{4,8},{12,16},{20,24},{0,0},{8,4},{16,12},{24,20},{28,28},{5,9},{1... | collective-permute-start | bytes 368648 | tf_op jit(solution)/shard_map/ppermute | solution.py:493
  61.9 0.0 collective-permute-done.12.refs_1_
  61.9 2.3 %collective-permute-done.13.refs_2_ = bf16[192,640]{1,0:T(8,128)(2,1)S(1)} collective-permute-done((bf16[192,640]{1,0:T(8,128)(2,1)S(1)}, bf16[192,640]{1,0:T(8,128)(2,1)S(1)}, u32[]{:S(2)}, u32[]{:S(2)}) %collective-permute-start.13) | collective-permute-done | bytes 245792 | tf_op jit(solution)/shard_map/ppermute | solution.py:485
  64.2 4.2 %collective-permute-done.14.refs_3_ = bf16[192,640]{1,0:T(8,128)(2,1)S(1)} collective-permute-done((bf16[192,640]{1,0:T(8,128)(2,1)S(1)}, bf16[192,640]{1,0:T(8,128)(2,1)S(1)}, u32[]{:S(2)}, u32[]{:S(2)}) %collective-permute-start.14) | collective-permute-done | bytes 245792 | tf_op jit(solution)/shard_map/ppermute | solution.py:485
  68.4 0.0 collective-permute-done.10.pair_ref
  68.4 0.0 collective-permute-done.11.diagonal_ref
  68.4 1.7 %shard_map.47 = (f32[4,96,640]{2,1,0:T(8,128)S(1)}, f32[4,96,640]{2,1,0:T(8,128)S(1)}, f32[4,96,640]{2,1,0:T(8,128)S(1)}, bf16[96,640]{1,0:T(8,128)(2,1)S(1)}, bf16[96,640]{1,0:T(8,128)(2,1)S(1)}) custom-call(s32[1]{0:T(128)} %bitcast.odd_ref, s32[1]{0:T(128)} %bitcast.1.end_ref, s32[1]{0:T(128)} %bitcast.2.lev_ref, f32[96,96]{1,0:T(8,128)S(1)} %copy-done, ...), custom_call_target="tpu_custom_call" | custom-call | flops 4000000 | bytes 4000000 | tf_op jit(solution)/shard_map/pallas_call | solution.py:470
  70.1 1.0 %collective-permute-start.15 = (bf16[96,640]{1,0:T(8,128)(2,1)S(1)}, bf16[96,640]{1,0:T(8,128)(2,1)S(1)}, u32[]{:S(2)}, u32[]{:S(2)}) collective-permute-start(bf16[96,640]{1,0:T(8,128)(2,1)S(1)} %get-tuple-element.49), channel_id=1, source_target_pairs={{0,4},{4,0},{8,12},{12,8},{16,20},{20,16},{24,28},{28,24},{1,5},{5... | collective-permute-start | bytes 368648 | tf_op jit(solution)/shard_map/ppermute | solution.py:494
  71.2 2.1 %collective-permute-start.16 = (bf16[96,640]{1,0:T(8,128)(2,1)S(1)}, bf16[96,640]{1,0:T(8,128)(2,1)S(1)}, u32[]{:S(2)}, u32[]{:S(2)}) collective-permute-start(bf16[96,640]{1,0:T(8,128)(2,1)S(1)} %get-tuple-element.50), channel_id=1, source_target_pairs={{4,8},{12,16},{20,24},{0,0},{8,4},{16,12},{24,20},{28,28},{5,9},{1... | collective-permute-start | bytes 368648 | tf_op jit(solution)/shard_map/ppermute | solution.py:493
  73.3 2.5 %collective-permute-done.15.pair_ref = bf16[96,640]{1,0:T(8,128)(2,1)S(1)} collective-permute-done((bf16[96,640]{1,0:T(8,128)(2,1)S(1)}, bf16[96,640]{1,0:T(8,128)(2,1)S(1)}, u32[]{:S(2)}, u32[]{:S(2)}) %collective-permute-start.15) | collective-permute-done | bytes 122912 | tf_op jit(solution)/shard_map/ppermute | solution.py:494
  75.8 3.2 %collective-permute-done.16.diagonal_ref = bf16[96,640]{1,0:T(8,128)(2,1)S(1)} collective-permute-done((bf16[96,640]{1,0:T(8,128)(2,1)S(1)}, bf16[96,640]{1,0:T(8,128)(2,1)S(1)}, u32[]{:S(2)}, u32[]{:S(2)}) %collective-permute-start.16) | collective-permute-done | bytes 122912 | tf_op jit(solution)/shard_map/ppermute | solution.py:493
  79.0 1.8 %shard_map.48 = f32[96,4,512]{2,1,0:T(4,128)} custom-call(s32[1]{0:T(128)} %bitcast.odd_ref, s32[1]{0:T(128)} %bitcast.1.end_ref, f32[4,96,640]{2,1,0:T(8,128)S(1)} %get-tuple-element.48.tracer_ref, bf16[96,640]{1,0:T(8,128)(2,1)S(1)} %collective-permute-done.15.pair_ref, bf16[96,640]{1,0:T(8,128)(2,1)S(1)} %collective-permute-done.16.diagonal_ref, ...), custom_call_target="tpu_custom_call" | custom-call | flops 4000000 | bytes 4000000 | tf_op jit(solution)/shard_map/pallas_call | solution.py:470
  (1 shorter events, 0.0 us)
Async XLA Ops:
  0.0 23.6 %copy-start.2 = (s32[1024]{0:T(1024)S(1)}, s32[1024]{0:T(1024)}, u32[]{:S(2)}) copy-start(s32[1024]{0:T(1024)} %numbers_ref.1) | copy-start | bytes 12292
  16.2 32.6 %copy-start.1 = (bf16[3,2,4,24,128]{4,3,2,1,0:T(8,128)(2,1)S(1)}, bf16[3,2,4,24,128]{4,3,2,1,0:T(8,128)(2,1)}, u32[]{:S(2)}) copy-start(bf16[3,2,4,24,128]{4,3,2,1,0:T(8,128)(2,1)} %get-tuple-element.29.refs_0_) | copy-start | bytes 442372
  16.2 7.7 %collective-permute-start = (bf16[3,2,4,24,128]{4,3,2,1,0:T(8,128)(2,1)}, bf16[3,2,4,24,128]{4,3,2,1,0:T(8,128)(2,1)S(1)}, u32[]{:S(2)}, u32[]{:S(2)}) collective-permute-start(bf16[3,2,4,24,128]{4,3,2,1,0:T(8,128)(2,1)} %get-tuple-element.30), channel_id=1, source_target_pairs={{0,4},{4,0},{8,12},{12,8},{16,20},{20,16},{24,28},{28,24},{1,5},{5... | collective-permute-start | bytes 442376 | tf_op jit(solution)/shard_map/ppermute | solution.py:485
  17.8 9.8 %collective-permute-start.1 = (bf16[3,2,4,24,128]{4,3,2,1,0:T(8,128)(2,1)}, bf16[3,2,4,24,128]{4,3,2,1,0:T(8,128)(2,1)S(1)}, u32[]{:S(2)}, u32[]{:S(2)}) collective-permute-start(bf16[3,2,4,24,128]{4,3,2,1,0:T(8,128)(2,1)} %get-tuple-element.31), channel_id=1, source_target_pairs={{0,8},{4,12},{8,0},{12,4},{16,24},{20,28},{24,16},{28,20},{1,9},{5... | collective-permute-start | bytes 442376 | tf_op jit(solution)/shard_map/ppermute | solution.py:485
  19.4 12.2 %collective-permute-start.2 = (bf16[3,2,4,24,128]{4,3,2,1,0:T(8,128)(2,1)}, bf16[3,2,4,24,128]{4,3,2,1,0:T(8,128)(2,1)S(1)}, u32[]{:S(2)}, u32[]{:S(2)}) collective-permute-start(bf16[3,2,4,24,128]{4,3,2,1,0:T(8,128)(2,1)} %get-tuple-element.32), channel_id=1, source_target_pairs={{0,12},{4,8},{8,4},{12,0},{16,28},{20,24},{24,20},{28,16},{1,13},{... | collective-permute-start | bytes 442376 | tf_op jit(solution)/shard_map/ppermute | solution.py:485
  19.8 11.8 %collective-permute-start.3 = (bf16[3,2,4,24,128]{4,3,2,1,0:T(8,128)(2,1)}, bf16[3,2,4,24,128]{4,3,2,1,0:T(8,128)(2,1)S(1)}, u32[]{:S(2)}, u32[]{:S(2)}) collective-permute-start(bf16[3,2,4,24,128]{4,3,2,1,0:T(8,128)(2,1)} %get-tuple-element.33), channel_id=1, source_target_pairs={{0,16},{4,20},{8,24},{12,28},{16,0},{20,4},{24,8},{28,12},{1,17},{... | collective-permute-start | bytes 442376 | tf_op jit(solution)/shard_map/ppermute | solution.py:485
  19.8 20.6 %collective-permute-start.4 = (bf16[3,2,4,24,128]{4,3,2,1,0:T(8,128)(2,1)}, bf16[3,2,4,24,128]{4,3,2,1,0:T(8,128)(2,1)S(1)}, u32[]{:S(2)}, u32[]{:S(2)}) collective-permute-start(bf16[3,2,4,24,128]{4,3,2,1,0:T(8,128)(2,1)} %get-tuple-element.34), channel_id=1, source_target_pairs={{0,20},{4,16},{8,28},{12,24},{16,4},{20,0},{24,12},{28,8},{1,21},{... | collective-permute-start | bytes 442376 | tf_op jit(solution)/shard_map/ppermute | solution.py:485
  24.0 22.4 %collective-permute-start.5 = (bf16[3,2,4,24,128]{4,3,2,1,0:T(8,128)(2,1)}, bf16[3,2,4,24,128]{4,3,2,1,0:T(8,128)(2,1)S(1)}, u32[]{:S(2)}, u32[]{:S(2)}) collective-permute-start(bf16[3,2,4,24,128]{4,3,2,1,0:T(8,128)(2,1)} %get-tuple-element.35), channel_id=1, source_target_pairs={{0,24},{4,28},{8,16},{12,20},{16,8},{20,12},{24,0},{28,4},{1,25},{... | collective-permute-start | bytes 442376 | tf_op jit(solution)/shard_map/ppermute | solution.py:485
  27.6 21.2 %collective-permute-start.6 = (bf16[3,2,4,24,128]{4,3,2,1,0:T(8,128)(2,1)}, bf16[3,2,4,24,128]{4,3,2,1,0:T(8,128)(2,1)S(1)}, u32[]{:S(2)}, u32[]{:S(2)}) collective-permute-start(bf16[3,2,4,24,128]{4,3,2,1,0:T(8,128)(2,1)} %get-tuple-element.36), channel_id=1, source_target_pairs={{0,28},{4,24},{8,20},{12,16},{16,12},{20,8},{24,4},{28,0},{1,29},{... | collective-permute-start | bytes 442376 | tf_op jit(solution)/shard_map/ppermute | solution.py:485
  50.0 8.0 %copy-start = (f32[96,96]{1,0:T(8,128)S(1)}, f32[96,96]{1,0:T(8,128)}, u32[]{:S(2)}) copy-start(f32[96,96]{1,0:T(8,128)} %vertical_ref.3) | copy-start | bytes 110596
  50.0 5.9 %collective-permute-start.7 = (bf16[96,640]{1,0:T(8,128)(2,1)S(1)}, bf16[96,640]{1,0:T(8,128)(2,1)S(1)}, u32[]{:S(2)}, u32[]{:S(2)}) collective-permute-start(bf16[96,640]{1,0:T(8,128)(2,1)S(1)} %get-tuple-element.38), channel_id=1, source_target_pairs={{0,1},{1,0},{2,3},{3,2},{4,5},{5,4},{6,7},{7,6},{8,9},{9,8},{10,11... | collective-permute-start | bytes 368648 | tf_op jit(solution)/shard_map/ppermute | solution.py:485
  50.1 6.3 %collective-permute-start.8 = (bf16[96,640]{1,0:T(8,128)(2,1)S(1)}, bf16[96,640]{1,0:T(8,128)(2,1)S(1)}, u32[]{:S(2)}, u32[]{:S(2)}) collective-permute-start(bf16[96,640]{1,0:T(8,128)(2,1)S(1)} %get-tuple-element.39), channel_id=1, source_target_pairs={{0,2},{1,3},{2,0},{3,1},{4,6},{5,7},{6,4},{7,5},{8,10},{9,11},{10,... | collective-permute-start | bytes 368648 | tf_op jit(solution)/shard_map/ppermute | solution.py:485
  51.7 6.3 %collective-permute-start.9 = (bf16[96,640]{1,0:T(8,128)(2,1)S(1)}, bf16[96,640]{1,0:T(8,128)(2,1)S(1)}, u32[]{:S(2)}, u32[]{:S(2)}) collective-permute-start(bf16[96,640]{1,0:T(8,128)(2,1)S(1)} %get-tuple-element.40), channel_id=1, source_target_pairs={{0,3},{1,2},{2,1},{3,0},{4,7},{5,6},{6,5},{7,4},{8,11},{9,10},{10,... | collective-permute-start | bytes 368648 | tf_op jit(solution)/shard_map/ppermute | solution.py:485
  53.9 8.0 %collective-permute-start.12 = (bf16[192,640]{1,0:T(8,128)(2,1)S(1)}, bf16[192,640]{1,0:T(8,128)(2,1)S(1)}, u32[]{:S(2)}, u32[]{:S(2)}) collective-permute-start(bf16[192,640]{1,0:T(8,128)(2,1)S(1)} %get-tuple-element.45), channel_id=1, source_target_pairs={{0,1},{1,0},{2,3},{3,2},{4,5},{5,4},{6,7},{7,6},{8,9},{9,8},{10,11... | collective-permute-start | bytes 737288 | tf_op jit(solution)/shard_map/ppermute | solution.py:485
  54.3 9.9 %collective-permute-start.13 = (bf16[192,640]{1,0:T(8,128)(2,1)S(1)}, bf16[192,640]{1,0:T(8,128)(2,1)S(1)}, u32[]{:S(2)}, u32[]{:S(2)}) collective-permute-start(bf16[192,640]{1,0:T(8,128)(2,1)S(1)} %get-tuple-element.46), channel_id=1, source_target_pairs={{0,2},{1,3},{2,0},{3,1},{4,6},{5,7},{6,4},{7,5},{8,10},{9,11},{10,... | collective-permute-start | bytes 737288 | tf_op jit(solution)/shard_map/ppermute | solution.py:485
  55.8 12.6 %collective-permute-start.14 = (bf16[192,640]{1,0:T(8,128)(2,1)S(1)}, bf16[192,640]{1,0:T(8,128)(2,1)S(1)}, u32[]{:S(2)}, u32[]{:S(2)}) collective-permute-start(bf16[192,640]{1,0:T(8,128)(2,1)S(1)} %get-tuple-element.47), channel_id=1, source_target_pairs={{0,3},{1,2},{2,1},{3,0},{4,7},{5,6},{6,5},{7,4},{8,11},{9,10},{10,... | collective-permute-start | bytes 737288 | tf_op jit(solution)/shard_map/ppermute | solution.py:485
  58.8 9.6 %collective-permute-start.10 = (bf16[96,640]{1,0:T(8,128)(2,1)S(1)}, bf16[96,640]{1,0:T(8,128)(2,1)S(1)}, u32[]{:S(2)}, u32[]{:S(2)}) collective-permute-start(bf16[96,640]{1,0:T(8,128)(2,1)S(1)} %get-tuple-element.42), channel_id=1, source_target_pairs={{0,4},{4,0},{8,12},{12,8},{16,20},{20,16},{24,28},{28,24},{1,5},{5... | collective-permute-start | bytes 368648 | tf_op jit(solution)/shard_map/ppermute | solution.py:494
  59.4 9.0 %collective-permute-start.11 = (bf16[96,640]{1,0:T(8,128)(2,1)S(1)}, bf16[96,640]{1,0:T(8,128)(2,1)S(1)}, u32[]{:S(2)}, u32[]{:S(2)}) collective-permute-start(bf16[96,640]{1,0:T(8,128)(2,1)S(1)} %get-tuple-element.43), channel_id=1, source_target_pairs={{4,8},{12,16},{20,24},{0,0},{8,4},{16,12},{24,20},{28,28},{5,9},{1... | collective-permute-start | bytes 368648 | tf_op jit(solution)/shard_map/ppermute | solution.py:493
  70.1 5.6 %collective-permute-start.15 = (bf16[96,640]{1,0:T(8,128)(2,1)S(1)}, bf16[96,640]{1,0:T(8,128)(2,1)S(1)}, u32[]{:S(2)}, u32[]{:S(2)}) collective-permute-start(bf16[96,640]{1,0:T(8,128)(2,1)S(1)} %get-tuple-element.49), channel_id=1, source_target_pairs={{0,4},{4,0},{8,12},{12,8},{16,20},{20,16},{24,28},{28,24},{1,5},{5... | collective-permute-start | bytes 368648 | tf_op jit(solution)/shard_map/ppermute | solution.py:494
  71.2 7.8 %collective-permute-start.16 = (bf16[96,640]{1,0:T(8,128)(2,1)S(1)}, bf16[96,640]{1,0:T(8,128)(2,1)S(1)}, u32[]{:S(2)}, u32[]{:S(2)}) collective-permute-start(bf16[96,640]{1,0:T(8,128)(2,1)S(1)} %get-tuple-element.50), channel_id=1, source_target_pairs={{4,8},{12,16},{20,24},{0,0},{8,4},{16,12},{24,20},{28,28},{5,9},{1... | collective-permute-start | bytes 368648 | tf_op jit(solution)/shard_map/ppermute | solution.py:493

commit v5 on v4

--- a/solution.py
+++ b/solution.py
@@ -16,7 +16,7 @@
 TILE = 256
 PAIRS = 8
 GROUP = 4
-AHEAD = 2
+AHEAD = 7
 
 courant_max = 0.45
 
@@ -175,8 +175,7 @@
         if fetches:
             fetch(step + ahead, lax.rem(step + ahead, buffers))
         lane = lax.broadcasted_iota(jnp.int32, (half, CHUNK), 1)
-        sign = jnp.where(lane % 2 == 0, 1.0, -1.0)
-        results = []
+        sign = jnp.where(lane % 2 == 0, 1.0, -1.0).astype(jnp.bfloat16)
         for pair in range(pairs):
             index = step * pairs + pair
             first, second, edge = plan(index)
@@ -187,29 +186,27 @@
                 block = jnp.where(inside, t, t - edge)
                 start = pl.multiple_of(block * CHUNK, CHUNK)
                 length = jnp.where(inside, first, second) - start
-                values = basis_held[now, local, :, pl.ds(start, CHUNK)].astype(jnp.float32)
-                values = jnp.where(lane < length, values, 0.0)
-                north_first = values * jnp.where(inside, 1.0, 0.0)
-                north_second = values - north_first
-                parts = [north_first, north_first * sign, north_second, north_second * sign]
-                columns.append(jnp.concatenate(parts, axis=0).astype(jnp.bfloat16))
+                values = basis_held[now, local, :, pl.ds(start, CHUNK)]
+                own = jnp.where(inside, length, 0)
+                own_mask = jnp.where(lane < own, 1.0, 0.0).astype(jnp.bfloat16)
+                other_mask = jnp.where(lane < length - own, 1.0, 0.0).astype(jnp.bfloat16)
+                flip = values * sign
+                columns.append(
+                    jnp.concatenate([values * own_mask, flip * own_mask, values * other_mask, flip * other_mask], axis=0)
+                )
             result = lax.dot_general(
                 jnp.concatenate(columns, axis=1),
                 held[now, pair],
                 (((1,), (1,)), ((), ())),
                 preferred_element_type=jnp.float32,
             )
-            results.append(result.astype(jnp.bfloat16))
-            if len(results) == GROUP:
-                slot = pl.multiple_of(2 * (index - (GROUP - 1)), many)
-                ordered = jnp.dot(
-                    order[...], jnp.concatenate(results, axis=0), preferred_element_type=jnp.float32
-                )
-                results = []
+            for which in range(2):
+                part = result[which * 2 * half : (which + 1) * 2 * half]
                 for low in range(0, rows, LANES):
                     width = min(LANES, rows - low)
-                    part = ordered[:, low : low + width].reshape(2 * half, many, width)
-                    sums[low // LANES, :, pl.ds(slot, many), :width] = part
+                    sums[low // LANES, pl.ds(2 * index + which, 2 * half, stride=slots), :width] = (
+                        part[:, low : low + width]
+                    )
 
     lax.fori_loop(0, steps - ahead, lambda step, _: work(step, True), None)
     lax.fori_loop(steps - ahead, steps, lambda step, _: work(step, False), None)
@@ -219,7 +216,7 @@
             lat = (place ^ d) * lats + l
             row = jnp.where(lat < half, lat, 3 * half - 1 - lat)
             turned = [
-                sums[low // LANES, row].T.astype(jnp.bfloat16) for low in range(0, rows, LANES)
+                sums[low // LANES, pl.ds(pl.multiple_of(row * slots, slots), slots), :].T.astype(jnp.bfloat16) for low in range(0, rows, LANES)
             ]
             whole = jnp.concatenate(turned, axis=0)
             for f in range(FIELDS):
@@ -248,7 +245,7 @@
             pltpu.VMEM((AHEAD + 1, PAIRS, rows, chunks * CHUNK), jnp.bfloat16),
             pltpu.VMEM((AHEAD + 1, 2 * PAIRS, half, degrees), jnp.bfloat16),
             pltpu.VMEM((GROUP * 4 * half, GROUP * 4 * half), jnp.bfloat16),
-            pltpu.VMEM((tiles, 2 * half, slots, LANES), jnp.float32),
+            pltpu.VMEM((tiles, 2 * half * slots, LANES), jnp.float32),
             pltpu.SemaphoreType.DMA((AHEAD + 1,)),
         ],
         compiler_params=pltpu.CompilerParams(vmem_limit_bytes=58 << 20),
@@ -411,58 +408,76 @@
     )
 
 
-def stepped(lat, odd_ref, end_ref, tracer_ref, pair_ref, diagonal_ref, courant_x, courant_y):
-    lats, _, width = tracer_ref.shape
-    center = tracer_ref[lat]
-
-    def outside(takes_pair):
-        pair = pair_ref[...].astype(jnp.float32)
-        diagonal = jnp.where(end_ref[0] == 1, 0.0, diagonal_ref[...].astype(jnp.float32))
-        return jnp.where(odd_ref[0] == takes_pair, pair, diagonal)
-
-    northern = tracer_ref[lat - 1] if lat > 0 else outside(1)
-    southern = tracer_ref[lat + 1] if lat < lats - 1 else outside(0)
-    return upwind(
-        center,
-        pltpu.roll(center, 1, 1),
-        pltpu.roll(center, width - 1, 1),
-        northern,
-        southern,
-        courant_x,
-        courant_y,
-    )
-
-
-def first_step_kernel(
+def row_step(center, northern, southern, courant_x, courant_y):
+    width = center.shape[1]
+    western, eastern = pltpu.roll(center, 1, 1), pltpu.roll(center, width - 1, 1)
+    return upwind(center, western, eastern, northern, southern, courant_x, courant_y)
+
+
+def outside(takes_pair, odd_ref, end_ref, pair_ref, diagonal_ref):
+    pair = pair_ref[...].astype(jnp.float32)
+    diagonal = jnp.where(end_ref[0] == 1, 0.0, diagonal_ref[...].astype(jnp.float32))
+    return jnp.where(odd_ref[0] == takes_pair, pair, diagonal)
+
+
+def courants(lev_ref, vertical_ref, blocks, gathered, lats, modes):
+    terms = three_terms(vertical_ref[...])
+
+    def of(field, lat):
+        base = (field * lats + lat) * modes
+        velocity = levels_of(terms, lev_ref[0], blocks, gathered.at[field], base, modes)
+        return courant_max * jnp.tanh(velocity)
+
+    return of
+
+
+def edge_step_kernel(
     modes, odd_ref, end_ref, lev_ref, vertical_ref, tracer_ref, pair_ref, diagonal_ref, *refs
 ):
     blocks, (x_ref, y_ref, out_ref, next_pair_ref, next_diagonal_ref, gathered) = refs[:-6], refs[-6:]
-    terms = three_terms(vertical_ref[...])
     lats = tracer_ref.shape[0]
-
-    def courant(field, lat):
-        base = (field * lats + lat) * modes
-        velocity = levels_of(terms, lev_ref[0], blocks, gathered.at[field], base, modes)
-        return courant_max * jnp.tanh(velocity)
-
-    for lat in (0, lats - 1, *range(1, lats - 1)):
-        courant_x, courant_y = courant(0, lat), courant(1, lat)
-        x_ref[lat] = courant_x
-        y_ref[lat] = courant_y
-        values = stepped(
-            lat, odd_ref, end_ref, tracer_ref, pair_ref, diagonal_ref, courant_x, courant_y
+    courant = courants(lev_ref, vertical_ref, blocks, gathered, lats, modes)
+    for place, lat in enumerate((0, lats - 1)):
+        other = outside(1 - place, odd_ref, end_ref, pair_ref, diagonal_ref)
+        northern = other if place == 0 else tracer_ref[lat - 1]
+        southern = tracer_ref[lat + 1] if place == 0 else other
+        x_ref[place], y_ref[place] = courant(0, lat), courant(1, lat)
+        values = row_step(tracer_ref[lat], northern, southern, x_ref[place], y_ref[place])
+        out_ref[place] = values
+        keep_edges(lat, lats, values, odd_ref[0], next_pair_ref, next_diagonal_ref)
+
+
+def inner_steps_kernel(modes, lev_ref, vertical_ref, tracer_ref, edge_ref, *refs):
+    blocks, (inner_ref, out_ref, x_ref, y_ref, gathered) = refs[:-5], refs[-5:]
+    lats = tracer_ref.shape[0]
+    width = out_ref.shape[2]
+    courant = courants(lev_ref, vertical_ref, blocks, gathered, lats, modes)
+    inner = lats - 2
+    for place in range(inner):
+        lat = place + 1
+        x_ref[place], y_ref[place] = courant(0, lat), courant(1, lat)
+        inner_ref[place] = row_step(
+            tracer_ref[lat], tracer_ref[lat - 1], tracer_ref[lat + 1], x_ref[place], y_ref[place]
         )
-        out_ref[lat] = values
-        keep_edges(lat, lats, values, odd_ref[0], next_pair_ref, next_diagonal_ref)
-
-
-def second_step_kernel(odd_ref, end_ref, tracer_ref, pair_ref, diagonal_ref, x_ref, y_ref, out_ref):
-    width = out_ref.shape[2]
-    for lat in range(tracer_ref.shape[0]):
-        values = stepped(
-            lat, odd_ref, end_ref, tracer_ref, pair_ref, diagonal_ref, x_ref[lat], y_ref[lat]
-        )
-        out_ref[:, lat, :] = values[:, :width]
+    for place in range(inner):
+        northern = inner_ref[place - 1] if place > 0 else edge_ref[0]
+        southern = inner_ref[place + 1] if place < inner - 1 else edge_ref[1]
+        values = row_step(inner_ref[place], northern, southern, x_ref[place], y_ref[place])
+        out_ref[place] = values[:, :width]
+
+
+def last_step_kernel(
+    odd_ref, end_ref, edge_ref, inner_ref, done_ref, pair_ref, diagonal_ref, x_ref, y_ref, out_ref
+):
+    inner, _, width = done_ref.shape
+    for place in range(inner):
+        out_ref[:, place + 1, :] = done_ref[place]
+    for place in range(2):
+        other = outside(1 - place, odd_ref, end_ref, pair_ref, diagonal_ref)
+        northern = other if place == 0 else inner_ref[inner - 1]
+        southern = inner_ref[0] if place == 0 else other
+        values = row_step(edge_ref[place], northern, southern, x_ref[place], y_ref[place])
+        out_ref[:, place * (inner + 1), :] = values[:, :width]
 
 
 def local_call(kernel, outs, scratch, *operands):
@@ -520,6 +535,7 @@
 
     whole = jax.ShapeDtypeStruct((lats, levels, width + LANES), jnp.float32)
     row = jax.ShapeDtypeStruct((levels, width + LANES), jnp.bfloat16)
+    pair_of_rows = jax.ShapeDtypeStruct((2, *whole.shape[1:]), jnp.float32)
     gathered = (levs * modes, width + LANES)
     tracer, pair, diagonal = local_call(
         functools.partial(tracer_kernel, modes),
@@ -531,9 +547,9 @@
         *columns[0],
     )
     pair, diagonal = edges(pair, diagonal)
-    courant_x, courant_y, tracer, next_pair, next_diagonal = local_call(
-        functools.partial(first_step_kernel, modes),
-        (whole, whole, whole, row, row),
+    courant_x, courant_y, edge, pair, diagonal = local_call(
+        functools.partial(edge_step_kernel, modes),
+        (pair_of_rows, pair_of_rows, pair_of_rows, row, row),
         [pltpu.VMEM((2, *gathered), jnp.float32)],
         odd,
         at_end,
@@ -544,14 +560,33 @@
         diagonal,
         *columns[1],
     )
-    pair, diagonal = edges(next_pair, next_diagonal)
+    pair, diagonal = edges(pair, diagonal)
+    inner, done = local_call(
+        functools.partial(inner_steps_kernel, modes),
+        (
+            jax.ShapeDtypeStruct((lats - 2, levels, width + LANES), jnp.float32),
+            jax.ShapeDtypeStruct((lats - 2, levels, width), jnp.float32),
+        ),
+        [
+            pltpu.VMEM((lats - 2, levels, width + LANES), jnp.float32),
+            pltpu.VMEM((lats - 2, levels, width + LANES), jnp.float32),
+            pltpu.VMEM((2, *gathered), jnp.float32),
+        ],
+        lev_place,
+        vertical,
+        tracer,
+        edge,
+        *columns[1],
+    )
     return local_call(
-        second_step_kernel,
+        last_step_kernel,
         jax.ShapeDtypeStruct((levels, lats, width), jnp.float32),
         [],
         odd,
         at_end,
-        tracer,
+        edge,
+        inner,
+        done,
         pair,
         diagonal,
         courant_x,
@@ -573,7 +608,7 @@
         and levs & (levs - 1) == 0
         and NLON // levs % TILE == 0
         and levs % 2 == 0
-        and 2 * legendre.shape[2] // waves >= 2
+        and 2 * legendre.shape[2] // waves >= 3
     )
     form = tiled_body if tiled else plain_body
     return form(spectrum, legendre, wave_numbers, vertical)

time: 81.1 us -> 78.7 us (0.970)
  Pallas kernels: 25.4 us -> 24.1 us
  waiting for transfers between devices: 34.8 us -> 33.8 us
    pallas_call x1, Pallas kernels: 16.2 us -> 15 us  [legendre_stage(): pl.pallas_call(legendre_kernel, out_shape=[jax.ShapeDtypeStruct((FIELDS,...]
    ppermute x2, waiting for transfers between devices: 2.53 us -> 1.54 us  [edges(): pair = lax.ppermute(pair, 'wave', [(i, i ^ 1) for i in range(count)])]
    pallas_call x3 -> x4, Pallas kernels: 4.32 us -> 4.21 us  [local_call(): pl.pallas_call(kernel, out_shape=outs, in_specs=[smem if operand.dtype ==...]
  transfers between devices with their start and end apart: 17 -> 17, of which waited for: 10 -> 10; matrix products, arithmetic and copies ran while one was open for 3% -> 3% of each run, Pallas kernels for 6% -> 7%
where the time goes in v5:
time: 78.7 us; the launch traced here: 78.5 us
  waiting for transfers between devices  33.8 us (43%)
  Pallas kernels  24.1 us (31%)
  starting transfers between devices  18 us (23%)
  other arithmetic  2.3 us (3%)
    ppermute x13, waiting for transfers between devices, exchange(): lax.ppermute(blocks[d], axis, [(i, i ^ d) for i in range(count)])  29.1 us
    pallas_call x1, Pallas kernels, legendre_stage(): pl.pallas_call(legendre_kernel, out_shape=[jax.ShapeDtypeStruct((FIELDS,...  15 us
    ppermute x13, starting transfers between devices, exchange(): lax.ppermute(blocks[d], axis, [(i, i ^ d) for i in range(count)])  11.8 us
    ppermute x2, starting transfers between devices, edges(): diagonal = lax.ppermute(diagonal, 'wave', steps)  4.55 us
    pallas_call x4, Pallas kernels, local_call(): pl.pallas_call(kernel, out_shape=outs, in_specs=[smem if operand.dtype ==...  4.21 us
    ppermute x2, waiting for transfers between devices, edges(): diagonal = lax.ppermute(diagonal, 'wave', steps)  3.22 us
    pallas_call x2, Pallas kernels, synthesis_stage(): pl.pallas_call(functools.partial(synthesis_kernel, waves, levs, fields),...  3.07 us
    mul x1, other arithmetic, twiddle_stage(): weight * jnp.sin(low)  2.14 us
  transfers between devices with their start and end apart: 17, of which 10 were waited for; matrix products, arithmetic and copies ran while one was open for 3% of the time, Pallas kernels for 7%

profile of v5, /device:TPU:16, one launch (start us, length us, event | category | flops | bytes accessed | tf_op | source)
XLA Modules:
  0.0 78.5 jit_solution(16191425755455938139)
XLA Ops:
  0.0 0.0 copy-start.2
  0.0 15.0 %legendre_sums.1 = (bf16[3,2,4,24,128]{4,3,2,1,0:T(8,128)(2,1)}, bf16[3,2,4,24,128]{4,3,2,1,0:T(8,128)(2,1)}, bf16[3,2,4,24,128]{4,3,2,1,0:T(8,128)(2,1)}, bf16[...) custom-call(s32[1024]{0:T(1024)} %numbers_ref.1, ...), custom_call_target="tpu_custom_call" | custom-call | flops 603979776 | bytes 18874368 | tf_op jit(solution)/shard_map/legendre_sums/pallas_call | solution.py:239
  15.0 0.0 copy-start.1
  15.0 1.6 %collective-permute-start = (bf16[3,2,4,24,128]{4,3,2,1,0:T(8,128)(2,1)}, bf16[3,2,4,24,128]{4,3,2,1,0:T(8,128)(2,1)S(1)}, u32[]{:S(2)}, u32[]{:S(2)}) collective-permute-start(bf16[3,2,4,24,128]{4,3,2,1,0:T(8,128)(2,1)} %get-tuple-element.32), channel_id=1, source_target_pairs={{0,4},{4,0},{8,12},{12,8},{16,20},{20,16},{24,28},{28,24},{1,5},{5... | collective-permute-start | bytes 442376 | tf_op jit(solution)/shard_map/ppermute | solution.py:500
  16.5 1.6 %collective-permute-start.1 = (bf16[3,2,4,24,128]{4,3,2,1,0:T(8,128)(2,1)}, bf16[3,2,4,24,128]{4,3,2,1,0:T(8,128)(2,1)S(1)}, u32[]{:S(2)}, u32[]{:S(2)}) collective-permute-start(bf16[3,2,4,24,128]{4,3,2,1,0:T(8,128)(2,1)} %get-tuple-element.33), channel_id=1, source_target_pairs={{0,8},{4,12},{8,0},{12,4},{16,24},{20,28},{24,16},{28,20},{1,9},{5... | collective-permute-start | bytes 442376 | tf_op jit(solution)/shard_map/ppermute | solution.py:500
  18.1 0.4 collective-permute-start.2
  18.5 0.0 collective-permute-start.3
  18.5 3.9 %collective-permute-start.4 = (bf16[3,2,4,24,128]{4,3,2,1,0:T(8,128)(2,1)}, bf16[3,2,4,24,128]{4,3,2,1,0:T(8,128)(2,1)S(1)}, u32[]{:S(2)}, u32[]{:S(2)}) collective-permute-start(bf16[3,2,4,24,128]{4,3,2,1,0:T(8,128)(2,1)} %get-tuple-element.36), channel_id=1, source_target_pairs={{0,20},{4,16},{8,28},{12,24},{16,4},{20,0},{24,12},{28,8},{1,21},{... | collective-permute-start | bytes 442376 | tf_op jit(solution)/shard_map/ppermute | solution.py:500
  22.4 0.0 copy-done.2
  22.4 0.2 fusion.11
  22.6 0.1 cos.7.turn_cos_ref
  22.7 0.0 collective-permute-done.refs_1_
  22.7 0.5 collective-permute-start.5
  23.2 3.1 %collective-permute-done.1.refs_2_ = bf16[3,2,4,24,128]{4,3,2,1,0:T(8,128)(2,1)S(1)} collective-permute-done((bf16[3,2,4,24,128]{4,3,2,1,0:T(8,128)(2,1)}, bf16[3,2,4,24,128]{4,3,2,1,0:T(8,128)(2,1)S(1)}, u32[]{:S(2)}, u32[]{:S(2)}) %collective-permute-start.1) | collective-permute-done | bytes 147488 | tf_op jit(solution)/shard_map/ppermute | solution.py:500
  26.4 0.0 collective-permute-start.6
  26.4 2.1 %sine_multiply_fusion = (f32[8,128,128]{2,1,0:T(8,128)S(1)}, f32[8,128,128]{2,1,0:T(8,128)S(1)}) fusion(s32[8,128]{1,0:T(8,128)S(1)} %bitcast.14, f32[8,128]{1,0:T(8,128)S(1)} %compare_select_fusion.5), kind=kLoop, calls=%fused_computation.6 | loop fusion | flops 2097152 | bytes 1056768 | tf_op jit(solution)/shard_map/mul | solution.py:296
  28.5 1.8 %twiddles.1.refs_9_ = bf16[8,2,128,1024]{3,2,1,0:T(8,128)(2,1)S(1)} custom-call(s32[1]{0:T(128)} %bitcast.3.place_ref.wave_ref, f32[8,128,128]{2,1,0:T(8,128)S(1)} %get-tuple-element.60.low_cos_ref, f32[8,128,128]{2,1,0:T(8,128)S(1)} %get-tuple-element.59.low_sin_ref, f32[8,1,128]{2,1,0:T(1,128)S(1)} %cos.7.turn_cos_ref, ...), custom_call_target="tpu_custom_call" | custom-call | flops 8388608 | bytes 4194304 | tf_op jit(solution)/shard_map/twiddles/pallas_call | solution.py:284
  30.3 0.0 collective-permute-done.2.refs_3_
  30.3 0.0 collective-permute-done.3.refs_4_
  30.4 8.8 %collective-permute-done.4.refs_5_ = bf16[3,2,4,24,128]{4,3,2,1,0:T(8,128)(2,1)S(1)} collective-permute-done((bf16[3,2,4,24,128]{4,3,2,1,0:T(8,128)(2,1)}, bf16[3,2,4,24,128]{4,3,2,1,0:T(8,128)(2,1)S(1)}, u32[]{:S(2)}, u32[]{:S(2)}) %collective-permute-start.4) | collective-permute-done | bytes 147488 | tf_op jit(solution)/shard_map/ppermute | solution.py:500
  39.1 5.9 %collective-permute-done.5.refs_6_ = bf16[3,2,4,24,128]{4,3,2,1,0:T(8,128)(2,1)S(1)} collective-permute-done((bf16[3,2,4,24,128]{4,3,2,1,0:T(8,128)(2,1)}, bf16[3,2,4,24,128]{4,3,2,1,0:T(8,128)(2,1)S(1)}, u32[]{:S(2)}, u32[]{:S(2)}) %collective-permute-start.5) | collective-permute-done | bytes 147488 | tf_op jit(solution)/shard_map/ppermute | solution.py:500
  45.1 2.5 %collective-permute-done.6.refs_7_ = bf16[3,2,4,24,128]{4,3,2,1,0:T(8,128)(2,1)S(1)} collective-permute-done((bf16[3,2,4,24,128]{4,3,2,1,0:T(8,128)(2,1)}, bf16[3,2,4,24,128]{4,3,2,1,0:T(8,128)(2,1)S(1)}, u32[]{:S(2)}, u32[]{:S(2)}) %collective-permute-start.6) | collective-permute-done | bytes 147488 | tf_op jit(solution)/shard_map/ppermute | solution.py:500
  47.6 0.0 copy-done.1
  47.6 1.1 %synthesis.2 = (bf16[96,640]{1,0:T(8,128)(2,1)S(1)}, bf16[96,640]{1,0:T(8,128)(2,1)S(1)}, bf16[96,640]{1,0:T(8,128)(2,1)S(1)}, bf16[96,640]{1,0:T(8,128)(2,1)S(1)}) custom-call(s32[1]{0:T(128)} %bitcast.3.place_ref.wave_ref, s32[1]{0:T(128)} %bitcast.2.lev_ref, bf16[3,2,4,24,128]{4,3,2,1,0:T(8,128)(2,1)S(1)} %copy-done.1, ...), custom_call_target="tpu_custom_call" | custom-call | flops 805306368 | bytes 4194304 | tf_op jit(solution)/shard_map/synthesis/pallas_call | solution.py:343
  48.7 0.0 copy-start
  48.7 0.1 collective-permute-start.7
  48.8 1.6 %collective-permute-start.8 = (bf16[96,640]{1,0:T(8,128)(2,1)S(1)}, bf16[96,640]{1,0:T(8,128)(2,1)S(1)}, u32[]{:S(2)}, u32[]{:S(2)}) collective-permute-start(bf16[96,640]{1,0:T(8,128)(2,1)S(1)} %get-tuple-element.41), channel_id=1, source_target_pairs={{0,2},{1,3},{2,0},{3,1},{4,6},{5,7},{6,4},{7,5},{8,10},{9,11},{10,... | collective-permute-start | bytes 368648 | tf_op jit(solution)/shard_map/ppermute | solution.py:500
  50.4 0.3 collective-permute-start.9
  50.7 2.0 %synthesis.3 = (bf16[192,640]{1,0:T(8,128)(2,1)S(1)}, bf16[192,640]{1,0:T(8,128)(2,1)S(1)}, bf16[192,640]{1,0:T(8,128)(2,1)S(1)}, bf16[192,640]{1,0:T(8,128)(2,1)S(1)}) custom-call(s32[1]{0:T(128)} %bitcast.3.place_ref.wave_ref, s32[1]{0:T(128)} %bitcast.2.lev_ref, bf16[3,2,4,24,128]{4,3,2,1,0:T(8,128)(2,1)S(1)} %copy-done.1, ...), custom_call_target="tpu_custom_call" | custom-call | flops 1610612736 | bytes 4194304 | tf_op jit(solution)/shard_map/synthesis/pallas_call | solution.py:343
  52.6 0.4 collective-permute-start.12
  53.1 1.5 %collective-permute-start.13 = (bf16[192,640]{1,0:T(8,128)(2,1)S(1)}, bf16[192,640]{1,0:T(8,128)(2,1)S(1)}, u32[]{:S(2)}, u32[]{:S(2)}) collective-permute-start(bf16[192,640]{1,0:T(8,128)(2,1)S(1)} %get-tuple-element.48), channel_id=1, source_target_pairs={{0,2},{1,3},{2,0},{3,1},{4,6},{5,7},{6,4},{7,5},{8,10},{9,11},{10,... | collective-permute-start | bytes 737288 | tf_op jit(solution)/shard_map/ppermute | solution.py:500
  54.6 0.0 collective-permute-done.7.refs_1_
  54.6 0.0 collective-permute-start.14
  54.6 0.5 collective-permute-done.8.refs_2_
  55.1 1.7 %collective-permute-done.9.refs_3_ = bf16[96,640]{1,0:T(8,128)(2,1)S(1)} collective-permute-done((bf16[96,640]{1,0:T(8,128)(2,1)S(1)}, bf16[96,640]{1,0:T(8,128)(2,1)S(1)}, u32[]{:S(2)}, u32[]{:S(2)}) %collective-permute-start.9) | collective-permute-done | bytes 122912 | tf_op jit(solution)/shard_map/ppermute | solution.py:500
  56.7 0.0 copy-done
  56.7 0.8 shard_map.46
  57.5 0.6 collective-permute-start.10
  58.1 2.5 %collective-permute-start.11 = (bf16[96,640]{1,0:T(8,128)(2,1)S(1)}, bf16[96,640]{1,0:T(8,128)(2,1)S(1)}, u32[]{:S(2)}, u32[]{:S(2)}) collective-permute-start(bf16[96,640]{1,0:T(8,128)(2,1)S(1)} %get-tuple-element.45), channel_id=1, source_target_pairs={{4,8},{12,16},{20,24},{0,0},{8,4},{16,12},{24,20},{28,28},{5,9},{1... | collective-permute-start | bytes 368648 | tf_op jit(solution)/shard_map/ppermute | solution.py:508
  60.6 0.0 collective-permute-done.12.refs_1_
  60.6 2.3 %collective-permute-done.13.refs_2_ = bf16[192,640]{1,0:T(8,128)(2,1)S(1)} collective-permute-done((bf16[192,640]{1,0:T(8,128)(2,1)S(1)}, bf16[192,640]{1,0:T(8,128)(2,1)S(1)}, u32[]{:S(2)}, u32[]{:S(2)}) %collective-permute-start.13) | collective-permute-done | bytes 245792 | tf_op jit(solution)/shard_map/ppermute | solution.py:500
  63.0 4.2 %collective-permute-done.14.refs_3_ = bf16[192,640]{1,0:T(8,128)(2,1)S(1)} collective-permute-done((bf16[192,640]{1,0:T(8,128)(2,1)S(1)}, bf16[192,640]{1,0:T(8,128)(2,1)S(1)}, u32[]{:S(2)}, u32[]{:S(2)}) %collective-permute-start.14) | collective-permute-done | bytes 245792 | tf_op jit(solution)/shard_map/ppermute | solution.py:500
  67.2 0.0 collective-permute-done.10.pair_ref
  67.2 0.0 collective-permute-done.11.diagonal_ref
  67.2 0.9 %shard_map.47 = (f32[2,96,640]{2,1,0:T(8,128)S(1)}, f32[2,96,640]{2,1,0:T(8,128)S(1)}, f32[2,96,640]{2,1,0:T(8,128)S(1)}, bf16[96,640]{1,0:T(8,128)(2,1)S(1)}, bf16[96,640]{1,0:T(8,128)(2,1)S(1)}) custom-call(s32[1]{0:T(128)} %bitcast.odd_ref, s32[1]{0:T(128)} %bitcast.1.end_ref, s32[1]{0:T(128)} %bitcast.2.lev_ref, f32[96,96]{1,0:T(8,128)S(1)} %copy-done, ...), custom_call_target="tpu_custom_call" | custom-call | flops 4000000 | bytes 4000000 | tf_op jit(solution)/shard_map/pallas_call | solution.py:485
  68.1 1.0 %collective-permute-start.15 = (bf16[96,640]{1,0:T(8,128)(2,1)S(1)}, bf16[96,640]{1,0:T(8,128)(2,1)S(1)}, u32[]{:S(2)}, u32[]{:S(2)}) collective-permute-start(bf16[96,640]{1,0:T(8,128)(2,1)S(1)} %get-tuple-element.53), channel_id=1, source_target_pairs={{0,4},{4,0},{8,12},{12,8},{16,20},{20,16},{24,28},{28,24},{1,5},{5... | collective-permute-start | bytes 368648 | tf_op jit(solution)/shard_map/ppermute | solution.py:509
  69.1 2.1 %collective-permute-start.16 = (bf16[96,640]{1,0:T(8,128)(2,1)S(1)}, bf16[96,640]{1,0:T(8,128)(2,1)S(1)}, u32[]{:S(2)}, u32[]{:S(2)}) collective-permute-start(bf16[96,640]{1,0:T(8,128)(2,1)S(1)} %get-tuple-element.54), channel_id=1, source_target_pairs={{4,8},{12,16},{20,24},{0,0},{8,4},{16,12},{24,20},{28,28},{5,9},{1... | collective-permute-start | bytes 368648 | tf_op jit(solution)/shard_map/ppermute | solution.py:508
  71.2 1.0 %shard_map.48 = (f32[2,96,640]{2,1,0:T(8,128)S(1)}, f32[2,96,512]{2,1,0:T(8,128)S(1)}) custom-call(s32[1]{0:T(128)} %bitcast.2.lev_ref, f32[96,96]{1,0:T(8,128)S(1)} %copy-done, f32[4,96,640]{2,1,0:T(8,128)S(1)} %get-tuple-element.43.tracer_ref, f32[2,96,640]{2,1,0:T(8,128)S(1)} %get-tuple-element.50.edge_ref, ...), custom_call_target="tpu_custom_call" | custom-call | flops 4000000 | bytes 4000000 | tf_op jit(solution)/shard_map/pallas_call | solution.py:485
  72.2 1.5 %collective-permute-done.15.pair_ref = bf16[96,640]{1,0:T(8,128)(2,1)S(1)} collective-permute-done((bf16[96,640]{1,0:T(8,128)(2,1)S(1)}, bf16[96,640]{1,0:T(8,128)(2,1)S(1)}, u32[]{:S(2)}, u32[]{:S(2)}) %collective-permute-start.15) | collective-permute-done | bytes 122912 | tf_op jit(solution)/shard_map/ppermute | solution.py:509
  73.8 3.2 %collective-permute-done.16.diagonal_ref = bf16[96,640]{1,0:T(8,128)(2,1)S(1)} collective-permute-done((bf16[96,640]{1,0:T(8,128)(2,1)S(1)}, bf16[96,640]{1,0:T(8,128)(2,1)S(1)}, u32[]{:S(2)}, u32[]{:S(2)}) %collective-permute-start.16) | collective-permute-done | bytes 122912 | tf_op jit(solution)/shard_map/ppermute | solution.py:508
  77.0 1.5 %shard_map.49 = f32[96,4,512]{2,1,0:T(4,128)} custom-call(s32[1]{0:T(128)} %bitcast.odd_ref, s32[1]{0:T(128)} %bitcast.1.end_ref, f32[2,96,640]{2,1,0:T(8,128)S(1)} %get-tuple-element.50.edge_ref, f32[2,96,640]{2,1,0:T(8,128)S(1)} %get-tuple-element.51.inner_ref, f32[2,96,512]{2,1,0:T(8,128)S(1)} %get-tuple-element.52.done_ref, ...), custom_call_target="tpu_custom_call" | custom-call | flops 4000000 | bytes 4000000 | tf_op jit(solution)/shard_map/pallas_call | solution.py:485
  (1 shorter events, 0.0 us)
Async XLA Ops:
  0.0 22.4 %copy-start.2 = (s32[1024]{0:T(1024)S(1)}, s32[1024]{0:T(1024)}, u32[]{:S(2)}) copy-start(s32[1024]{0:T(1024)} %numbers_ref.1) | copy-start | bytes 12292
  15.0 32.6 %copy-start.1 = (bf16[3,2,4,24,128]{4,3,2,1,0:T(8,128)(2,1)S(1)}, bf16[3,2,4,24,128]{4,3,2,1,0:T(8,128)(2,1)}, u32[]{:S(2)}) copy-start(bf16[3,2,4,24,128]{4,3,2,1,0:T(8,128)(2,1)} %get-tuple-element.31.refs_0_) | copy-start | bytes 442372
  15.0 7.7 %collective-permute-start = (bf16[3,2,4,24,128]{4,3,2,1,0:T(8,128)(2,1)}, bf16[3,2,4,24,128]{4,3,2,1,0:T(8,128)(2,1)S(1)}, u32[]{:S(2)}, u32[]{:S(2)}) collective-permute-start(bf16[3,2,4,24,128]{4,3,2,1,0:T(8,128)(2,1)} %get-tuple-element.32), channel_id=1, source_target_pairs={{0,4},{4,0},{8,12},{12,8},{16,20},{20,16},{24,28},{28,24},{1,5},{5... | collective-permute-start | bytes 442376 | tf_op jit(solution)/shard_map/ppermute | solution.py:500
  16.5 9.8 %collective-permute-start.1 = (bf16[3,2,4,24,128]{4,3,2,1,0:T(8,128)(2,1)}, bf16[3,2,4,24,128]{4,3,2,1,0:T(8,128)(2,1)S(1)}, u32[]{:S(2)}, u32[]{:S(2)}) collective-permute-start(bf16[3,2,4,24,128]{4,3,2,1,0:T(8,128)(2,1)} %get-tuple-element.33), channel_id=1, source_target_pairs={{0,8},{4,12},{8,0},{12,4},{16,24},{20,28},{24,16},{28,20},{1,9},{5... | collective-permute-start | bytes 442376 | tf_op jit(solution)/shard_map/ppermute | solution.py:500
  18.1 12.2 %collective-permute-start.2 = (bf16[3,2,4,24,128]{4,3,2,1,0:T(8,128)(2,1)}, bf16[3,2,4,24,128]{4,3,2,1,0:T(8,128)(2,1)S(1)}, u32[]{:S(2)}, u32[]{:S(2)}) collective-permute-start(bf16[3,2,4,24,128]{4,3,2,1,0:T(8,128)(2,1)} %get-tuple-element.34), channel_id=1, source_target_pairs={{0,12},{4,8},{8,4},{12,0},{16,28},{20,24},{24,20},{28,16},{1,13},{... | collective-permute-start | bytes 442376 | tf_op jit(solution)/shard_map/ppermute | solution.py:500
  18.5 11.8 %collective-permute-start.3 = (bf16[3,2,4,24,128]{4,3,2,1,0:T(8,128)(2,1)}, bf16[3,2,4,24,128]{4,3,2,1,0:T(8,128)(2,1)S(1)}, u32[]{:S(2)}, u32[]{:S(2)}) collective-permute-start(bf16[3,2,4,24,128]{4,3,2,1,0:T(8,128)(2,1)} %get-tuple-element.35), channel_id=1, source_target_pairs={{0,16},{4,20},{8,24},{12,28},{16,0},{20,4},{24,8},{28,12},{1,17},{... | collective-permute-start | bytes 442376 | tf_op jit(solution)/shard_map/ppermute | solution.py:500
  18.5 20.6 %collective-permute-start.4 = (bf16[3,2,4,24,128]{4,3,2,1,0:T(8,128)(2,1)}, bf16[3,2,4,24,128]{4,3,2,1,0:T(8,128)(2,1)S(1)}, u32[]{:S(2)}, u32[]{:S(2)}) collective-permute-start(bf16[3,2,4,24,128]{4,3,2,1,0:T(8,128)(2,1)} %get-tuple-element.36), channel_id=1, source_target_pairs={{0,20},{4,16},{8,28},{12,24},{16,4},{20,0},{24,12},{28,8},{1,21},{... | collective-permute-start | bytes 442376 | tf_op jit(solution)/shard_map/ppermute | solution.py:500
  22.7 22.4 %collective-permute-start.5 = (bf16[3,2,4,24,128]{4,3,2,1,0:T(8,128)(2,1)}, bf16[3,2,4,24,128]{4,3,2,1,0:T(8,128)(2,1)S(1)}, u32[]{:S(2)}, u32[]{:S(2)}) collective-permute-start(bf16[3,2,4,24,128]{4,3,2,1,0:T(8,128)(2,1)} %get-tuple-element.37), channel_id=1, source_target_pairs={{0,24},{4,28},{8,16},{12,20},{16,8},{20,12},{24,0},{28,4},{1,25},{... | collective-permute-start | bytes 442376 | tf_op jit(solution)/shard_map/ppermute | solution.py:500
  26.4 21.2 %collective-permute-start.6 = (bf16[3,2,4,24,128]{4,3,2,1,0:T(8,128)(2,1)}, bf16[3,2,4,24,128]{4,3,2,1,0:T(8,128)(2,1)S(1)}, u32[]{:S(2)}, u32[]{:S(2)}) collective-permute-start(bf16[3,2,4,24,128]{4,3,2,1,0:T(8,128)(2,1)} %get-tuple-element.38), channel_id=1, source_target_pairs={{0,28},{4,24},{8,20},{12,16},{16,12},{20,8},{24,4},{28,0},{1,29},{... | collective-permute-start | bytes 442376 | tf_op jit(solution)/shard_map/ppermute | solution.py:500
  48.7 8.0 %copy-start = (f32[96,96]{1,0:T(8,128)S(1)}, f32[96,96]{1,0:T(8,128)}, u32[]{:S(2)}) copy-start(f32[96,96]{1,0:T(8,128)} %vertical_ref.5) | copy-start | bytes 110596
  48.7 5.9 %collective-permute-start.7 = (bf16[96,640]{1,0:T(8,128)(2,1)S(1)}, bf16[96,640]{1,0:T(8,128)(2,1)S(1)}, u32[]{:S(2)}, u32[]{:S(2)}) collective-permute-start(bf16[96,640]{1,0:T(8,128)(2,1)S(1)} %get-tuple-element.40), channel_id=1, source_target_pairs={{0,1},{1,0},{2,3},{3,2},{4,5},{5,4},{6,7},{7,6},{8,9},{9,8},{10,11... | collective-permute-start | bytes 368648 | tf_op jit(solution)/shard_map/ppermute | solution.py:500
  48.8 6.3 %collective-permute-start.8 = (bf16[96,640]{1,0:T(8,128)(2,1)S(1)}, bf16[96,640]{1,0:T(8,128)(2,1)S(1)}, u32[]{:S(2)}, u32[]{:S(2)}) collective-permute-start(bf16[96,640]{1,0:T(8,128)(2,1)S(1)} %get-tuple-element.41), channel_id=1, source_target_pairs={{0,2},{1,3},{2,0},{3,1},{4,6},{5,7},{6,4},{7,5},{8,10},{9,11},{10,... | collective-permute-start | bytes 368648 | tf_op jit(solution)/shard_map/ppermute | solution.py:500
  50.4 6.3 %collective-permute-start.9 = (bf16[96,640]{1,0:T(8,128)(2,1)S(1)}, bf16[96,640]{1,0:T(8,128)(2,1)S(1)}, u32[]{:S(2)}, u32[]{:S(2)}) collective-permute-start(bf16[96,640]{1,0:T(8,128)(2,1)S(1)} %get-tuple-element.42), channel_id=1, source_target_pairs={{0,3},{1,2},{2,1},{3,0},{4,7},{5,6},{6,5},{7,4},{8,11},{9,10},{10,... | collective-permute-start | bytes 368648 | tf_op jit(solution)/shard_map/ppermute | solution.py:500
  52.6 8.0 %collective-permute-start.12 = (bf16[192,640]{1,0:T(8,128)(2,1)S(1)}, bf16[192,640]{1,0:T(8,128)(2,1)S(1)}, u32[]{:S(2)}, u32[]{:S(2)}) collective-permute-start(bf16[192,640]{1,0:T(8,128)(2,1)S(1)} %get-tuple-element.47), channel_id=1, source_target_pairs={{0,1},{1,0},{2,3},{3,2},{4,5},{5,4},{6,7},{7,6},{8,9},{9,8},{10,11... | collective-permute-start | bytes 737288 | tf_op jit(solution)/shard_map/ppermute | solution.py:500
  53.1 9.9 %collective-permute-start.13 = (bf16[192,640]{1,0:T(8,128)(2,1)S(1)}, bf16[192,640]{1,0:T(8,128)(2,1)S(1)}, u32[]{:S(2)}, u32[]{:S(2)}) collective-permute-start(bf16[192,640]{1,0:T(8,128)(2,1)S(1)} %get-tuple-element.48), channel_id=1, source_target_pairs={{0,2},{1,3},{2,0},{3,1},{4,6},{5,7},{6,4},{7,5},{8,10},{9,11},{10,... | collective-permute-start | bytes 737288 | tf_op jit(solution)/shard_map/ppermute | solution.py:500
  54.6 12.6 %collective-permute-start.14 = (bf16[192,640]{1,0:T(8,128)(2,1)S(1)}, bf16[192,640]{1,0:T(8,128)(2,1)S(1)}, u32[]{:S(2)}, u32[]{:S(2)}) collective-permute-start(bf16[192,640]{1,0:T(8,128)(2,1)S(1)} %get-tuple-element.49), channel_id=1, source_target_pairs={{0,3},{1,2},{2,1},{3,0},{4,7},{5,6},{6,5},{7,4},{8,11},{9,10},{10,... | collective-permute-start | bytes 737288 | tf_op jit(solution)/shard_map/ppermute | solution.py:500
  57.5 9.6 %collective-permute-start.10 = (bf16[96,640]{1,0:T(8,128)(2,1)S(1)}, bf16[96,640]{1,0:T(8,128)(2,1)S(1)}, u32[]{:S(2)}, u32[]{:S(2)}) collective-permute-start(bf16[96,640]{1,0:T(8,128)(2,1)S(1)} %get-tuple-element.44), channel_id=1, source_target_pairs={{0,4},{4,0},{8,12},{12,8},{16,20},{20,16},{24,28},{28,24},{1,5},{5... | collective-permute-start | bytes 368648 | tf_op jit(solution)/shard_map/ppermute | solution.py:509
  58.1 9.0 %collective-permute-start.11 = (bf16[96,640]{1,0:T(8,128)(2,1)S(1)}, bf16[96,640]{1,0:T(8,128)(2,1)S(1)}, u32[]{:S(2)}, u32[]{:S(2)}) collective-permute-start(bf16[96,640]{1,0:T(8,128)(2,1)S(1)} %get-tuple-element.45), channel_id=1, source_target_pairs={{4,8},{12,16},{20,24},{0,0},{8,4},{16,12},{24,20},{28,28},{5,9},{1... | collective-permute-start | bytes 368648 | tf_op jit(solution)/shard_map/ppermute | solution.py:508
  68.1 5.7 %collective-permute-start.15 = (bf16[96,640]{1,0:T(8,128)(2,1)S(1)}, bf16[96,640]{1,0:T(8,128)(2,1)S(1)}, u32[]{:S(2)}, u32[]{:S(2)}) collective-permute-start(bf16[96,640]{1,0:T(8,128)(2,1)S(1)} %get-tuple-element.53), channel_id=1, source_target_pairs={{0,4},{4,0},{8,12},{12,8},{16,20},{20,16},{24,28},{28,24},{1,5},{5... | collective-permute-start | bytes 368648 | tf_op jit(solution)/shard_map/ppermute | solution.py:509
  69.1 7.9 %collective-permute-start.16 = (bf16[96,640]{1,0:T(8,128)(2,1)S(1)}, bf16[96,640]{1,0:T(8,128)(2,1)S(1)}, u32[]{:S(2)}, u32[]{:S(2)}) collective-permute-start(bf16[96,640]{1,0:T(8,128)(2,1)S(1)} %get-tuple-element.54), channel_id=1, source_target_pairs={{4,8},{12,16},{20,24},{0,0},{8,4},{16,12},{24,20},{28,28},{5,9},{1... | collective-permute-start | bytes 368648 | tf_op jit(solution)/shard_map/ppermute | solution.py:508

commit v6 on v5

--- a/solution.py
+++ b/solution.py
@@ -15,7 +15,7 @@
 CHUNK = 256
 TILE = 256
 PAIRS = 8
-GROUP = 4
+HALO = 4
 AHEAD = 7
 
 courant_max = 0.45
@@ -124,7 +124,7 @@
 
 
 def legendre_kernel(numbers_ref, place_ref, spectrum_ref, legendre_ref, *refs):
-    outs, (held, basis_held, order, sums, arrived) = refs[:-5], refs[-5:]
+    outs, (held, basis_held, sums, arrived) = refs[:-4], refs[-4:]
     waves = len(outs)
     _, _, lats, modes, _ = outs[0].shape
     buffers, pairs, rows, _ = held.shape
@@ -133,7 +133,6 @@
     steps = slots // (2 * pairs)
     ahead = buffers - 1
     place = place_ref[0]
-    many = 2 * GROUP
 
     def plan(index):
         first = degrees - numbers_ref[place * slots + 2 * index]
@@ -162,11 +161,6 @@
 
     for group in range(min(ahead, steps)):
         fetch(group, group)
-
-    row = lax.broadcasted_iota(jnp.int32, order.shape, 0)
-    column = lax.broadcasted_iota(jnp.int32, order.shape, 1)
-    wanted = lax.rem(row, many) * (2 * half) + lax.div(row, many)
-    order[...] = jnp.where(column == wanted, 1.0, 0.0).astype(jnp.bfloat16)
 
     def work(step, fetches):
         now = lax.rem(step, buffers)
@@ -244,7 +238,6 @@
         scratch_shapes=[
             pltpu.VMEM((AHEAD + 1, PAIRS, rows, chunks * CHUNK), jnp.bfloat16),
             pltpu.VMEM((AHEAD + 1, 2 * PAIRS, half, degrees), jnp.bfloat16),
-            pltpu.VMEM((GROUP * 4 * half, GROUP * 4 * half), jnp.bfloat16),
             pltpu.VMEM((tiles, 2 * half * slots, LANES), jnp.float32),
             pltpu.SemaphoreType.DMA((AHEAD + 1,)),
         ],
@@ -314,7 +307,6 @@
     width = NLON // levs
     ratio = width // TILE
     steps = twiddle_ref.shape[3] // TILE
-    lane = lax.broadcasted_iota(jnp.int32, (rows, LANES), 1)
     for step in range(steps):
         right = twiddle_ref[:, :, :, pl.ds(step * TILE, TILE)]
         right = right.reshape(waves * PARTS * slots, TILE)
@@ -322,13 +314,22 @@
         result = result.astype(jnp.bfloat16)
         for which in range(2):
             owner, inner = divmod(step + which * steps, ratio)
-            grid[owner, :, pl.ds(inner * TILE, TILE)] = result[which * rows : (which + 1) * rows]
+            part = result[which * rows : (which + 1) * rows]
+            grid[owner, :rows, pl.ds(inner * TILE, TILE)] = part
+    lane = lax.broadcasted_iota(jnp.int32, (modes, LANES), 1)
     for owner in range(levs):
-        grid[owner, :, pl.ds(width, LANES)] = jnp.where(
-            lane < LANES // 2,
-            grid[(owner + 1) % levs, :, :LANES],
-            grid[(owner - 1) % levs, :, pl.ds(width - LANES, LANES)],
-        )
+        halos = jnp.zeros((modes, LANES), jnp.float32)
+        for k in range(rows // modes):
+            own = pl.ds(k * modes, modes)
+            east = grid[(owner + 1) % levs, own, :LANES]
+            west = grid[(owner - 1) % levs, own, pl.ds(width - LANES, LANES)]
+            halo = jnp.where(lane < LANES // 2, east.astype(jnp.float32), west.astype(jnp.float32))
+            turned = pltpu.roll(halo, HALO * k, 1) if k else halo
+            inside = lax.rem(lane + (LANES + HALO // 2 - HALO * k), LANES) < HALO
+            halos = jnp.where(inside, turned, halos)
+        for g in range(width // LANES):
+            part = halos[8 * g : 8 * g + 8] if 8 * g < modes else jnp.zeros((8, LANES), jnp.float32)
+            grid[owner, pl.ds(rows, 8), pl.ds(g * LANES, LANES)] = part.astype(jnp.bfloat16)
     place = lev_ref[0]
     for e in range(levs):
         outs[e][...] = grid[place ^ e]
@@ -338,16 +339,16 @@
     waves, _, slots, count = twiddle.shape
     _, _, lats, modes, _ = blocks[0].shape
     rows = lats * modes * len(fields)
-    width = NLON // levs + LANES
+    width = NLON // levs
     depth = waves * PARTS * slots
     return pl.pallas_call(
         functools.partial(synthesis_kernel, waves, levs, fields),
-        out_shape=[jax.ShapeDtypeStruct((rows, width), jnp.bfloat16)] * levs,
+        out_shape=[jax.ShapeDtypeStruct((rows + 8, width), jnp.bfloat16)] * levs,
         in_specs=[pl.BlockSpec(memory_space=pltpu.SMEM)] * 2 + [vmem()] * (waves + 2),
         out_specs=[vmem()] * levs,
         scratch_shapes=[
             pltpu.VMEM((2 * rows, depth), jnp.bfloat16),
-            pltpu.VMEM((levs, rows, width), jnp.bfloat16),
+            pltpu.VMEM((levs, rows + 8, width), jnp.bfloat16),
         ],
         compiler_params=pltpu.CompilerParams(vmem_limit_bytes=12 << 20),
         cost_estimate=cost(4 * rows * depth * count, 2 * depth * count),
@@ -367,7 +368,18 @@
     count = terms.shape[0] // 3
     for e, block in enumerate(blocks):
         start = pl.multiple_of((place ^ e) * modes, modes)
-        gathered[pl.ds(start, modes)] = block[base : base + modes].astype(jnp.float32)
+        rows, width = block.shape
+        gathered[pl.ds(start, modes), :width] = block[base : base + modes].astype(jnp.float32)
+        halos = jnp.concatenate(
+            [
+                block[rows - 8 :, g * LANES : (g + 1) * LANES].astype(jnp.float32)
+                for g in range(modes // 8)
+            ],
+            axis=0,
+        )
+        turn = HALO * (base // modes)
+        halo = pltpu.roll(halos, LANES - turn, 1) if turn else halos
+        gathered[pl.ds(start, modes), pl.ds(width, LANES)] = halo
     rows = gathered[...].astype(jnp.bfloat16)
     result = jnp.dot(terms, rows, preferred_element_type=jnp.float32)
     return result[:count] + (result[count : 2 * count] + result[2 * count :])
@@ -608,6 +620,8 @@
         and levs & (levs - 1) == 0
         and NLON // levs % TILE == 0
         and levs % 2 == 0
+        and modes // 8 * LANES <= NLON // levs
+        and 2 * HALO * (2 * legendre.shape[2] // waves) <= LANES
         and 2 * legendre.shape[2] // waves >= 3
     )
     form = tiled_body if tiled else plain_body

time: 78.7 us -> 78 us (level)
  waiting for transfers between devices: 33.8 us -> 32.4 us
    ppermute x13, waiting for transfers between devices: 29.1 us -> 26.5 us  [exchange(): lax.ppermute(blocks[d], axis, [(i, i ^ d) for i in range(count)])]
    ppermute x2, waiting for transfers between devices: 3.22 us -> 5.58 us  [edges(): diagonal = lax.ppermute(diagonal, 'wave', steps)]
    ppermute x2, waiting for transfers between devices: 1.54 us -> 0.36 us  [edges(): pair = lax.ppermute(pair, 'wave', [(i, i ^ 1) for i in range(count)])]
  transfers between devices with their start and end apart: 17 -> 17, of which waited for: 10 -> 11; matrix products, arithmetic and copies ran while one was open for 3% -> 3% of each run, Pallas kernels for 7% -> 7%
where the time goes in v6:
time: 78 us; the launch traced here: 77.8 us
  waiting for transfers between devices  32.4 us (42%)
  Pallas kernels  24.4 us (31%)
  starting transfers between devices  18.4 us (24%)
  other arithmetic  2.3 us (3%)
    ppermute x13, waiting for transfers between devices, exchange(): lax.ppermute(blocks[d], axis, [(i, i ^ d) for i in range(count)])  26.5 us
    pallas_call x1, Pallas kernels, legendre_stage(): pl.pallas_call(legendre_kernel, out_shape=[jax.ShapeDtypeStruct((FIELDS,...  15 us
    ppermute x13, starting transfers between devices, exchange(): lax.ppermute(blocks[d], axis, [(i, i ^ d) for i in range(count)])  11.8 us
    ppermute x2, waiting for transfers between devices, edges(): diagonal = lax.ppermute(diagonal, 'wave', steps)  5.58 us
    ppermute x2, starting transfers between devices, edges(): diagonal = lax.ppermute(diagonal, 'wave', steps)  4.43 us
    pallas_call x4, Pallas kernels, local_call(): pl.pallas_call(kernel, out_shape=outs, in_specs=[smem if operand.dtype ==...  4.4 us
    pallas_call x2, Pallas kernels, synthesis_stage(): pl.pallas_call(functools.partial(synthesis_kernel, waves, levs, fields),...  3.18 us
    ppermute x2, starting transfers between devices, edges(): pair = lax.ppermute(pair, 'wave', [(i, i ^ 1) for i in range(count)])  2.17 us
  transfers between devices with their start and end apart: 17, of which 11 were waited for; matrix products, arithmetic and copies ran while one was open for 3% of the time, Pallas kernels for 7%

profile of v6, /device:TPU:16, one launch (start us, length us, event | category | flops | bytes accessed | tf_op | source)
XLA Modules:
  0.0 77.8 jit_solution(12282887089123966587)
XLA Ops:
  0.0 0.0 copy-start.2
  0.0 15.0 %legendre_sums.1 = (bf16[3,2,4,24,128]{4,3,2,1,0:T(8,128)(2,1)}, bf16[3,2,4,24,128]{4,3,2,1,0:T(8,128)(2,1)}, bf16[3,2,4,24,128]{4,3,2,1,0:T(8,128)(2,1)}, bf16[...) custom-call(s32[1024]{0:T(1024)} %numbers_ref.1, ...), custom_call_target="tpu_custom_call" | custom-call | flops 603979776 | bytes 18874368 | tf_op jit(solution)/shard_map/legendre_sums/pallas_call | solution.py:233
  15.0 0.0 copy-start.1
  15.0 1.6 %collective-permute-start = (bf16[3,2,4,24,128]{4,3,2,1,0:T(8,128)(2,1)}, bf16[3,2,4,24,128]{4,3,2,1,0:T(8,128)(2,1)S(1)}, u32[]{:S(2)}, u32[]{:S(2)}) collective-permute-start(bf16[3,2,4,24,128]{4,3,2,1,0:T(8,128)(2,1)} %get-tuple-element.32), channel_id=1, source_target_pairs={{0,4},{4,0},{8,12},{12,8},{16,20},{20,16},{24,28},{28,24},{1,5},{5... | collective-permute-start | bytes 442376 | tf_op jit(solution)/shard_map/ppermute | solution.py:512
  16.6 1.6 %collective-permute-start.1 = (bf16[3,2,4,24,128]{4,3,2,1,0:T(8,128)(2,1)}, bf16[3,2,4,24,128]{4,3,2,1,0:T(8,128)(2,1)S(1)}, u32[]{:S(2)}, u32[]{:S(2)}) collective-permute-start(bf16[3,2,4,24,128]{4,3,2,1,0:T(8,128)(2,1)} %get-tuple-element.33), channel_id=1, source_target_pairs={{0,8},{4,12},{8,0},{12,4},{16,24},{20,28},{24,16},{28,20},{1,9},{5... | collective-permute-start | bytes 442376 | tf_op jit(solution)/shard_map/ppermute | solution.py:512
  18.1 0.4 collective-permute-start.2
  18.5 0.0 collective-permute-start.3
  18.6 3.9 %collective-permute-start.4 = (bf16[3,2,4,24,128]{4,3,2,1,0:T(8,128)(2,1)}, bf16[3,2,4,24,128]{4,3,2,1,0:T(8,128)(2,1)S(1)}, u32[]{:S(2)}, u32[]{:S(2)}) collective-permute-start(bf16[3,2,4,24,128]{4,3,2,1,0:T(8,128)(2,1)} %get-tuple-element.36), channel_id=1, source_target_pairs={{0,20},{4,16},{8,28},{12,24},{16,4},{20,0},{24,12},{28,8},{1,21},{... | collective-permute-start | bytes 442376 | tf_op jit(solution)/shard_map/ppermute | solution.py:512
  22.4 0.0 copy-done.2
  22.4 0.2 fusion.11
  22.6 0.1 cos.7.turn_cos_ref
  22.7 0.0 collective-permute-done.refs_1_
  22.7 0.5 collective-permute-start.5
  23.2 3.1 %collective-permute-done.1.refs_2_ = bf16[3,2,4,24,128]{4,3,2,1,0:T(8,128)(2,1)S(1)} collective-permute-done((bf16[3,2,4,24,128]{4,3,2,1,0:T(8,128)(2,1)}, bf16[3,2,4,24,128]{4,3,2,1,0:T(8,128)(2,1)S(1)}, u32[]{:S(2)}, u32[]{:S(2)}) %collective-permute-start.1) | collective-permute-done | bytes 147488 | tf_op jit(solution)/shard_map/ppermute | solution.py:512
  26.4 0.0 collective-permute-start.6
  26.4 2.1 %sine_multiply_fusion = (f32[8,128,128]{2,1,0:T(8,128)S(1)}, f32[8,128,128]{2,1,0:T(8,128)S(1)}) fusion(s32[8,128]{1,0:T(8,128)S(1)} %bitcast.14, f32[8,128]{1,0:T(8,128)S(1)} %compare_select_fusion.5), kind=kLoop, calls=%fused_computation.6 | loop fusion | flops 2097152 | bytes 1056768 | tf_op jit(solution)/shard_map/mul | solution.py:289
  28.5 1.8 %twiddles.1.refs_9_ = bf16[8,2,128,1024]{3,2,1,0:T(8,128)(2,1)S(1)} custom-call(s32[1]{0:T(128)} %bitcast.3.place_ref.wave_ref, f32[8,128,128]{2,1,0:T(8,128)S(1)} %get-tuple-element.60.low_cos_ref, f32[8,128,128]{2,1,0:T(8,128)S(1)} %get-tuple-element.59.low_sin_ref, f32[8,1,128]{2,1,0:T(1,128)S(1)} %cos.7.turn_cos_ref, ...), custom_call_target="tpu_custom_call" | custom-call | flops 8388608 | bytes 4194304 | tf_op jit(solution)/shard_map/twiddles/pallas_call | solution.py:277
  30.3 0.0 collective-permute-done.2.refs_3_
  30.3 0.0 collective-permute-done.3.refs_4_
  30.4 8.8 %collective-permute-done.4.refs_5_ = bf16[3,2,4,24,128]{4,3,2,1,0:T(8,128)(2,1)S(1)} collective-permute-done((bf16[3,2,4,24,128]{4,3,2,1,0:T(8,128)(2,1)}, bf16[3,2,4,24,128]{4,3,2,1,0:T(8,128)(2,1)S(1)}, u32[]{:S(2)}, u32[]{:S(2)}) %collective-permute-start.4) | collective-permute-done | bytes 147488 | tf_op jit(solution)/shard_map/ppermute | solution.py:512
  39.2 5.9 %collective-permute-done.5.refs_6_ = bf16[3,2,4,24,128]{4,3,2,1,0:T(8,128)(2,1)S(1)} collective-permute-done((bf16[3,2,4,24,128]{4,3,2,1,0:T(8,128)(2,1)}, bf16[3,2,4,24,128]{4,3,2,1,0:T(8,128)(2,1)S(1)}, u32[]{:S(2)}, u32[]{:S(2)}) %collective-permute-start.5) | collective-permute-done | bytes 147488 | tf_op jit(solution)/shard_map/ppermute | solution.py:512
  45.1 2.5 %collective-permute-done.6.refs_7_ = bf16[3,2,4,24,128]{4,3,2,1,0:T(8,128)(2,1)S(1)} collective-permute-done((bf16[3,2,4,24,128]{4,3,2,1,0:T(8,128)(2,1)}, bf16[3,2,4,24,128]{4,3,2,1,0:T(8,128)(2,1)S(1)}, u32[]{:S(2)}, u32[]{:S(2)}) %collective-permute-start.6) | collective-permute-done | bytes 147488 | tf_op jit(solution)/shard_map/ppermute | solution.py:512
  47.6 0.0 copy-done.1
  47.6 1.2 %synthesis.2 = (bf16[104,512]{1,0:T(8,128)(2,1)S(1)}, bf16[104,512]{1,0:T(8,128)(2,1)S(1)}, bf16[104,512]{1,0:T(8,128)(2,1)S(1)}, bf16[104,512]{1,0:T(8,128)(2,1)S(1)}) custom-call(s32[1]{0:T(128)} %bitcast.3.place_ref.wave_ref, s32[1]{0:T(128)} %bitcast.2.lev_ref, bf16[3,2,4,24,128]{4,3,2,1,0:T(8,128)(2,1)S(1)} %copy-done.1, ...), custom_call_target="tpu_custom_call" | custom-call | flops 805306368 | bytes 4194304 | tf_op jit(solution)/shard_map/synthesis/pallas_call | solution.py:344
  48.8 0.0 copy-start
  48.8 0.1 collective-permute-start.7
  48.9 1.6 %collective-permute-start.8 = (bf16[104,512]{1,0:T(8,128)(2,1)S(1)}, bf16[104,512]{1,0:T(8,128)(2,1)S(1)}, u32[]{:S(2)}, u32[]{:S(2)}) collective-permute-start(bf16[104,512]{1,0:T(8,128)(2,1)S(1)} %get-tuple-element.41), channel_id=1, source_target_pairs={{0,2},{1,3},{2,0},{3,1},{4,6},{5,7},{6,4},{7,5},{8,10},{9,11},{10,... | collective-permute-start | bytes 319496 | tf_op jit(solution)/shard_map/ppermute | solution.py:512
  50.5 0.3 collective-permute-start.9
  50.7 2.0 %synthesis.3 = (bf16[200,512]{1,0:T(8,128)(2,1)S(1)}, bf16[200,512]{1,0:T(8,128)(2,1)S(1)}, bf16[200,512]{1,0:T(8,128)(2,1)S(1)}, bf16[200,512]{1,0:T(8,128)(2,1)S(1)}) custom-call(s32[1]{0:T(128)} %bitcast.3.place_ref.wave_ref, s32[1]{0:T(128)} %bitcast.2.lev_ref, bf16[3,2,4,24,128]{4,3,2,1,0:T(8,128)(2,1)S(1)} %copy-done.1, ...), custom_call_target="tpu_custom_call" | custom-call | flops 1610612736 | bytes 4194304 | tf_op jit(solution)/shard_map/synthesis/pallas_call | solution.py:344
  52.7 0.4 collective-permute-start.12
  53.2 1.5 %collective-permute-start.13 = (bf16[200,512]{1,0:T(8,128)(2,1)S(1)}, bf16[200,512]{1,0:T(8,128)(2,1)S(1)}, u32[]{:S(2)}, u32[]{:S(2)}) collective-permute-start(bf16[200,512]{1,0:T(8,128)(2,1)S(1)} %get-tuple-element.48), channel_id=1, source_target_pairs={{0,2},{1,3},{2,0},{3,1},{4,6},{5,7},{6,4},{7,5},{8,10},{9,11},{10,... | collective-permute-start | bytes 614408 | tf_op jit(solution)/shard_map/ppermute | solution.py:512
  54.7 0.0 collective-permute-done.7.refs_1_
  54.7 0.0 collective-permute-start.14
  54.7 0.1 collective-permute-done.8.refs_2_
  54.8 1.3 %collective-permute-done.9.refs_3_ = bf16[104,512]{1,0:T(8,128)(2,1)S(1)} collective-permute-done((bf16[104,512]{1,0:T(8,128)(2,1)S(1)}, bf16[104,512]{1,0:T(8,128)(2,1)S(1)}, u32[]{:S(2)}, u32[]{:S(2)}) %collective-permute-start.9) | collective-permute-done | bytes 106528 | tf_op jit(solution)/shard_map/ppermute | solution.py:512
  56.1 0.0 copy-done
  56.1 0.9 %shard_map.46 = (f32[4,96,640]{2,1,0:T(8,128)S(1)}, bf16[96,640]{1,0:T(8,128)(2,1)S(1)}, bf16[96,640]{1,0:T(8,128)(2,1)S(1)}) custom-call(s32[1]{0:T(128)} %bitcast.odd_ref, s32[1]{0:T(128)} %bitcast.2.lev_ref, f32[96,96]{1,0:T(8,128)S(1)} %copy-done, bf16[104,512]{1,0:T(8,128)(2,1)S(1)} %get-tuple-element.39.refs_0_, ...), custom_call_target="tpu_custom_call" | custom-call | flops 4000000 | bytes 4000000 | tf_op jit(solution)/shard_map/pallas_call | solution.py:497
  57.0 0.6 collective-permute-start.10
  57.6 2.5 %collective-permute-start.11 = (bf16[96,640]{1,0:T(8,128)(2,1)S(1)}, bf16[96,640]{1,0:T(8,128)(2,1)S(1)}, u32[]{:S(2)}, u32[]{:S(2)}) collective-permute-start(bf16[96,640]{1,0:T(8,128)(2,1)S(1)} %get-tuple-element.45), channel_id=1, source_target_pairs={{4,8},{12,16},{20,24},{0,0},{8,4},{16,12},{24,20},{28,28},{5,9},{1... | collective-permute-start | bytes 368648 | tf_op jit(solution)/shard_map/ppermute | solution.py:520
  60.1 0.0 collective-permute-done.12.refs_1_
  60.1 1.4 %collective-permute-done.13.refs_2_ = bf16[200,512]{1,0:T(8,128)(2,1)S(1)} collective-permute-done((bf16[200,512]{1,0:T(8,128)(2,1)S(1)}, bf16[200,512]{1,0:T(8,128)(2,1)S(1)}, u32[]{:S(2)}, u32[]{:S(2)}) %collective-permute-start.13) | collective-permute-done | bytes 204832 | tf_op jit(solution)/shard_map/ppermute | solution.py:512
  61.5 3.3 %collective-permute-done.14.refs_3_ = bf16[200,512]{1,0:T(8,128)(2,1)S(1)} collective-permute-done((bf16[200,512]{1,0:T(8,128)(2,1)S(1)}, bf16[200,512]{1,0:T(8,128)(2,1)S(1)}, u32[]{:S(2)}, u32[]{:S(2)}) %collective-permute-start.14) | collective-permute-done | bytes 204832 | tf_op jit(solution)/shard_map/ppermute | solution.py:512
  64.8 0.0 collective-permute-done.10.pair_ref
  64.8 1.3 %collective-permute-done.11.diagonal_ref = bf16[96,640]{1,0:T(8,128)(2,1)S(1)} collective-permute-done((bf16[96,640]{1,0:T(8,128)(2,1)S(1)}, bf16[96,640]{1,0:T(8,128)(2,1)S(1)}, u32[]{:S(2)}, u32[]{:S(2)}) %collective-permute-start.11) | collective-permute-done | bytes 122912 | tf_op jit(solution)/shard_map/ppermute | solution.py:520
  66.1 1.0 %shard_map.47 = (f32[2,96,640]{2,1,0:T(8,128)S(1)}, f32[2,96,640]{2,1,0:T(8,128)S(1)}, f32[2,96,640]{2,1,0:T(8,128)S(1)}, bf16[96,640]{1,0:T(8,128)(2,1)S(1)}, bf16[96,640]{1,0:T(8,128)(2,1)S(1)}) custom-call(s32[1]{0:T(128)} %bitcast.odd_ref, s32[1]{0:T(128)} %bitcast.1.end_ref, s32[1]{0:T(128)} %bitcast.2.lev_ref, f32[96,96]{1,0:T(8,128)S(1)} %copy-done, ...), custom_call_target="tpu_custom_call" | custom-call | flops 4000000 | bytes 4000000 | tf_op jit(solution)/shard_map/pallas_call | solution.py:497
  67.0 1.6 %collective-permute-start.15 = (bf16[96,640]{1,0:T(8,128)(2,1)S(1)}, bf16[96,640]{1,0:T(8,128)(2,1)S(1)}, u32[]{:S(2)}, u32[]{:S(2)}) collective-permute-start(bf16[96,640]{1,0:T(8,128)(2,1)S(1)} %get-tuple-element.53), channel_id=1, source_target_pairs={{0,4},{4,0},{8,12},{12,8},{16,20},{20,16},{24,28},{28,24},{1,5},{5... | collective-permute-start | bytes 368648 | tf_op jit(solution)/shard_map/ppermute | solution.py:521
  68.6 1.9 %collective-permute-start.16 = (bf16[96,640]{1,0:T(8,128)(2,1)S(1)}, bf16[96,640]{1,0:T(8,128)(2,1)S(1)}, u32[]{:S(2)}, u32[]{:S(2)}) collective-permute-start(bf16[96,640]{1,0:T(8,128)(2,1)S(1)} %get-tuple-element.54), channel_id=1, source_target_pairs={{4,8},{12,16},{20,24},{0,0},{8,4},{16,12},{24,20},{28,28},{5,9},{1... | collective-permute-start | bytes 368648 | tf_op jit(solution)/shard_map/ppermute | solution.py:520
  70.5 1.1 %shard_map.48 = (f32[2,96,640]{2,1,0:T(8,128)S(1)}, f32[2,96,512]{2,1,0:T(8,128)S(1)}) custom-call(s32[1]{0:T(128)} %bitcast.2.lev_ref, f32[96,96]{1,0:T(8,128)S(1)} %copy-done, f32[4,96,640]{2,1,0:T(8,128)S(1)} %get-tuple-element.43.tracer_ref, f32[2,96,640]{2,1,0:T(8,128)S(1)} %get-tuple-element.50.edge_ref, ...), custom_call_target="tpu_custom_call" | custom-call | flops 4000000 | bytes 4000000 | tf_op jit(solution)/shard_map/pallas_call | solution.py:497
  71.6 0.4 collective-permute-done.15.pair_ref
  72.0 4.3 %collective-permute-done.16.diagonal_ref = bf16[96,640]{1,0:T(8,128)(2,1)S(1)} collective-permute-done((bf16[96,640]{1,0:T(8,128)(2,1)S(1)}, bf16[96,640]{1,0:T(8,128)(2,1)S(1)}, u32[]{:S(2)}, u32[]{:S(2)}) %collective-permute-start.16) | collective-permute-done | bytes 122912 | tf_op jit(solution)/shard_map/ppermute | solution.py:520
  76.3 1.5 %shard_map.49 = f32[96,4,512]{2,1,0:T(4,128)} custom-call(s32[1]{0:T(128)} %bitcast.odd_ref, s32[1]{0:T(128)} %bitcast.1.end_ref, f32[2,96,640]{2,1,0:T(8,128)S(1)} %get-tuple-element.50.edge_ref, f32[2,96,640]{2,1,0:T(8,128)S(1)} %get-tuple-element.51.inner_ref, f32[2,96,512]{2,1,0:T(8,128)S(1)} %get-tuple-element.52.done_ref, ...), custom_call_target="tpu_custom_call" | custom-call | flops 4000000 | bytes 4000000 | tf_op jit(solution)/shard_map/pallas_call | solution.py:497
  (1 shorter events, 0.0 us)
Async XLA Ops:
  0.0 22.4 %copy-start.2 = (s32[1024]{0:T(1024)S(1)}, s32[1024]{0:T(1024)}, u32[]{:S(2)}) copy-start(s32[1024]{0:T(1024)} %numbers_ref.1) | copy-start | bytes 12292
  15.0 32.6 %copy-start.1 = (bf16[3,2,4,24,128]{4,3,2,1,0:T(8,128)(2,1)S(1)}, bf16[3,2,4,24,128]{4,3,2,1,0:T(8,128)(2,1)}, u32[]{:S(2)}) copy-start(bf16[3,2,4,24,128]{4,3,2,1,0:T(8,128)(2,1)} %get-tuple-element.31.refs_0_) | copy-start | bytes 442372
  15.0 7.7 %collective-permute-start = (bf16[3,2,4,24,128]{4,3,2,1,0:T(8,128)(2,1)}, bf16[3,2,4,24,128]{4,3,2,1,0:T(8,128)(2,1)S(1)}, u32[]{:S(2)}, u32[]{:S(2)}) collective-permute-start(bf16[3,2,4,24,128]{4,3,2,1,0:T(8,128)(2,1)} %get-tuple-element.32), channel_id=1, source_target_pairs={{0,4},{4,0},{8,12},{12,8},{16,20},{20,16},{24,28},{28,24},{1,5},{5... | collective-permute-start | bytes 442376 | tf_op jit(solution)/shard_map/ppermute | solution.py:512
  16.6 9.8 %collective-permute-start.1 = (bf16[3,2,4,24,128]{4,3,2,1,0:T(8,128)(2,1)}, bf16[3,2,4,24,128]{4,3,2,1,0:T(8,128)(2,1)S(1)}, u32[]{:S(2)}, u32[]{:S(2)}) collective-permute-start(bf16[3,2,4,24,128]{4,3,2,1,0:T(8,128)(2,1)} %get-tuple-element.33), channel_id=1, source_target_pairs={{0,8},{4,12},{8,0},{12,4},{16,24},{20,28},{24,16},{28,20},{1,9},{5... | collective-permute-start | bytes 442376 | tf_op jit(solution)/shard_map/ppermute | solution.py:512
  18.1 12.2 %collective-permute-start.2 = (bf16[3,2,4,24,128]{4,3,2,1,0:T(8,128)(2,1)}, bf16[3,2,4,24,128]{4,3,2,1,0:T(8,128)(2,1)S(1)}, u32[]{:S(2)}, u32[]{:S(2)}) collective-permute-start(bf16[3,2,4,24,128]{4,3,2,1,0:T(8,128)(2,1)} %get-tuple-element.34), channel_id=1, source_target_pairs={{0,12},{4,8},{8,4},{12,0},{16,28},{20,24},{24,20},{28,16},{1,13},{... | collective-permute-start | bytes 442376 | tf_op jit(solution)/shard_map/ppermute | solution.py:512
  18.5 11.8 %collective-permute-start.3 = (bf16[3,2,4,24,128]{4,3,2,1,0:T(8,128)(2,1)}, bf16[3,2,4,24,128]{4,3,2,1,0:T(8,128)(2,1)S(1)}, u32[]{:S(2)}, u32[]{:S(2)}) collective-permute-start(bf16[3,2,4,24,128]{4,3,2,1,0:T(8,128)(2,1)} %get-tuple-element.35), channel_id=1, source_target_pairs={{0,16},{4,20},{8,24},{12,28},{16,0},{20,4},{24,8},{28,12},{1,17},{... | collective-permute-start | bytes 442376 | tf_op jit(solution)/shard_map/ppermute | solution.py:512
  18.6 20.6 %collective-permute-start.4 = (bf16[3,2,4,24,128]{4,3,2,1,0:T(8,128)(2,1)}, bf16[3,2,4,24,128]{4,3,2,1,0:T(8,128)(2,1)S(1)}, u32[]{:S(2)}, u32[]{:S(2)}) collective-permute-start(bf16[3,2,4,24,128]{4,3,2,1,0:T(8,128)(2,1)} %get-tuple-element.36), channel_id=1, source_target_pairs={{0,20},{4,16},{8,28},{12,24},{16,4},{20,0},{24,12},{28,8},{1,21},{... | collective-permute-start | bytes 442376 | tf_op jit(solution)/shard_map/ppermute | solution.py:512
  22.7 22.4 %collective-permute-start.5 = (bf16[3,2,4,24,128]{4,3,2,1,0:T(8,128)(2,1)}, bf16[3,2,4,24,128]{4,3,2,1,0:T(8,128)(2,1)S(1)}, u32[]{:S(2)}, u32[]{:S(2)}) collective-permute-start(bf16[3,2,4,24,128]{4,3,2,1,0:T(8,128)(2,1)} %get-tuple-element.37), channel_id=1, source_target_pairs={{0,24},{4,28},{8,16},{12,20},{16,8},{20,12},{24,0},{28,4},{1,25},{... | collective-permute-start | bytes 442376 | tf_op jit(solution)/shard_map/ppermute | solution.py:512
  26.4 21.3 %collective-permute-start.6 = (bf16[3,2,4,24,128]{4,3,2,1,0:T(8,128)(2,1)}, bf16[3,2,4,24,128]{4,3,2,1,0:T(8,128)(2,1)S(1)}, u32[]{:S(2)}, u32[]{:S(2)}) collective-permute-start(bf16[3,2,4,24,128]{4,3,2,1,0:T(8,128)(2,1)} %get-tuple-element.38), channel_id=1, source_target_pairs={{0,28},{4,24},{8,20},{12,16},{16,12},{20,8},{24,4},{28,0},{1,29},{... | collective-permute-start | bytes 442376 | tf_op jit(solution)/shard_map/ppermute | solution.py:512
  48.8 7.3 %copy-start = (f32[96,96]{1,0:T(8,128)S(1)}, f32[96,96]{1,0:T(8,128)}, u32[]{:S(2)}) copy-start(f32[96,96]{1,0:T(8,128)} %vertical_ref.5) | copy-start | bytes 110596
  48.8 5.9 %collective-permute-start.7 = (bf16[104,512]{1,0:T(8,128)(2,1)S(1)}, bf16[104,512]{1,0:T(8,128)(2,1)S(1)}, u32[]{:S(2)}, u32[]{:S(2)}) collective-permute-start(bf16[104,512]{1,0:T(8,128)(2,1)S(1)} %get-tuple-element.40), channel_id=1, source_target_pairs={{0,1},{1,0},{2,3},{3,2},{4,5},{5,4},{6,7},{7,6},{8,9},{9,8},{10,11... | collective-permute-start | bytes 319496 | tf_op jit(solution)/shard_map/ppermute | solution.py:512
  48.9 5.9 %collective-permute-start.8 = (bf16[104,512]{1,0:T(8,128)(2,1)S(1)}, bf16[104,512]{1,0:T(8,128)(2,1)S(1)}, u32[]{:S(2)}, u32[]{:S(2)}) collective-permute-start(bf16[104,512]{1,0:T(8,128)(2,1)S(1)} %get-tuple-element.41), channel_id=1, source_target_pairs={{0,2},{1,3},{2,0},{3,1},{4,6},{5,7},{6,4},{7,5},{8,10},{9,11},{10,... | collective-permute-start | bytes 319496 | tf_op jit(solution)/shard_map/ppermute | solution.py:512
  50.5 5.6 %collective-permute-start.9 = (bf16[104,512]{1,0:T(8,128)(2,1)S(1)}, bf16[104,512]{1,0:T(8,128)(2,1)S(1)}, u32[]{:S(2)}, u32[]{:S(2)}) collective-permute-start(bf16[104,512]{1,0:T(8,128)(2,1)S(1)} %get-tuple-element.42), channel_id=1, source_target_pairs={{0,3},{1,2},{2,1},{3,0},{4,7},{5,6},{6,5},{7,4},{8,11},{9,10},{10,... | collective-permute-start | bytes 319496 | tf_op jit(solution)/shard_map/ppermute | solution.py:512
  52.7 7.3 %collective-permute-start.12 = (bf16[200,512]{1,0:T(8,128)(2,1)S(1)}, bf16[200,512]{1,0:T(8,128)(2,1)S(1)}, u32[]{:S(2)}, u32[]{:S(2)}) collective-permute-start(bf16[200,512]{1,0:T(8,128)(2,1)S(1)} %get-tuple-element.47), channel_id=1, source_target_pairs={{0,1},{1,0},{2,3},{3,2},{4,5},{5,4},{6,7},{7,6},{8,9},{9,8},{10,11... | collective-permute-start | bytes 614408 | tf_op jit(solution)/shard_map/ppermute | solution.py:512
  53.2 8.3 %collective-permute-start.13 = (bf16[200,512]{1,0:T(8,128)(2,1)S(1)}, bf16[200,512]{1,0:T(8,128)(2,1)S(1)}, u32[]{:S(2)}, u32[]{:S(2)}) collective-permute-start(bf16[200,512]{1,0:T(8,128)(2,1)S(1)} %get-tuple-element.48), channel_id=1, source_target_pairs={{0,2},{1,3},{2,0},{3,1},{4,6},{5,7},{6,4},{7,5},{8,10},{9,11},{10,... | collective-permute-start | bytes 614408 | tf_op jit(solution)/shard_map/ppermute | solution.py:512
  54.7 10.1 %collective-permute-start.14 = (bf16[200,512]{1,0:T(8,128)(2,1)S(1)}, bf16[200,512]{1,0:T(8,128)(2,1)S(1)}, u32[]{:S(2)}, u32[]{:S(2)}) collective-permute-start(bf16[200,512]{1,0:T(8,128)(2,1)S(1)} %get-tuple-element.49), channel_id=1, source_target_pairs={{0,3},{1,2},{2,1},{3,0},{4,7},{5,6},{6,5},{7,4},{8,11},{9,10},{10,... | collective-permute-start | bytes 614408 | tf_op jit(solution)/shard_map/ppermute | solution.py:512
  57.0 7.8 %collective-permute-start.10 = (bf16[96,640]{1,0:T(8,128)(2,1)S(1)}, bf16[96,640]{1,0:T(8,128)(2,1)S(1)}, u32[]{:S(2)}, u32[]{:S(2)}) collective-permute-start(bf16[96,640]{1,0:T(8,128)(2,1)S(1)} %get-tuple-element.44), channel_id=1, source_target_pairs={{0,4},{4,0},{8,12},{12,8},{16,20},{20,16},{24,28},{28,24},{1,5},{5... | collective-permute-start | bytes 368648 | tf_op jit(solution)/shard_map/ppermute | solution.py:521
  57.6 8.5 %collective-permute-start.11 = (bf16[96,640]{1,0:T(8,128)(2,1)S(1)}, bf16[96,640]{1,0:T(8,128)(2,1)S(1)}, u32[]{:S(2)}, u32[]{:S(2)}) collective-permute-start(bf16[96,640]{1,0:T(8,128)(2,1)S(1)} %get-tuple-element.45), channel_id=1, source_target_pairs={{4,8},{12,16},{20,24},{0,0},{8,4},{16,12},{24,20},{28,28},{5,9},{1... | collective-permute-start | bytes 368648 | tf_op jit(solution)/shard_map/ppermute | solution.py:520
  67.0 5.0 %collective-permute-start.15 = (bf16[96,640]{1,0:T(8,128)(2,1)S(1)}, bf16[96,640]{1,0:T(8,128)(2,1)S(1)}, u32[]{:S(2)}, u32[]{:S(2)}) collective-permute-start(bf16[96,640]{1,0:T(8,128)(2,1)S(1)} %get-tuple-element.53), channel_id=1, source_target_pairs={{0,4},{4,0},{8,12},{12,8},{16,20},{20,16},{24,28},{28,24},{1,5},{5... | collective-permute-start | bytes 368648 | tf_op jit(solution)/shard_map/ppermute | solution.py:521
  68.6 7.7 %collective-permute-start.16 = (bf16[96,640]{1,0:T(8,128)(2,1)S(1)}, bf16[96,640]{1,0:T(8,128)(2,1)S(1)}, u32[]{:S(2)}, u32[]{:S(2)}) collective-permute-start(bf16[96,640]{1,0:T(8,128)(2,1)S(1)} %get-tuple-element.54), channel_id=1, source_target_pairs={{4,8},{12,16},{20,24},{0,0},{8,4},{16,12},{24,20},{28,28},{5,9},{1... | collective-permute-start | bytes 368648 | tf_op jit(solution)/shard_map/ppermute | solution.py:520

commit v7 on v6

--- a/solution.py
+++ b/solution.py
@@ -148,16 +148,19 @@
         for pair in range(pairs):
             index = group * pairs + pair
             _, _, edge = plan(index)
-            for t in range(chunks):
-                inside = t < edge
-                source = jnp.where(inside, 2 * index, 2 * index + 1)
-                block = jnp.where(inside, t, t - edge)
-                start = pl.multiple_of(block * CHUNK, CHUNK)
-                pltpu.make_async_copy(
-                    spectrum_ref.at[source, :, pl.ds(start, CHUNK)],
-                    held.at[slot, pair, :, pl.ds(t * CHUNK, CHUNK)],
-                    arrived.at[slot],
-                ).start()
+
+            def counted(first, index=index, pair=pair):
+                for source, start, count in (
+                    (2 * index, 0, first),
+                    (2 * index + 1, first, chunks - first),
+                ):
+                    pltpu.make_async_copy(
+                        spectrum_ref.at[source, :, pl.ds(0, count * CHUNK)],
+                        held.at[slot, pair, :, pl.ds(start * CHUNK, count * CHUNK)],
+                        arrived.at[slot],
+                    ).start()
+
+            lax.switch(edge - 1, [functools.partial(counted, n) for n in range(1, chunks)])
 
     for group in range(min(ahead, steps)):
         fetch(group, group)
@@ -386,7 +389,7 @@
 
 
 def keep_edges(lat, lats, values, odd, pair_ref, diagonal_ref):
-    edge = values.astype(jnp.bfloat16)
+    edge = values[:, : pair_ref.shape[1]].astype(jnp.bfloat16)
     if 0 < lat < lats - 1:
         return
     takes_pair = 1 if lat == 0 else 0
@@ -420,10 +423,11 @@
     )
 
 
-def row_step(center, northern, southern, courant_x, courant_y):
+def row_step(center, northern, southern, courant_x, courant_y, kept=None):
     width = center.shape[1]
     western, eastern = pltpu.roll(center, 1, 1), pltpu.roll(center, width - 1, 1)
-    return upwind(center, western, eastern, northern, southern, courant_x, courant_y)
+    rows = (center, western, eastern, northern, southern, courant_x, courant_y)
+    return upwind(*(row[:, :kept] for row in rows))
 
 
 def outside(takes_pair, odd_ref, end_ref, pair_ref, diagonal_ref):
@@ -474,8 +478,9 @@
     for place in range(inner):
         northern = inner_ref[place - 1] if place > 0 else edge_ref[0]
         southern = inner_ref[place + 1] if place < inner - 1 else edge_ref[1]
-        values = row_step(inner_ref[place], northern, southern, x_ref[place], y_ref[place])
-        out_ref[place] = values[:, :width]
+        out_ref[place] = row_step(
+            inner_ref[place], northern, southern, x_ref[place], y_ref[place], width
+        )
 
 
 def last_step_kernel(
@@ -488,8 +493,8 @@
         other = outside(1 - place, odd_ref, end_ref, pair_ref, diagonal_ref)
         northern = other if place == 0 else inner_ref[inner - 1]
         southern = inner_ref[0] if place == 0 else other
-        values = row_step(edge_ref[place], northern, southern, x_ref[place], y_ref[place])
-        out_ref[:, place * (inner + 1), :] = values[:, :width]
+        values = row_step(edge_ref[place], northern, southern, x_ref[place], y_ref[place], width)
+        out_ref[:, place * (inner + 1), :] = values
 
 
 def local_call(kernel, outs, scratch, *operands):
@@ -547,6 +552,7 @@
 
     whole = jax.ShapeDtypeStruct((lats, levels, width + LANES), jnp.float32)
     row = jax.ShapeDtypeStruct((levels, width + LANES), jnp.bfloat16)
+    own_row = jax.ShapeDtypeStruct((levels, width), jnp.bfloat16)
     pair_of_rows = jax.ShapeDtypeStruct((2, *whole.shape[1:]), jnp.float32)
     gathered = (levs * modes, width + LANES)
     tracer, pair, diagonal = local_call(
@@ -561,7 +567,7 @@
     pair, diagonal = edges(pair, diagonal)
     courant_x, courant_y, edge, pair, diagonal = local_call(
         functools.partial(edge_step_kernel, modes),
-        (pair_of_rows, pair_of_rows, pair_of_rows, row, row),
+        (pair_of_rows, pair_of_rows, pair_of_rows, own_row, own_row),
         [pltpu.VMEM((2, *gathered), jnp.float32)],
         odd,
         at_end,

time: 78 us -> 77.5 us (level)
  no operation moved by 1% of the time
where the time goes in v7:
time: 77.5 us; the launch traced here: 77.3 us
  waiting for transfers between devices  32.1 us (41%)
  Pallas kernels  24.2 us (31%)
  starting transfers between devices  18.3 us (24%)
  other arithmetic  2.3 us (3%)
    ppermute x13, waiting for transfers between devices, exchange(): lax.ppermute(blocks[d], axis, [(i, i ^ d) for i in range(count)])  26.5 us
    pallas_call x1, Pallas kernels, legendre_stage(): pl.pallas_call(legendre_kernel, out_shape=[jax.ShapeDtypeStruct((FIELDS,...  14.8 us
    ppermute x13, starting transfers between devices, exchange(): lax.ppermute(blocks[d], axis, [(i, i ^ d) for i in range(count)])  11.8 us
    ppermute x2, waiting for transfers between devices, edges(): diagonal = lax.ppermute(diagonal, 'wave', steps)  5.57 us
    ppermute x2, starting transfers between devices, edges(): diagonal = lax.ppermute(diagonal, 'wave', steps)  4.43 us
    pallas_call x4, Pallas kernels, local_call(): pl.pallas_call(kernel, out_shape=outs, in_specs=[smem if operand.dtype ==...  4.41 us
    pallas_call x2, Pallas kernels, synthesis_stage(): pl.pallas_call(functools.partial(synthesis_kernel, waves, levs, fields),...  3.18 us
    mul x1, other arithmetic, twiddle_stage(): weight * jnp.sin(low)  2.14 us
  transfers between devices with their start and end apart: 17, of which 11 were waited for; matrix products, arithmetic and copies ran while one was open for 3% of the time, Pallas kernels for 7%

profile of v7, /device:TPU:16, one launch (start us, length us, event | category | flops | bytes accessed | tf_op | source)
XLA Modules:
  0.0 77.3 jit_solution(14343393660477611128)
XLA Ops:
  0.0 0.0 copy-start.2
  0.0 14.8 %legendre_sums.1 = (bf16[3,2,4,24,128]{4,3,2,1,0:T(8,128)(2,1)}, bf16[3,2,4,24,128]{4,3,2,1,0:T(8,128)(2,1)}, bf16[3,2,4,24,128]{4,3,2,1,0:T(8,128)(2,1)}, bf16[...) custom-call(s32[1024]{0:T(1024)} %numbers_ref.1, ...), custom_call_target="tpu_custom_call" | custom-call | flops 603979776 | bytes 18874368 | tf_op jit(solution)/shard_map/legendre_sums/pallas_call | solution.py:236
  14.8 0.0 copy-start.1
  14.8 1.6 %collective-permute-start = (bf16[3,2,4,24,128]{4,3,2,1,0:T(8,128)(2,1)}, bf16[3,2,4,24,128]{4,3,2,1,0:T(8,128)(2,1)S(1)}, u32[]{:S(2)}, u32[]{:S(2)}) collective-permute-start(bf16[3,2,4,24,128]{4,3,2,1,0:T(8,128)(2,1)} %get-tuple-element.32), channel_id=1, source_target_pairs={{0,4},{4,0},{8,12},{12,8},{16,20},{20,16},{24,28},{28,24},{1,5},{5... | collective-permute-start | bytes 442376 | tf_op jit(solution)/shard_map/ppermute | solution.py:517
  16.4 1.6 %collective-permute-start.1 = (bf16[3,2,4,24,128]{4,3,2,1,0:T(8,128)(2,1)}, bf16[3,2,4,24,128]{4,3,2,1,0:T(8,128)(2,1)S(1)}, u32[]{:S(2)}, u32[]{:S(2)}) collective-permute-start(bf16[3,2,4,24,128]{4,3,2,1,0:T(8,128)(2,1)} %get-tuple-element.33), channel_id=1, source_target_pairs={{0,8},{4,12},{8,0},{12,4},{16,24},{20,28},{24,16},{28,20},{1,9},{5... | collective-permute-start | bytes 442376 | tf_op jit(solution)/shard_map/ppermute | solution.py:517
  17.9 0.4 collective-permute-start.2
  18.3 0.0 collective-permute-start.3
  18.3 3.9 %collective-permute-start.4 = (bf16[3,2,4,24,128]{4,3,2,1,0:T(8,128)(2,1)}, bf16[3,2,4,24,128]{4,3,2,1,0:T(8,128)(2,1)S(1)}, u32[]{:S(2)}, u32[]{:S(2)}) collective-permute-start(bf16[3,2,4,24,128]{4,3,2,1,0:T(8,128)(2,1)} %get-tuple-element.36), channel_id=1, source_target_pairs={{0,20},{4,16},{8,28},{12,24},{16,4},{20,0},{24,12},{28,8},{1,21},{... | collective-permute-start | bytes 442376 | tf_op jit(solution)/shard_map/ppermute | solution.py:517
  22.2 0.0 copy-done.2
  22.2 0.2 fusion.11
  22.4 0.1 cos.7.turn_cos_ref
  22.5 0.0 collective-permute-done.refs_1_
  22.5 0.5 collective-permute-start.5
  23.0 3.1 %collective-permute-done.1.refs_2_ = bf16[3,2,4,24,128]{4,3,2,1,0:T(8,128)(2,1)S(1)} collective-permute-done((bf16[3,2,4,24,128]{4,3,2,1,0:T(8,128)(2,1)}, bf16[3,2,4,24,128]{4,3,2,1,0:T(8,128)(2,1)S(1)}, u32[]{:S(2)}, u32[]{:S(2)}) %collective-permute-start.1) | collective-permute-done | bytes 147488 | tf_op jit(solution)/shard_map/ppermute | solution.py:517
  26.1 0.0 collective-permute-start.6
  26.1 2.1 %sine_multiply_fusion = (f32[8,128,128]{2,1,0:T(8,128)S(1)}, f32[8,128,128]{2,1,0:T(8,128)S(1)}) fusion(s32[8,128]{1,0:T(8,128)S(1)} %bitcast.14, f32[8,128]{1,0:T(8,128)S(1)} %compare_select_fusion.5), kind=kLoop, calls=%fused_computation.6 | loop fusion | flops 2097152 | bytes 1056768 | tf_op jit(solution)/shard_map/mul | solution.py:292
  28.3 1.8 %twiddles.1.refs_9_ = bf16[8,2,128,1024]{3,2,1,0:T(8,128)(2,1)S(1)} custom-call(s32[1]{0:T(128)} %bitcast.3.place_ref.wave_ref, f32[8,128,128]{2,1,0:T(8,128)S(1)} %get-tuple-element.60.low_cos_ref, f32[8,128,128]{2,1,0:T(8,128)S(1)} %get-tuple-element.59.low_sin_ref, f32[8,1,128]{2,1,0:T(1,128)S(1)} %cos.7.turn_cos_ref, ...), custom_call_target="tpu_custom_call" | custom-call | flops 8388608 | bytes 4194304 | tf_op jit(solution)/shard_map/twiddles/pallas_call | solution.py:280
  30.1 0.0 collective-permute-done.2.refs_3_
  30.1 0.0 collective-permute-done.3.refs_4_
  30.1 8.8 %collective-permute-done.4.refs_5_ = bf16[3,2,4,24,128]{4,3,2,1,0:T(8,128)(2,1)S(1)} collective-permute-done((bf16[3,2,4,24,128]{4,3,2,1,0:T(8,128)(2,1)}, bf16[3,2,4,24,128]{4,3,2,1,0:T(8,128)(2,1)S(1)}, u32[]{:S(2)}, u32[]{:S(2)}) %collective-permute-start.4) | collective-permute-done | bytes 147488 | tf_op jit(solution)/shard_map/ppermute | solution.py:517
  38.9 5.9 %collective-permute-done.5.refs_6_ = bf16[3,2,4,24,128]{4,3,2,1,0:T(8,128)(2,1)S(1)} collective-permute-done((bf16[3,2,4,24,128]{4,3,2,1,0:T(8,128)(2,1)}, bf16[3,2,4,24,128]{4,3,2,1,0:T(8,128)(2,1)S(1)}, u32[]{:S(2)}, u32[]{:S(2)}) %collective-permute-start.5) | collective-permute-done | bytes 147488 | tf_op jit(solution)/shard_map/ppermute | solution.py:517
  44.9 2.5 %collective-permute-done.6.refs_7_ = bf16[3,2,4,24,128]{4,3,2,1,0:T(8,128)(2,1)S(1)} collective-permute-done((bf16[3,2,4,24,128]{4,3,2,1,0:T(8,128)(2,1)}, bf16[3,2,4,24,128]{4,3,2,1,0:T(8,128)(2,1)S(1)}, u32[]{:S(2)}, u32[]{:S(2)}) %collective-permute-start.6) | collective-permute-done | bytes 147488 | tf_op jit(solution)/shard_map/ppermute | solution.py:517
  47.4 0.0 copy-done.1
  47.4 1.2 %synthesis.2 = (bf16[104,512]{1,0:T(8,128)(2,1)S(1)}, bf16[104,512]{1,0:T(8,128)(2,1)S(1)}, bf16[104,512]{1,0:T(8,128)(2,1)S(1)}, bf16[104,512]{1,0:T(8,128)(2,1)S(1)}) custom-call(s32[1]{0:T(128)} %bitcast.3.place_ref.wave_ref, s32[1]{0:T(128)} %bitcast.2.lev_ref, bf16[3,2,4,24,128]{4,3,2,1,0:T(8,128)(2,1)S(1)} %copy-done.1, ...), custom_call_target="tpu_custom_call" | custom-call | flops 805306368 | bytes 4194304 | tf_op jit(solution)/shard_map/synthesis/pallas_call | solution.py:347
  48.6 0.0 copy-start
  48.6 0.1 collective-permute-start.7
  48.7 1.6 %collective-permute-start.8 = (bf16[104,512]{1,0:T(8,128)(2,1)S(1)}, bf16[104,512]{1,0:T(8,128)(2,1)S(1)}, u32[]{:S(2)}, u32[]{:S(2)}) collective-permute-start(bf16[104,512]{1,0:T(8,128)(2,1)S(1)} %get-tuple-element.41), channel_id=1, source_target_pairs={{0,2},{1,3},{2,0},{3,1},{4,6},{5,7},{6,4},{7,5},{8,10},{9,11},{10,... | collective-permute-start | bytes 319496 | tf_op jit(solution)/shard_map/ppermute | solution.py:517
  50.3 0.3 collective-permute-start.9
  50.5 2.0 %synthesis.3 = (bf16[200,512]{1,0:T(8,128)(2,1)S(1)}, bf16[200,512]{1,0:T(8,128)(2,1)S(1)}, bf16[200,512]{1,0:T(8,128)(2,1)S(1)}, bf16[200,512]{1,0:T(8,128)(2,1)S(1)}) custom-call(s32[1]{0:T(128)} %bitcast.3.place_ref.wave_ref, s32[1]{0:T(128)} %bitcast.2.lev_ref, bf16[3,2,4,24,128]{4,3,2,1,0:T(8,128)(2,1)S(1)} %copy-done.1, ...), custom_call_target="tpu_custom_call" | custom-call | flops 1610612736 | bytes 4194304 | tf_op jit(solution)/shard_map/synthesis/pallas_call | solution.py:347
  52.5 0.4 collective-permute-start.12
  53.0 1.5 %collective-permute-start.13 = (bf16[200,512]{1,0:T(8,128)(2,1)S(1)}, bf16[200,512]{1,0:T(8,128)(2,1)S(1)}, u32[]{:S(2)}, u32[]{:S(2)}) collective-permute-start(bf16[200,512]{1,0:T(8,128)(2,1)S(1)} %get-tuple-element.48), channel_id=1, source_target_pairs={{0,2},{1,3},{2,0},{3,1},{4,6},{5,7},{6,4},{7,5},{8,10},{9,11},{10,... | collective-permute-start | bytes 614408 | tf_op jit(solution)/shard_map/ppermute | solution.py:517
  54.5 0.0 collective-permute-done.7.refs_1_
  54.5 0.0 collective-permute-start.14
  54.5 0.1 collective-permute-done.8.refs_2_
  54.6 1.3 %collective-permute-done.9.refs_3_ = bf16[104,512]{1,0:T(8,128)(2,1)S(1)} collective-permute-done((bf16[104,512]{1,0:T(8,128)(2,1)S(1)}, bf16[104,512]{1,0:T(8,128)(2,1)S(1)}, u32[]{:S(2)}, u32[]{:S(2)}) %collective-permute-start.9) | collective-permute-done | bytes 106528 | tf_op jit(solution)/shard_map/ppermute | solution.py:517
  55.9 0.0 copy-done
  55.9 0.9 %shard_map.46 = (f32[4,96,640]{2,1,0:T(8,128)S(1)}, bf16[96,640]{1,0:T(8,128)(2,1)S(1)}, bf16[96,640]{1,0:T(8,128)(2,1)S(1)}) custom-call(s32[1]{0:T(128)} %bitcast.odd_ref, s32[1]{0:T(128)} %bitcast.2.lev_ref, f32[96,96]{1,0:T(8,128)S(1)} %copy-done, bf16[104,512]{1,0:T(8,128)(2,1)S(1)} %get-tuple-element.39.refs_0_, ...), custom_call_target="tpu_custom_call" | custom-call | flops 4000000 | bytes 4000000 | tf_op jit(solution)/shard_map/pallas_call | solution.py:502
  56.8 0.6 collective-permute-start.10
  57.4 2.5 %collective-permute-start.11 = (bf16[96,640]{1,0:T(8,128)(2,1)S(1)}, bf16[96,640]{1,0:T(8,128)(2,1)S(1)}, u32[]{:S(2)}, u32[]{:S(2)}) collective-permute-start(bf16[96,640]{1,0:T(8,128)(2,1)S(1)} %get-tuple-element.45), channel_id=1, source_target_pairs={{4,8},{12,16},{20,24},{0,0},{8,4},{16,12},{24,20},{28,28},{5,9},{1... | collective-permute-start | bytes 368648 | tf_op jit(solution)/shard_map/ppermute | solution.py:525
  59.9 0.0 collective-permute-done.12.refs_1_
  59.9 1.3 %collective-permute-done.13.refs_2_ = bf16[200,512]{1,0:T(8,128)(2,1)S(1)} collective-permute-done((bf16[200,512]{1,0:T(8,128)(2,1)S(1)}, bf16[200,512]{1,0:T(8,128)(2,1)S(1)}, u32[]{:S(2)}, u32[]{:S(2)}) %collective-permute-start.13) | collective-permute-done | bytes 204832 | tf_op jit(solution)/shard_map/ppermute | solution.py:517
  61.3 3.3 %collective-permute-done.14.refs_3_ = bf16[200,512]{1,0:T(8,128)(2,1)S(1)} collective-permute-done((bf16[200,512]{1,0:T(8,128)(2,1)S(1)}, bf16[200,512]{1,0:T(8,128)(2,1)S(1)}, u32[]{:S(2)}, u32[]{:S(2)}) %collective-permute-start.14) | collective-permute-done | bytes 204832 | tf_op jit(solution)/shard_map/ppermute | solution.py:517
  64.6 0.0 collective-permute-done.10.pair_ref
  64.6 1.3 %collective-permute-done.11.diagonal_ref = bf16[96,640]{1,0:T(8,128)(2,1)S(1)} collective-permute-done((bf16[96,640]{1,0:T(8,128)(2,1)S(1)}, bf16[96,640]{1,0:T(8,128)(2,1)S(1)}, u32[]{:S(2)}, u32[]{:S(2)}) %collective-permute-start.11) | collective-permute-done | bytes 122912 | tf_op jit(solution)/shard_map/ppermute | solution.py:525
  65.9 1.0 %shard_map.47 = (f32[2,96,640]{2,1,0:T(8,128)S(1)}, f32[2,96,640]{2,1,0:T(8,128)S(1)}, f32[2,96,640]{2,1,0:T(8,128)S(1)}, bf16[96,512]{1,0:T(8,128)(2,1)S(1)}, bf16[96,512]{1,0:T(8,128)(2,1)S(1)}) custom-call(s32[1]{0:T(128)} %bitcast.odd_ref, s32[1]{0:T(128)} %bitcast.1.end_ref, s32[1]{0:T(128)} %bitcast.2.lev_ref, f32[96,96]{1,0:T(8,128)S(1)} %copy-done, ...), custom_call_target="tpu_custom_call" | custom-call | flops 4000000 | bytes 4000000 | tf_op jit(solution)/shard_map/pallas_call | solution.py:502
  66.9 1.5 %collective-permute-start.15 = (bf16[96,512]{1,0:T(8,128)(2,1)S(1)}, bf16[96,512]{1,0:T(8,128)(2,1)S(1)}, u32[]{:S(2)}, u32[]{:S(2)}) collective-permute-start(bf16[96,512]{1,0:T(8,128)(2,1)S(1)} %get-tuple-element.53), channel_id=1, source_target_pairs={{0,4},{4,0},{8,12},{12,8},{16,20},{20,16},{24,28},{28,24},{1,5},{5... | collective-permute-start | bytes 294920 | tf_op jit(solution)/shard_map/ppermute | solution.py:526
  68.4 1.9 %collective-permute-start.16 = (bf16[96,512]{1,0:T(8,128)(2,1)S(1)}, bf16[96,512]{1,0:T(8,128)(2,1)S(1)}, u32[]{:S(2)}, u32[]{:S(2)}) collective-permute-start(bf16[96,512]{1,0:T(8,128)(2,1)S(1)} %get-tuple-element.54), channel_id=1, source_target_pairs={{4,8},{12,16},{20,24},{0,0},{8,4},{16,12},{24,20},{28,28},{5,9},{1... | collective-permute-start | bytes 294920 | tf_op jit(solution)/shard_map/ppermute | solution.py:525
  70.3 1.1 %shard_map.48 = (f32[2,96,640]{2,1,0:T(8,128)S(1)}, f32[2,96,512]{2,1,0:T(8,128)S(1)}) custom-call(s32[1]{0:T(128)} %bitcast.2.lev_ref, f32[96,96]{1,0:T(8,128)S(1)} %copy-done, f32[4,96,640]{2,1,0:T(8,128)S(1)} %get-tuple-element.43.tracer_ref, f32[2,96,640]{2,1,0:T(8,128)S(1)} %get-tuple-element.50.edge_ref, ...), custom_call_target="tpu_custom_call" | custom-call | flops 4000000 | bytes 4000000 | tf_op jit(solution)/shard_map/pallas_call | solution.py:502
  71.4 0.1 collective-permute-done.15.pair_ref
  71.5 4.3 %collective-permute-done.16.diagonal_ref = bf16[96,512]{1,0:T(8,128)(2,1)S(1)} collective-permute-done((bf16[96,512]{1,0:T(8,128)(2,1)S(1)}, bf16[96,512]{1,0:T(8,128)(2,1)S(1)}, u32[]{:S(2)}, u32[]{:S(2)}) %collective-permute-start.16) | collective-permute-done | bytes 98336 | tf_op jit(solution)/shard_map/ppermute | solution.py:525
  75.8 1.5 %shard_map.49 = f32[96,4,512]{2,1,0:T(4,128)} custom-call(s32[1]{0:T(128)} %bitcast.odd_ref, s32[1]{0:T(128)} %bitcast.1.end_ref, f32[2,96,640]{2,1,0:T(8,128)S(1)} %get-tuple-element.50.edge_ref, f32[2,96,640]{2,1,0:T(8,128)S(1)} %get-tuple-element.51.inner_ref, f32[2,96,512]{2,1,0:T(8,128)S(1)} %get-tuple-element.52.done_ref, ...), custom_call_target="tpu_custom_call" | custom-call | flops 4000000 | bytes 4000000 | tf_op jit(solution)/shard_map/pallas_call | solution.py:502
  (1 shorter events, 0.0 us)
Async XLA Ops:
  0.0 22.2 %copy-start.2 = (s32[1024]{0:T(1024)S(1)}, s32[1024]{0:T(1024)}, u32[]{:S(2)}) copy-start(s32[1024]{0:T(1024)} %numbers_ref.1) | copy-start | bytes 12292
  14.8 32.6 %copy-start.1 = (bf16[3,2,4,24,128]{4,3,2,1,0:T(8,128)(2,1)S(1)}, bf16[3,2,4,24,128]{4,3,2,1,0:T(8,128)(2,1)}, u32[]{:S(2)}) copy-start(bf16[3,2,4,24,128]{4,3,2,1,0:T(8,128)(2,1)} %get-tuple-element.31.refs_0_) | copy-start | bytes 442372
  14.8 7.7 %collective-permute-start = (bf16[3,2,4,24,128]{4,3,2,1,0:T(8,128)(2,1)}, bf16[3,2,4,24,128]{4,3,2,1,0:T(8,128)(2,1)S(1)}, u32[]{:S(2)}, u32[]{:S(2)}) collective-permute-start(bf16[3,2,4,24,128]{4,3,2,1,0:T(8,128)(2,1)} %get-tuple-element.32), channel_id=1, source_target_pairs={{0,4},{4,0},{8,12},{12,8},{16,20},{20,16},{24,28},{28,24},{1,5},{5... | collective-permute-start | bytes 442376 | tf_op jit(solution)/shard_map/ppermute | solution.py:517
  16.4 9.8 %collective-permute-start.1 = (bf16[3,2,4,24,128]{4,3,2,1,0:T(8,128)(2,1)}, bf16[3,2,4,24,128]{4,3,2,1,0:T(8,128)(2,1)S(1)}, u32[]{:S(2)}, u32[]{:S(2)}) collective-permute-start(bf16[3,2,4,24,128]{4,3,2,1,0:T(8,128)(2,1)} %get-tuple-element.33), channel_id=1, source_target_pairs={{0,8},{4,12},{8,0},{12,4},{16,24},{20,28},{24,16},{28,20},{1,9},{5... | collective-permute-start | bytes 442376 | tf_op jit(solution)/shard_map/ppermute | solution.py:517
  17.9 12.2 %collective-permute-start.2 = (bf16[3,2,4,24,128]{4,3,2,1,0:T(8,128)(2,1)}, bf16[3,2,4,24,128]{4,3,2,1,0:T(8,128)(2,1)S(1)}, u32[]{:S(2)}, u32[]{:S(2)}) collective-permute-start(bf16[3,2,4,24,128]{4,3,2,1,0:T(8,128)(2,1)} %get-tuple-element.34), channel_id=1, source_target_pairs={{0,12},{4,8},{8,4},{12,0},{16,28},{20,24},{24,20},{28,16},{1,13},{... | collective-permute-start | bytes 442376 | tf_op jit(solution)/shard_map/ppermute | solution.py:517
  18.3 11.8 %collective-permute-start.3 = (bf16[3,2,4,24,128]{4,3,2,1,0:T(8,128)(2,1)}, bf16[3,2,4,24,128]{4,3,2,1,0:T(8,128)(2,1)S(1)}, u32[]{:S(2)}, u32[]{:S(2)}) collective-permute-start(bf16[3,2,4,24,128]{4,3,2,1,0:T(8,128)(2,1)} %get-tuple-element.35), channel_id=1, source_target_pairs={{0,16},{4,20},{8,24},{12,28},{16,0},{20,4},{24,8},{28,12},{1,17},{... | collective-permute-start | bytes 442376 | tf_op jit(solution)/shard_map/ppermute | solution.py:517
  18.3 20.6 %collective-permute-start.4 = (bf16[3,2,4,24,128]{4,3,2,1,0:T(8,128)(2,1)}, bf16[3,2,4,24,128]{4,3,2,1,0:T(8,128)(2,1)S(1)}, u32[]{:S(2)}, u32[]{:S(2)}) collective-permute-start(bf16[3,2,4,24,128]{4,3,2,1,0:T(8,128)(2,1)} %get-tuple-element.36), channel_id=1, source_target_pairs={{0,20},{4,16},{8,28},{12,24},{16,4},{20,0},{24,12},{28,8},{1,21},{... | collective-permute-start | bytes 442376 | tf_op jit(solution)/shard_map/ppermute | solution.py:517
  22.5 22.4 %collective-permute-start.5 = (bf16[3,2,4,24,128]{4,3,2,1,0:T(8,128)(2,1)}, bf16[3,2,4,24,128]{4,3,2,1,0:T(8,128)(2,1)S(1)}, u32[]{:S(2)}, u32[]{:S(2)}) collective-permute-start(bf16[3,2,4,24,128]{4,3,2,1,0:T(8,128)(2,1)} %get-tuple-element.37), channel_id=1, source_target_pairs={{0,24},{4,28},{8,16},{12,20},{16,8},{20,12},{24,0},{28,4},{1,25},{... | collective-permute-start | bytes 442376 | tf_op jit(solution)/shard_map/ppermute | solution.py:517
  26.1 21.3 %collective-permute-start.6 = (bf16[3,2,4,24,128]{4,3,2,1,0:T(8,128)(2,1)}, bf16[3,2,4,24,128]{4,3,2,1,0:T(8,128)(2,1)S(1)}, u32[]{:S(2)}, u32[]{:S(2)}) collective-permute-start(bf16[3,2,4,24,128]{4,3,2,1,0:T(8,128)(2,1)} %get-tuple-element.38), channel_id=1, source_target_pairs={{0,28},{4,24},{8,20},{12,16},{16,12},{20,8},{24,4},{28,0},{1,29},{... | collective-permute-start | bytes 442376 | tf_op jit(solution)/shard_map/ppermute | solution.py:517
  48.6 7.3 %copy-start = (f32[96,96]{1,0:T(8,128)S(1)}, f32[96,96]{1,0:T(8,128)}, u32[]{:S(2)}) copy-start(f32[96,96]{1,0:T(8,128)} %vertical_ref.5) | copy-start | bytes 110596
  48.6 5.9 %collective-permute-start.7 = (bf16[104,512]{1,0:T(8,128)(2,1)S(1)}, bf16[104,512]{1,0:T(8,128)(2,1)S(1)}, u32[]{:S(2)}, u32[]{:S(2)}) collective-permute-start(bf16[104,512]{1,0:T(8,128)(2,1)S(1)} %get-tuple-element.40), channel_id=1, source_target_pairs={{0,1},{1,0},{2,3},{3,2},{4,5},{5,4},{6,7},{7,6},{8,9},{9,8},{10,11... | collective-permute-start | bytes 319496 | tf_op jit(solution)/shard_map/ppermute | solution.py:517
  48.7 5.9 %collective-permute-start.8 = (bf16[104,512]{1,0:T(8,128)(2,1)S(1)}, bf16[104,512]{1,0:T(8,128)(2,1)S(1)}, u32[]{:S(2)}, u32[]{:S(2)}) collective-permute-start(bf16[104,512]{1,0:T(8,128)(2,1)S(1)} %get-tuple-element.41), channel_id=1, source_target_pairs={{0,2},{1,3},{2,0},{3,1},{4,6},{5,7},{6,4},{7,5},{8,10},{9,11},{10,... | collective-permute-start | bytes 319496 | tf_op jit(solution)/shard_map/ppermute | solution.py:517
  50.3 5.6 %collective-permute-start.9 = (bf16[104,512]{1,0:T(8,128)(2,1)S(1)}, bf16[104,512]{1,0:T(8,128)(2,1)S(1)}, u32[]{:S(2)}, u32[]{:S(2)}) collective-permute-start(bf16[104,512]{1,0:T(8,128)(2,1)S(1)} %get-tuple-element.42), channel_id=1, source_target_pairs={{0,3},{1,2},{2,1},{3,0},{4,7},{5,6},{6,5},{7,4},{8,11},{9,10},{10,... | collective-permute-start | bytes 319496 | tf_op jit(solution)/shard_map/ppermute | solution.py:517
  52.5 7.4 %collective-permute-start.12 = (bf16[200,512]{1,0:T(8,128)(2,1)S(1)}, bf16[200,512]{1,0:T(8,128)(2,1)S(1)}, u32[]{:S(2)}, u32[]{:S(2)}) collective-permute-start(bf16[200,512]{1,0:T(8,128)(2,1)S(1)} %get-tuple-element.47), channel_id=1, source_target_pairs={{0,1},{1,0},{2,3},{3,2},{4,5},{5,4},{6,7},{7,6},{8,9},{9,8},{10,11... | collective-permute-start | bytes 614408 | tf_op jit(solution)/shard_map/ppermute | solution.py:517
  53.0 8.3 %collective-permute-start.13 = (bf16[200,512]{1,0:T(8,128)(2,1)S(1)}, bf16[200,512]{1,0:T(8,128)(2,1)S(1)}, u32[]{:S(2)}, u32[]{:S(2)}) collective-permute-start(bf16[200,512]{1,0:T(8,128)(2,1)S(1)} %get-tuple-element.48), channel_id=1, source_target_pairs={{0,2},{1,3},{2,0},{3,1},{4,6},{5,7},{6,4},{7,5},{8,10},{9,11},{10,... | collective-permute-start | bytes 614408 | tf_op jit(solution)/shard_map/ppermute | solution.py:517
  54.5 10.1 %collective-permute-start.14 = (bf16[200,512]{1,0:T(8,128)(2,1)S(1)}, bf16[200,512]{1,0:T(8,128)(2,1)S(1)}, u32[]{:S(2)}, u32[]{:S(2)}) collective-permute-start(bf16[200,512]{1,0:T(8,128)(2,1)S(1)} %get-tuple-element.49), channel_id=1, source_target_pairs={{0,3},{1,2},{2,1},{3,0},{4,7},{5,6},{6,5},{7,4},{8,11},{9,10},{10,... | collective-permute-start | bytes 614408 | tf_op jit(solution)/shard_map/ppermute | solution.py:517
  56.8 7.8 %collective-permute-start.10 = (bf16[96,640]{1,0:T(8,128)(2,1)S(1)}, bf16[96,640]{1,0:T(8,128)(2,1)S(1)}, u32[]{:S(2)}, u32[]{:S(2)}) collective-permute-start(bf16[96,640]{1,0:T(8,128)(2,1)S(1)} %get-tuple-element.44), channel_id=1, source_target_pairs={{0,4},{4,0},{8,12},{12,8},{16,20},{20,16},{24,28},{28,24},{1,5},{5... | collective-permute-start | bytes 368648 | tf_op jit(solution)/shard_map/ppermute | solution.py:526
  57.4 8.5 %collective-permute-start.11 = (bf16[96,640]{1,0:T(8,128)(2,1)S(1)}, bf16[96,640]{1,0:T(8,128)(2,1)S(1)}, u32[]{:S(2)}, u32[]{:S(2)}) collective-permute-start(bf16[96,640]{1,0:T(8,128)(2,1)S(1)} %get-tuple-element.45), channel_id=1, source_target_pairs={{4,8},{12,16},{20,24},{0,0},{8,4},{16,12},{24,20},{28,28},{5,9},{1... | collective-permute-start | bytes 368648 | tf_op jit(solution)/shard_map/ppermute | solution.py:525
  66.9 4.7 %collective-permute-start.15 = (bf16[96,512]{1,0:T(8,128)(2,1)S(1)}, bf16[96,512]{1,0:T(8,128)(2,1)S(1)}, u32[]{:S(2)}, u32[]{:S(2)}) collective-permute-start(bf16[96,512]{1,0:T(8,128)(2,1)S(1)} %get-tuple-element.53), channel_id=1, source_target_pairs={{0,4},{4,0},{8,12},{12,8},{16,20},{20,16},{24,28},{28,24},{1,5},{5... | collective-permute-start | bytes 294920 | tf_op jit(solution)/shard_map/ppermute | solution.py:526
  68.4 7.4 %collective-permute-start.16 = (bf16[96,512]{1,0:T(8,128)(2,1)S(1)}, bf16[96,512]{1,0:T(8,128)(2,1)S(1)}, u32[]{:S(2)}, u32[]{:S(2)}) collective-permute-start(bf16[96,512]{1,0:T(8,128)(2,1)S(1)} %get-tuple-element.54), channel_id=1, source_target_pairs={{4,8},{12,16},{20,24},{0,0},{8,4},{16,12},{24,20},{28,28},{5,9},{1... | collective-permute-start | bytes 294920 | tf_op jit(solution)/shard_map/ppermute | solution.py:525
